TPU v7x, 32 devices: a whole 2x2x4 slice. The times are simulated.
32 devices in a mesh: lat: 4 (over y, core), lon: 8 (over z, x).
Axes of the slice: x: 2, y: 2, z: 4, core: 2. Of those that a mesh axis runs over, the one named last changes fastest.
Arguments:
- source_fields: bfloat16 [8192, 64, 128], P(('lat', 'lon')), may hold values from -16 to 16
- weight_blocks: bfloat16 [8192, 128, 128], P(('lat', 'lon')), may hold values from -0.5 to 0.5
- pair_source: int32 [8192], P(('lat', 'lon')), may hold values from 0 to 255
- pair_target: int32 [8192, 1], P(('lat', 'lon')), may hold values from 0 to 7; in each aligned block of 256 rows (0 to 255, 256 to 511, ...) at most 64 rows name the same one
- pair_block: int32 [8192], P(('lat', 'lon')), may hold values from 0 to 255
Outputs:
- correlation: float32 [256, 4096], P('lat', 'lon')
Inputs may be any that keep to these rules, and one draw needn't show every extreme that they name: `pair_target`: among the rows of one device, no longitude tile is named by more than 64 pairs, a bound that some block reaches of them.
All inputs are finite; a program needn't handle non-finite values.
Results may differ from a plain program's by a relative error of at most 0.0006.
Values may be sent and summed in bfloat16 or wider, within the bound.
No kernel may reach another device: no remote copies, remote signals or barrier semaphores. Data moves between devices by JAX's collectives and lax.ppermute only.
A program may use at most 128 MiB of HBM per device.

v0:
```python
import jax
import jax.numpy as jnp
from jax import lax
from jax.sharding import PartitionSpec as P

WINDOW_HALF = 16
LAT_DEV = 64
LON_DEV = 512


def padded(x, sides, width, wrap):
    for axis, dim in sides:
        count, length = (lax.axis_size(axis), x.shape[dim])
        up = [(i, (i + 1) % count) for i in range(count if wrap else count - 1)]
        down = [(j, i) for i, j in up]
        last = lax.slice_in_dim(x, length - width, length, axis=dim)
        leading = lax.slice_in_dim(x, 0, width, axis=dim)
        before = lax.ppermute(last, axis, up)
        after = lax.ppermute(leading, axis, down)
        x = jnp.concatenate([before, x, after], axis=dim)
    return x


def gaussian_taps():
    offsets = jnp.arange(2 * WINDOW_HALF + 1).astype(jnp.float32) - WINDOW_HALF
    return jnp.exp(-offsets * offsets / (0.5 * WINDOW_HALF * WINDOW_HALF))


def band_matrix(length):
    outer = jnp.arange(length + 2 * WINDOW_HALF, dtype=jnp.int32)[:, None]
    inner = jnp.arange(length, dtype=jnp.int32)[None, :]
    offsets = (outer - inner - WINDOW_HALF).astype(jnp.float32)
    values = jnp.exp(-offsets * offsets / (0.5 * WINDOW_HALF * WINDOW_HALF))
    return jnp.where(jnp.abs(offsets) <= WINDOW_HALF, values, 0.0)


def smooth_lon(fields, lon_band):
    return jnp.einsum("krb,bj->krj", fields, lon_band, precision=lax.Precision.HIGHEST)


def smooth_lat(fields, lat_band):
    return jnp.einsum("ai,kaj->kij", lat_band, fields, precision=lax.Precision.HIGHEST)


def local(source_fields, weight_blocks, pair_source, pair_target, pair_block):
    lon_count = lax.axis_size("lon")
    pair_count = pair_source.shape[0]
    capacity = max(2, 2 * pair_count // lon_count)
    blocks_dev = source_fields.shape[0]
    channels = source_fields.shape[1]
    cell_count = source_fields.shape[2]
    targets = pair_target[:, 0]
    lanes = jnp.arange(lon_count, dtype=jnp.int32)
    matches = (targets[:, None] == lanes[None, :]).astype(jnp.int32)
    earlier = jnp.cumsum(matches, axis=0) - matches
    slots = jnp.sum(earlier * matches, axis=1)
    position = targets * capacity + slots
    outgoing = jnp.zeros((lon_count * capacity,), jnp.int32).at[position].set(pair_block)
    arriving = lax.all_to_all(
        outgoing.reshape(lon_count, capacity), "lon", split_axis=0, concat_axis=0, tiled=True
    )
    picked = source_fields[pair_source]
    terms = jnp.einsum("pck,pjk->pcj", picked, weight_blocks, preferred_element_type=jnp.float32)
    packed = (
        jnp.zeros((lon_count * capacity, channels, cell_count), jnp.float32).at[position].set(terms)
    )
    received = lax.all_to_all(
        packed.reshape(lon_count, capacity, channels, cell_count).astype(jnp.bfloat16),
        "lon",
        split_axis=0,
        concat_axis=0,
        tiled=True,
    ).astype(jnp.float32)
    remapped = jax.ops.segment_sum(
        received.reshape(lon_count * capacity, channels, cell_count),
        arriving.reshape(-1),
        num_segments=blocks_dev,
    )
    days = channels // 2
    temper = remapped[:, :days]
    moist = remapped[:, days:]
    moments = jnp.stack(
        [
            temper.sum(1),
            moist.sum(1),
            (temper * temper).sum(1),
            (moist * moist).sum(1),
            (temper * moist).sum(1),
        ]
    )
    moments = moments.reshape(5, LAT_DEV, LON_DEV)
    lon_band = band_matrix(LON_DEV)
    lat_band = band_matrix(LAT_DEV)
    taller = padded(moments.astype(jnp.bfloat16), (("lat", 1),), WINDOW_HALF, False).astype(
        moments.dtype
    )
    wider = padded(taller.astype(jnp.bfloat16), (("lon", 2),), WINDOW_HALF, True).astype(
        taller.dtype
    )
    smoothed = smooth_lat(smooth_lon(wider, lon_band), lat_band)
    kernel = gaussian_taps()
    height = LAT_DEV * lax.axis_size("lat")
    rows = (
        lax.axis_index("lat") * LAT_DEV
        + jnp.arange(LAT_DEV, dtype=jnp.int32)[:, None]
        + jnp.arange(2 * WINDOW_HALF + 1, dtype=jnp.int32)[None, :]
        - WINDOW_HALF
    )
    inside = ((rows >= 0) & (rows < height)).astype(jnp.float32)
    lat_total = jnp.sum(inside * kernel[None, :], axis=1)
    weight_total = lat_total[:, None] * (jnp.sum(kernel) * days)
    mean_temper = smoothed[0] / weight_total
    mean_moist = smoothed[1] / weight_total
    var_temper = smoothed[2] / weight_total - mean_temper * mean_temper
    var_moist = smoothed[3] / weight_total - mean_moist * mean_moist
    covar = smoothed[4] / weight_total - mean_temper * mean_moist
    return covar / jnp.sqrt(var_temper * var_moist + 1e-06)


def solution(mesh):
    placed = (
        P(("lat", "lon"), None, None),
        P(("lat", "lon"), None, None),
        P(("lat", "lon")),
        P(("lat", "lon"), None),
        P(("lat", "lon")),
    )
    return jax.shard_map(
        local, mesh=mesh, in_specs=placed, out_specs=P("lat", "lon"), check_vma=False
    )
```

profile of v0, /device:TPU:1, one launch (start us, length us, event | category | flops | bytes accessed | tf_op | source)
XLA Modules:
  0.0 395.7 jit_solution(13790155770616325313)
XLA Ops:
  0.0 0.7 fusion.55
  0.7 0.6 reduce-window.6
  1.3 0.2 slice_reduce_fusion.2
  1.5 0.8 fusion.54
  2.3 0.7 compare_select_fusion
  3.0 1.6 scatter_custom_fusion
  4.5 0.7 all_to_all.9
  5.2 6.3 %all-to-all-start = ((s32[8,1,64]{2,1,0:T(1,128)}), s32[8,1,64]{2,1,0:T(1,128)S(1)}, u32[]{:S(2)}, u32[]{:S(2)}) async-start(s32[8,1,64]{2,1,0:T(1,128)} %all_to_all.9), calls=%async_computation | async-start | bytes 8192 | tf_op jit(solution)/shard_map/all_to_all | solution.py:59
  11.5 0.7 compare_select_fusion.1
  12.2 5.2 %gather_fusion = bf16[256,64,128]{2,1,0:T(8,128)(2,1)} fusion(bf16[256,64,128]{2,1,0:T(8,128)(2,1)} %param.5, s32[1024]{0:T(1024)S(1)} %pad_clamp_fusion), kind=kCustom, calls=%fused_computation | custom fusion | bytes 8389632 | tf_op jit(solution)/shard_map/gather | solution.py:62
  17.4 13.7 %fusion.71 = f32[256,64,128]{2,1,0:T(8,128)} fusion(bf16[256,64,128]{2,1,0:T(8,128)(2,1)} %gather_fusion, bf16[256,128,128]{2,1,0:T(8,128)(2,1)} %param.6), kind=kOutput, calls=%fused_computation.109 | convolution fusion | flops 536870912 | bytes 20971520 | tf_op jit(solution)/shard_map/pck,pjk->pcj/dot_general | solution.py:63
  31.2 7.9 %broadcast_in_dim.18 = f32[512,64,128]{2,1,0:T(8,128)} broadcast(f32[]{:T(128)} %constant.13.clone.1), dimensions={} | broadcast | bytes 16777220 | tf_op jit(solution)/shard_map/broadcast_in_dim | solution.py:65
  39.0 37.4 %scatter_fusion = f32[512,64,128]{2,1,0:T(8,128)} fusion(f32[512,64,128]{2,1,0:T(8,128)} %broadcast_in_dim.18, s32[256]{0:T(256)S(1)} %bitcast.73, f32[256,64,128]{2,1,0:T(8,128)} %fusion.71), kind=kCustom, calls=%fused_computation.2 | custom fusion | bytes 25166848 | tf_op jit(solution)/shard_map/scatter | solution.py:65
  76.4 9.4 %convert_element_type.36 = bf16[512,64,128]{2,1,0:T(8,128)(2,1)} convert(f32[512,64,128]{2,1,0:T(8,128)} %scatter_fusion) | non-fusion elementwise | flops 4194304 | bytes 25165824 | tf_op jit(solution)/shard_map/convert_element_type | solution.py:68
  85.8 0.0 all-to-all-done
  85.8 5.4 %all-to-all-start.1 = ((bf16[8,64,64,128]{3,2,1,0:T(8,128)(2,1)}), bf16[8,64,64,128]{3,2,1,0:T(8,128)(2,1)}, u32[]{:S(2)}, u32[]{:S(2)}) async-start(bf16[8,64,64,128]{3,2,1,0:T(8,128)(2,1)} %bitcast.69), calls=%async_computation.1 | async-start | bytes 16777216 | tf_op jit(solution)/shard_map/all_to_all | solution.py:67
  91.2 0.6 fusion.60
  92.5 0.5 broadcast.97
  93.0 0.7 reduce.5
  93.7 0.1 reshape.95
  93.8 179.3 %all-to-all-done.1 = bf16[8,64,64,128]{3,2,1,0:T(8,128)(2,1)} async-done(((bf16[8,64,64,128]{3,2,1,0:T(8,128)(2,1)}), bf16[8,64,64,128]{3,2,1,0:T(8,128)(2,1)}, u32[]{:S(2)}, u32[]{:S(2)}) %all-to-all-start.1) | async-done | bytes 8388640 | tf_op jit(solution)/shard_map/all_to_all | solution.py:67
  273.0 11.3 %bitcast_convert_fusion = f32[512,64,128]{2,1,0:T(8,128)} fusion(bf16[8,64,64,128]{3,2,1,0:T(8,128)(2,1)} %all-to-all-done.1), kind=kLoop, calls=%fused_computation.4 | loop fusion | flops 4194304 | bytes 25165824 | tf_op jit(solution)/shard_map/reshape | solution.py:75
  284.3 4.3 %broadcast_in_dim.16 = f32[256,64,128]{2,1,0:T(8,128)} broadcast(f32[]{:T(128)} %constant.13.clone.1), dimensions={} | broadcast | bytes 8388612 | tf_op jit(solution)/shard_map/broadcast_in_dim | solution.py:74
  288.6 79.6 %scatter_fusion.1 = f32[256,64,128]{2,1,0:T(8,128)} fusion(f32[256,64,128]{2,1,0:T(8,128)} %broadcast_in_dim.16, s32[512]{0:T(512)S(1)} %reshape.95, f32[512,64,128]{2,1,0:T(8,128)} %bitcast_convert_fusion), kind=kCustom, calls=%fused_computation.3 | custom fusion | flops 4194304 | bytes 50333696 | tf_op jit(solution)/shard_map/scatter-add | solution.py:74
  368.2 5.7 %multiply_reduce_fusion = (bf16[256,128]{1,0:T(8,128)(2,1)S(1)}, bf16[256,128]{1,0:T(8,128)(2,1)S(1)}, bf16[256,128]{1,0:T(8,128)(2,1)S(1)}, bf16[256,128]{1,0:T(8,128)(2,1)S(1)}, bf16[256,128]{1,0:T(8,128)(2,1)S(1)}) fusion(f32[256,64,128]{2,1,0:T(8,128)} %scatter_fusion.1), kind=kLoop, calls=%fused_computation.5 | loop fusion | flops 8224768 | bytes 8716288 | tf_op jit(solution)/shard_map/reduce_sum | solution.py:88
  373.9 0.1 stack.18
  373.9 0.1 stack.19
  374.0 0.1 stack.20
  374.1 0.1 stack.21
  374.1 0.1 stack.22
  374.3 4.8 %collective-permute-start = (bf16[5,16,512]{2,1,0:T(8,128)(2,1)S(1)}, bf16[5,16,512]{2,1,0:T(8,128)(2,1)S(1)}, u32[]{:S(2)}, u32[]{:S(2)}) collective-permute-start(bf16[5,16,512]{2,1,0:T(8,128)(2,1)S(1)} %get-tuple-element.12), channel_id=1, source_target_pairs={{0,8},{8,16},{16,24},{1,9},{9,17},{17,25},{2,10},{10,18},{18,26},{... | collective-permute-start | bytes 245768 | tf_op jit(solution)/shard_map/ppermute | solution.py:18
  379.1 1.9 collective-permute-start.1
  381.0 0.1 select_reduce_fusion
  381.1 0.0 collective-permute-done
  381.1 3.7 collective-permute-done.1
  384.9 0.1 pad_maximum_fusion.2
  385.0 1.4 collective-permute-start.2
  386.4 2.8 collective-permute-start.3
  389.2 2.4 collective-permute-done.2
  391.5 0.7 collective-permute-done.3
  392.2 1.9 fusion.4
  394.1 0.8 convolution_bitcast_fusion
  394.9 0.8 fusion.29
  (12 shorter events, 0.1 us)
Async XLA Ops:
  5.2 80.6 %all-to-all-start = ((s32[8,1,64]{2,1,0:T(1,128)}), s32[8,1,64]{2,1,0:T(1,128)S(1)}, u32[]{:S(2)}, u32[]{:S(2)}) async-start(s32[8,1,64]{2,1,0:T(1,128)} %all_to_all.9), calls=%async_computation | async-start | bytes 8192 | tf_op jit(solution)/shard_map/all_to_all | solution.py:59
  85.8 187.2 %all-to-all-start.1 = ((bf16[8,64,64,128]{3,2,1,0:T(8,128)(2,1)}), bf16[8,64,64,128]{3,2,1,0:T(8,128)(2,1)}, u32[]{:S(2)}, u32[]{:S(2)}) async-start(bf16[8,64,64,128]{3,2,1,0:T(8,128)(2,1)} %bitcast.69), calls=%async_computation.1 | async-start | bytes 16777216 | tf_op jit(solution)/shard_map/all_to_all | solution.py:67
  374.3 6.9 %collective-permute-start = (bf16[5,16,512]{2,1,0:T(8,128)(2,1)S(1)}, bf16[5,16,512]{2,1,0:T(8,128)(2,1)S(1)}, u32[]{:S(2)}, u32[]{:S(2)}) collective-permute-start(bf16[5,16,512]{2,1,0:T(8,128)(2,1)S(1)} %get-tuple-element.12), channel_id=1, source_target_pairs={{0,8},{8,16},{16,24},{1,9},{9,17},{17,25},{2,10},{10,18},{18,26},{... | collective-permute-start | bytes 245768 | tf_op jit(solution)/shard_map/ppermute | solution.py:18
  379.1 5.8 %collective-permute-start.1 = (bf16[5,16,512]{2,1,0:T(8,128)(2,1)S(1)}, bf16[5,16,512]{2,1,0:T(8,128)(2,1)S(1)}, u32[]{:S(2)}, u32[]{:S(2)}) collective-permute-start(bf16[5,16,512]{2,1,0:T(8,128)(2,1)S(1)} %get-tuple-element.13), channel_id=1, source_target_pairs={{8,0},{16,8},{24,16},{9,1},{17,9},{25,17},{10,2},{18,10},{26,18},{... | collective-permute-start | bytes 245768 | tf_op jit(solution)/shard_map/ppermute | solution.py:19
  385.0 6.6 %collective-permute-start.2 = (bf16[5,96,16]{2,1,0:T(8,128)(2,1)S(1)}, bf16[5,96,16]{2,1,0:T(8,128)(2,1)S(1)}, u32[]{:S(2)}, u32[]{:S(2)}) collective-permute-start(bf16[5,96,16]{2,1,0:T(8,128)(2,1)S(1)} %get-tuple-element.10), channel_id=1, source_target_pairs={{0,1},{1,2},{2,3},{3,4},{4,5},{5,6},{6,7},{7,0},{8,9},{9,10},{10,1... | collective-permute-start | bytes 46088 | tf_op jit(solution)/shard_map/ppermute | solution.py:18
  386.4 5.8 %collective-permute-start.3 = (bf16[5,96,16]{2,1,0:T(8,128)(2,1)S(1)}, bf16[5,96,16]{2,1,0:T(8,128)(2,1)S(1)}, u32[]{:S(2)}, u32[]{:S(2)}) collective-permute-start(bf16[5,96,16]{2,1,0:T(8,128)(2,1)S(1)} %get-tuple-element.11), channel_id=1, source_target_pairs={{1,0},{2,1},{3,2},{4,3},{5,4},{6,5},{7,6},{0,7},{9,8},{10,9},{11,1... | collective-permute-start | bytes 46088 | tf_op jit(solution)/shard_map/ppermute | solution.py:19
where the time goes:
time: 398 us; the launch traced here: 396 us
  waiting for transfers between devices  186 us (47%)
  other arithmetic  112 us (28%)
  local copies, waits for them, and re-layouts  58 us (15%)
  starting transfers between devices  22.7 us (6%)
  matrix products  16.4 us (4%)
    all_to_all x1, waiting for transfers between devices, local(): lax.all_to_all(packed.reshape(lon_count, capacity, channels, cell_count)....  179 us
    scatter-add x1, other arithmetic, local(): jax.ops.segment_sum(received.reshape(lon_count * capacity, channels, cell...  79.6 us
    scatter x1, local copies, waits for them, and re-layouts, local(): jnp.zeros((lon_count * capacity, channels, cell_count), jnp.float32)  37.4 us
    dot_general x1, matrix products, local(): jnp.einsum('pck,pjk->pcj', picked, weight_blocks, preferred_element_type=...  13.7 us
    reshape x1, other arithmetic, local(): received.reshape(lon_count * capacity, channels, cell_count)  11.3 us
    convert_element_type x1, other arithmetic, local(): packed.reshape(lon_count, capacity, channels, cell_count)  9.44 us
  transfers between devices with their start and end apart: 6, of which 4 were waited for; matrix products, arithmetic and copies ran while one was open for 19% of the time, Pallas kernels for 0%

commit v1 on v0

--- a/solution.py
+++ b/solution.py
@@ -1,11 +1,22 @@
+import functools
+
 import jax
 import jax.numpy as jnp
 from jax import lax
+from jax.experimental import pallas as pl
+from jax.experimental.pallas import tpu as pltpu
 from jax.sharding import PartitionSpec as P
 
 WINDOW_HALF = 16
 LAT_DEV = 64
 LON_DEV = 512
+LANES = 128
+RING = 32
+GROUP = 8
+CHUNK = 16
+F32 = jnp.float32
+BF16 = jnp.bfloat16
+I32 = jnp.int32
 
 
 def padded(x, sides, width, wrap):
@@ -42,14 +53,493 @@
     return jnp.einsum("ai,kaj->kij", lat_band, fields, precision=lax.Precision.HIGHEST)
 
 
-def local(source_fields, weight_blocks, pair_source, pair_target, pair_block):
+def iota(shape, dim):
+    return lax.broadcasted_iota(I32, shape, dim)
+
+
+def dot(a, b, dims=((1,), (0,)), exact=False):
+    return lax.dot_general(
+        a,
+        b,
+        (dims, ((), ())),
+        preferred_element_type=F32,
+        precision=lax.Precision.HIGHEST if exact else None,
+    )
+
+
+def repeat(count, body, carry):
+    if count <= 8:
+        for step in range(count):
+            carry = body(step, carry)
+        return carry
+    return lax.fori_loop(0, count, body, carry)
+
+
+def one_hots(row, height):
+    pairs = row.shape[1]
+    high = (iota((height, pairs), 0) == (row >> 7)).astype(F32)
+    low = (iota((LANES, pairs), 0) == (row & (LANES - 1))).astype(F32)
+    return high, low
+
+
+def look_up(table, high, low):
+    return jnp.sum(dot(table, low, exact=True) * high, axis=0, keepdims=True)
+
+
+def plan_kernel(
+    count, blocks, cap, mcap, me_ref, keys_ref, src_ref, table_ref, entry_ref, spot_ref, pres
+):
+    me = me_ref[0]
+    pairs = keys_ref.shape[1]
+    height = count * blocks // LANES
+    tile_rows = blocks // LANES
+    sends = count * cap
+
+    def held(d, carry):
+        high, low = one_hots(keys_ref[pl.ds(d, 1), :], height)
+        found = dot(high.astype(BF16), low.astype(BF16), ((1,), (1,)))
+        pres[d] = (found > 0.5).astype(F32)
+        return carry
+
+    repeat(count, held, 0)
+
+    row_at = iota((height, LANES), 0)
+    turn = (row_at * LANES + iota((height, LANES), 1)) % count
+
+    zero = jnp.zeros((height, LANES), F32)
+    holders = repeat(count, lambda d, total: total + pres[d], zero)
+
+    def choose(d, carry):
+        best, owner = carry
+        rank = (d - turn + count) % count
+        rank = jnp.where(pres[d] > 0.5, rank, 4 * count)
+        better = rank < best
+        return jnp.where(better, rank, best), jnp.where(better, d, owner)
+
+    _, owner = repeat(
+        count,
+        choose,
+        (jnp.full((height, LANES), 4 * count, I32), jnp.full((height, LANES), -1, I32)),
+    )
+
+    ahead = (iota((LANES, LANES), 0) < iota((LANES, LANES), 1)).astype(BF16)
+    ones = jnp.ones((LANES, LANES), BF16)
+    ahead_total = jnp.concatenate([ahead, ones], axis=1)
+    up, down = iota((height, height), 1), iota((height, height), 0)
+    rows_ahead = (up < down).astype(BF16)
+    same_tile = ((up < down) & (up // tile_rows == down // tile_rows)).astype(BF16)
+
+    def prefix(mask, rows):
+        both = dot(mask.astype(BF16), ahead_total)
+        return both[:, :LANES] + dot(rows, both[:, LANES:].astype(BF16))
+
+    mine = (owner == me).astype(F32)
+    several = mine * (holders > 1.5).astype(F32)
+    single = mine - several
+    rank_several = prefix(several, rows_ahead)
+    rank_single = prefix(single, rows_ahead)
+    total_several = jnp.sum(several, axis=(0, 1), keepdims=True)
+    total_mine = jnp.sum(mine, axis=(0, 1), keepdims=True)
+    held_here = pres[me]
+    entry_rows = entry_ref.shape[0] - 8
+    lane_at = iota((entry_rows, LANES), 1)
+    first_lane = iota((8, LANES), 1)
+
+    def route(d, carry):
+        place, finished, most, entries, counts = carry
+        away = jnp.where(d == me, 0.0, 1.0)
+        theirs = (owner == d).astype(F32)
+        rank_theirs = prefix(theirs, same_tile)
+        base = lax.convert_element_type(d, F32) if not isinstance(d, int) else float(d)
+        finished = finished + theirs * (base * mcap + rank_theirs + 1.0)
+        most = jnp.maximum(most, theirs * (rank_theirs + 1.0))
+        leaving = held_here * theirs * away
+        rank_leaving = prefix(leaving, rows_ahead)
+        place = place + leaving * (base * cap + rank_leaving + 1.0)
+        coming = pres[d] * mine * away
+        rank_coming = prefix(coming, rows_ahead)
+        code = coming * (rank_coming * 1024.0 + rank_several + 1.0)
+        high, low = one_hots(keys_ref[pl.ds(d, 1), :], height)
+        seen = (look_up(code, high, low) + 0.5).astype(I32) - 1
+        rank, local = seen >> 10, seen & 1023
+        hit = iota((entry_rows, pairs), 0) == rank
+        column = jnp.max(jnp.where(hit, local, -1), axis=1, keepdims=True)
+        entries = jnp.where(lane_at == d, column, entries)
+        arrivals = jnp.sum(coming, axis=(0, 1), keepdims=True).astype(I32)
+        counts = jnp.where(first_lane == d, arrivals, counts)
+        return place, finished, most, entries, counts
+
+    place, finished, most, entries, counts = repeat(
+        count,
+        route,
+        (
+            zero,
+            zero,
+            zero,
+            jnp.full((entry_rows, LANES), -1, I32),
+            jnp.zeros((8, LANES), I32),
+        ),
+    )
+    entry_ref[:entry_rows, :] = entries
+    entry_ref[entry_rows:, :] = counts
+
+    pick = (iota((8, height), 1) == me * tile_rows + iota((8, height), 0)).astype(F32)
+    spot_ref[...] = (dot(pick, finished, exact=True) + 0.5).astype(I32) - 1
+
+    wide = -(-count // 8) * 8
+    which = iota((wide, LANES), 0)
+    which_one = iota((wide, 1), 0)
+
+    def load_of(s, worst):
+        here = pres[s]
+
+        def into(d, sums):
+            part = jnp.sum(here * (owner == d).astype(F32), axis=0, keepdims=True)
+            return jnp.where(which == d, part, sums)
+
+        sums = repeat(count, into, jnp.zeros((wide, LANES), F32))
+        loads = jnp.sum(sums, axis=1, keepdims=True)
+        return jnp.maximum(worst, jnp.where(which_one == s, 0.0, loads))
+
+    worst = repeat(count, load_of, jnp.zeros((wide, 1), F32))
+    worst = jnp.max(worst, axis=0, keepdims=True)
+    most = jnp.max(jnp.max(most, axis=1, keepdims=True), axis=0, keepdims=True)
+    over = jnp.where((worst > cap + 0.5) | (most > mcap + 0.5), 1, 0)
+
+    place = place + several * (sends + rank_several + 1.0)
+    place = place + single * (sends + total_several + rank_single + 1.0)
+    tile_of = (row_at // tile_rows).astype(F32)
+    moment_place = mine * (tile_of * mcap + finished - 1.0 - me.astype(F32) * mcap)
+    high, low = one_hots(keys_ref[pl.ds(me, 1), :], height)
+    goes = look_up(place, high, low) - 1.0
+    lands = look_up(moment_place, high, low)
+    leaves = (goes < sends - 0.5).astype(F32)
+    square = (iota((pairs, pairs), 0) < iota((pairs, pairs), 1)).astype(BF16)
+    before = dot(jnp.broadcast_to(leaves, (8, pairs)).astype(BF16), square)[0:1, :]
+    leaving = jnp.sum(leaves, axis=1, keepdims=True)
+    at = iota((1, pairs), 1).astype(F32)
+    position = jnp.where(leaves > 0.5, before, leaving + at - before)
+    kind = iota((8, pairs), 0)
+    values = jnp.where(
+        kind == 0,
+        at,
+        jnp.where(kind == 1, goes, jnp.where(kind == 2, src_ref[...].astype(F32), 0.0)),
+    )
+    column_at = iota((pairs, pairs), 0)
+    order = (column_at == (position + 0.5).astype(I32)).astype(F32)
+    ordered = dot(values, order, ((1,), (1,)), exact=True)
+    slot = jnp.where(leaves > 0.5, -1, (goes - sends + 0.5).astype(I32))
+    in_slot = (column_at == slot).astype(F32)
+    weighed = jnp.where(kind == 0, lands, 1.0)
+    summed = dot(weighed, in_slot, ((1,), (1,)), exact=True)
+    landing = summed[0:1, :] / jnp.maximum(summed[1:2, :], 1.0)
+    result = (ordered + 0.5).astype(I32)
+    result = jnp.where(kind == 3, (landing + 0.25).astype(I32), result)
+    lane = iota((8, pairs), 1)
+    facts = jnp.where(
+        lane == 0,
+        leaving.astype(I32),
+        jnp.where(
+            lane == 1,
+            total_mine.astype(I32),
+            jnp.where(lane == 2, total_several.astype(I32), over),
+        ),
+    )
+    table_ref[...] = jnp.where(kind == 4, facts, result)
+
+
+def make_plan(keys, pair_source, count, blocks, cap, mcap):
+    pairs = keys.shape[1]
+    height = count * blocks // LANES
+    entry_rows = -(-cap // 8) * 8 + 8
+    vmem = pl.BlockSpec(memory_space=pltpu.VMEM)
+    return pl.pallas_call(
+        functools.partial(plan_kernel, count, blocks, cap, mcap),
+        out_shape=(
+            jax.ShapeDtypeStruct((8, pairs), I32),
+            jax.ShapeDtypeStruct((entry_rows, LANES), I32),
+            jax.ShapeDtypeStruct((8, LANES), I32),
+        ),
+        in_specs=[pl.BlockSpec(memory_space=pltpu.SMEM), vmem, vmem],
+        out_specs=(vmem, vmem, vmem),
+        scratch_shapes=[pltpu.VMEM((count, height, LANES), F32)],
+        name="plan",
+    )(lax.axis_index("lon").astype(I32)[None], keys, pair_source[None, :])
+
+
+def pair_copies(table, src, weights, xs, ws, x_sem, w_sem, i):
+    slot = i % RING
+    return (
+        pltpu.make_async_copy(src.at[table[2, i]], xs.at[slot], x_sem.at[slot]),
+        pltpu.make_async_copy(weights.at[table[0, i]], ws.at[slot], w_sem.at[slot]),
+    )
+
+
+def products(table, src, weights, xs, ws, x_sem, w_sem, low, high, target, first, last, dummy, while_loading):
+    copies = functools.partial(pair_copies, table, src, weights, xs, ws, x_sem, w_sem)
+
+    def start(i):
+        for copy in copies(i):
+            copy.start()
+
+    def prime(i, carry):
+        @pl.when(i < high)
+        def _():
+            start(i)
+
+        return carry
+
+    lax.fori_loop(low, low + RING, prime, 0)
+    while_loading()
+
+    def step(g, carry):
+        base = g * GROUP
+        for u in range(GROUP):
+            for copy in copies(base + u):
+                copy.wait()
+        results = []
+        for u in range(GROUP):
+            slot = (base + u) % RING
+            results.append(dot(xs[slot], ws[slot], ((1,), (1,))))
+        for u in range(GROUP):
+            place = table[1, base + u]
+            inside = (place >= first) & (place < last)
+            where = jnp.where(inside, place - first, dummy)
+            target[where] = target[where] + results[u]
+
+        @pl.when(base + RING < high)
+        def _():
+            for u in range(GROUP):
+                start(base + RING + u)
+
+        return carry
+
+    lax.fori_loop(low // GROUP, high // GROUP, step, 0)
+
+
+def send_kernel(sends, table, src, weights, out_ref, total, xs, ws, x_sem, w_sem):
+    leaving = table[4, 0]
+    high = (leaving + GROUP - 1) // GROUP * GROUP
+
+    def clear():
+        def one(i, carry):
+            total[i] = jnp.zeros(total.shape[1:], F32)
+            return carry
+
+        lax.fori_loop(0, sends, one, 0)
+
+    products(
+        table, src, weights, xs, ws, x_sem, w_sem, 0, high, total, 0, sends, sends, clear
+    )
+
+    def finish(i, carry):
+        out_ref[i] = total[i].astype(BF16)
+        return carry
+
+    lax.fori_loop(0, sends, finish, 0)
+
+
+def moment_rows(value):
+    days = value.shape[0] // 2
+    temper, moist = value[:days], value[days:]
+    return [
+        jnp.sum(each, axis=0, keepdims=True)
+        for each in (temper, moist, temper * temper, moist * moist, temper * moist)
+    ]
+
+
+def put_moments(table, total, moments, spare, begin, end):
+    def some(g, carry):
+        for u in range(4):
+            i = begin + g * 4 + u
+            good = i < end
+            at = jnp.where(good, i, 0)
+            place = jnp.where(good, table[3, at], spare)
+            for k, row in enumerate(moment_rows(total[at])):
+                moments[k, pl.ds(place, 1), :] = row
+        return carry
+
+    lax.fori_loop(0, (end - begin + 3) // 4, some, 0)
+
+
+def chunk_copies(source, target, sem, c):
+    rows = pl.ds(c * CHUNK, CHUNK)
+    return pltpu.make_async_copy(source.at[rows], target.at[rows], sem.at[c])
+
+
+def local_kernel(
+    sends, table, src, weights, local_ref, moments, total, xs, ws, x_sem, w_sem, out_sem
+):
+    pairs = weights.shape[0]
+    leaving, owned, several = table[4, 0], table[4, 1], table[4, 2]
+    low = leaving // GROUP * GROUP
+
+    def clear():
+        def one(i, carry):
+            total[i] = jnp.zeros(total.shape[1:], F32)
+            return carry
+
+        lax.fori_loop(0, owned, one, 0)
+        moments[...] = jnp.zeros(moments.shape, F32)
+
+    products(
+        table,
+        src,
+        weights,
+        xs,
+        ws,
+        x_sem,
+        w_sem,
+        low,
+        pairs,
+        total,
+        sends,
+        sends + pairs,
+        pairs,
+        clear,
+    )
+    chunks = (several + CHUNK - 1) // CHUNK
+
+    def begin(c, carry):
+        chunk_copies(total, local_ref, out_sem, c).start()
+        return carry
+
+    lax.fori_loop(0, chunks, begin, 0)
+    put_moments(table, total, moments, moments.shape[1] - 8, several, owned)
+
+    def end(c, carry):
+        chunk_copies(total, local_ref, out_sem, c).wait()
+        return carry
+
+    lax.fori_loop(0, chunks, end, 0)
+
+
+def merge_kernel(
+    count, cap, mcap, table, entry, local_ref, came, moments_in, out_ref, total, moments, in_sem
+):
+    several = table[4, 2]
+    spare = total.shape[0] - 1
+    counts_row = entry.shape[0] - 8
+    chunks = (several + CHUNK - 1) // CHUNK
+
+    def begin(c, carry):
+        chunk_copies(local_ref, total, in_sem, c).start()
+        return carry
+
+    lax.fori_loop(0, chunks, begin, 0)
+    moments[...] = moments_in[...]
+
+    def end(c, carry):
+        chunk_copies(local_ref, total, in_sem, c).wait()
+        return carry
+
+    lax.fori_loop(0, chunks, end, 0)
+
+    def from_one(s, carry):
+        number = entry[counts_row, s]
+
+        def some(g, inner):
+            for u in range(4):
+                r = g * 4 + u
+                good = r < number
+                at = jnp.where(good, r, 0)
+                where = jnp.where(good, entry[at, s], spare)
+                total[where] = total[where] + came[s * cap + at].astype(F32)
+            return inner
+
+        lax.fori_loop(0, (number + 3) // 4, some, 0)
+        return carry
+
+    lax.fori_loop(0, count, from_one, 0)
+    put_moments(table, total, moments, moments.shape[1] - 8, 0, several)
+    for o in range(count):
+        for k in range(5):
+            out_ref[o, k] = moments[k, o * mcap : (o + 1) * mcap, :].astype(BF16)
+
+
+def spread_kernel(count, mcap, spot_ref, came, map_ref, flat):
+    rows, blocks_wide = map_ref.shape[1], map_ref.shape[2] // LANES
+    for a in range(count):
+        for k in range(5):
+            flat[a * mcap : (a + 1) * mcap, k * LANES : (k + 1) * LANES] = came[a, k]
+    chosen = (iota((spot_ref.shape[0], count * mcap), 1) == spot_ref[...]).astype(F32)
+    laid = dot(chosen.astype(BF16), flat[...])
+    for q in range(blocks_wide):
+        for k in range(5):
+            map_ref[k, :, q * LANES : (q + 1) * LANES] = laid[
+                q * rows : (q + 1) * rows, k * LANES : (k + 1) * LANES
+            ].astype(BF16)
+
+
+def direct(cap, mcap, source_fields, weight_blocks, table, entry, spot):
+    count = lax.axis_size("lon")
+    blocks, channels, cells = source_fields.shape
+    pairs = weight_blocks.shape[0]
+    sends = count * cap
+    smem = pl.BlockSpec(memory_space=pltpu.SMEM)
+    vmem = pl.BlockSpec(memory_space=pltpu.VMEM)
+    hbm = pl.BlockSpec(memory_space=pl.ANY)
+    buffers = [
+        pltpu.VMEM((RING, channels, cells), BF16),
+        pltpu.VMEM((RING, cells, cells), BF16),
+        pltpu.SemaphoreType.DMA((RING,)),
+        pltpu.SemaphoreType.DMA((RING,)),
+    ]
+    packed = pl.pallas_call(
+        functools.partial(send_kernel, sends),
+        out_shape=jax.ShapeDtypeStruct((sends, channels, cells), BF16),
+        in_specs=[smem, hbm, hbm],
+        out_specs=vmem,
+        scratch_shapes=[pltpu.VMEM((sends + 1, channels, cells), F32)] + buffers,
+        name="leaving",
+    )(table, source_fields, weight_blocks)
+    came = lax.all_to_all(
+        packed.reshape(count, cap, channels, cells), "lon", split_axis=0, concat_axis=0, tiled=True
+    ).reshape(sends, channels, cells)
+    chunk_count = -(-pairs // CHUNK)
+    local, moments = pl.pallas_call(
+        functools.partial(local_kernel, sends),
+        out_shape=(
+            jax.ShapeDtypeStruct((pairs, channels, cells), F32),
+            jax.ShapeDtypeStruct((5, count * mcap + 8, cells), F32),
+        ),
+        in_specs=[smem, hbm, hbm],
+        out_specs=(hbm, vmem),
+        scratch_shapes=[pltpu.VMEM((pairs + 1, channels, cells), F32)]
+        + buffers
+        + [pltpu.SemaphoreType.DMA((chunk_count,))],
+        name="staying",
+    )(table, source_fields, weight_blocks)
+    finished = pl.pallas_call(
+        functools.partial(merge_kernel, count, cap, mcap),
+        out_shape=jax.ShapeDtypeStruct((count, 5, mcap, cells), BF16),
+        in_specs=[smem, smem, hbm, vmem, vmem],
+        out_specs=vmem,
+        scratch_shapes=[
+            pltpu.VMEM((pairs + 1, channels, cells), F32),
+            pltpu.VMEM((5, count * mcap + 8, cells), F32),
+            pltpu.SemaphoreType.DMA((chunk_count,)),
+        ],
+        name="merge",
+    )(table, entry, local, came, moments)
+    arrived = lax.all_to_all(finished, "lon", split_axis=0, concat_axis=0, tiled=True)
+    wide = LON_DEV // cells
+    where = spot.reshape(-1)[:blocks].reshape(LAT_DEV, wide).T.reshape(blocks, 1)
+    return pl.pallas_call(
+        functools.partial(spread_kernel, count, mcap),
+        out_shape=jax.ShapeDtypeStruct((5, LAT_DEV, LON_DEV), BF16),
+        in_specs=[vmem, vmem],
+        out_specs=vmem,
+        scratch_shapes=[pltpu.VMEM((count * mcap, 5 * cells), BF16)],
+        name="spread",
+    )(where, arrived)
+
+
+def padded_exchange(source_fields, weight_blocks, pair_source, targets, pair_block):
     lon_count = lax.axis_size("lon")
     pair_count = pair_source.shape[0]
     capacity = max(2, 2 * pair_count // lon_count)
-    blocks_dev = source_fields.shape[0]
-    channels = source_fields.shape[1]
-    cell_count = source_fields.shape[2]
-    targets = pair_target[:, 0]
+    blocks_dev, channels, cell_count = source_fields.shape
     lanes = jnp.arange(lon_count, dtype=jnp.int32)
     matches = (targets[:, None] == lanes[None, :]).astype(jnp.int32)
     earlier = jnp.cumsum(matches, axis=0) - matches
@@ -88,15 +578,32 @@
             (temper * moist).sum(1),
         ]
     )
-    moments = moments.reshape(5, LAT_DEV, LON_DEV)
+    return moments.reshape(5, LAT_DEV, LON_DEV).astype(BF16)
+
+
+def local(source_fields, weight_blocks, pair_source, pair_target, pair_block):
+    count = lax.axis_size("lon")
+    blocks, channels, _ = source_fields.shape
+    days = channels // 2
+    pairs = pair_source.shape[0]
+    share = -(-pairs // count)
+    cap = share
+    mcap = -(-share * 3 // 2 // 16) * 16
+    targets = pair_target[:, 0]
+    keys = targets * blocks + pair_block
+    all_keys = lax.all_to_all(
+        jnp.broadcast_to(keys[None, :], (count, pairs)), "lon", split_axis=0, concat_axis=0, tiled=True
+    )
+    table, entry, spot = make_plan(all_keys, pair_source, count, blocks, cap, mcap)
+    moments = lax.cond(
+        table[4, 3] == 0,
+        lambda: direct(cap, mcap, source_fields, weight_blocks, table, entry, spot),
+        lambda: padded_exchange(source_fields, weight_blocks, pair_source, targets, pair_block),
+    )
     lon_band = band_matrix(LON_DEV)
     lat_band = band_matrix(LAT_DEV)
-    taller = padded(moments.astype(jnp.bfloat16), (("lat", 1),), WINDOW_HALF, False).astype(
-        moments.dtype
-    )
-    wider = padded(taller.astype(jnp.bfloat16), (("lon", 2),), WINDOW_HALF, True).astype(
-        taller.dtype
-    )
+    taller = padded(moments, (("lat", 1),), WINDOW_HALF, False)
+    wider = padded(taller, (("lon", 2),), WINDOW_HALF, True).astype(F32)
     smoothed = smooth_lat(smooth_lon(wider, lon_band), lat_band)
     kernel = gaussian_taps()
     height = LAT_DEV * lax.axis_size("lat")

time: 398 us -> 176 us (0.44)
  other arithmetic: 112 us -> 2.32 us
  waiting for transfers between devices: 186 us -> 99.7 us
  local copies, waits for them, and re-layouts: 58 us -> 3.55 us
  Pallas kernels: 0 us -> 37.7 us
  matrix products: 16.4 us -> 2.7 us
  starting transfers between devices: 22.7 us -> 28.9 us
    all_to_all x2 -> x3, waiting for transfers between devices: 179 us -> 93.1 us  [the longest x1 76.7 us: direct(): lax.all_to_all(packed.reshape(count, cap, channels, cells), 'lon', split_...]
    scatter-add x1 -> x0, other arithmetic: 79.6 us -> none  [local(): jax.ops.segment_sum(received.reshape(lon_count * capacity, channels, cell...]
    scatter x2 -> x0, local copies, waits for them, and re-layouts: 38.9 us -> none  [the longest x1 37.4 us: local(): jnp.zeros((lon_count * capacity, channels, cell_count), jnp.float32)]
    pallas_call x0 -> x5, Pallas kernels: none -> 37.7 us  [the longest x1 14.1 us: direct(): pl.pallas_call(functools.partial(local_kernel, sends), out_shape=(jax.Sha...]
    dot_general x1 -> x0, matrix products: 13.7 us -> none  [local(): jnp.einsum('pck,pjk->pcj', picked, weight_blocks, preferred_element_type=...]
    broadcast_in_dim x2 -> x1, local copies, waits for them, and re-layouts: 12.1 us -> 0.6 us  [local(): jnp.broadcast_to(keys[None, :], (count, pairs))]
    reshape x1 -> x0, other arithmetic: 11.3 us -> none  [local(): received.reshape(lon_count * capacity, channels, cell_count)]
    convert_element_type x2 -> x0, other arithmetic: 10.1 us -> none  [the longest x1 9.44 us: local(): packed.reshape(lon_count, capacity, channels, cell_count)]
  transfers between devices with their start and end apart: 6 -> 7, of which waited for: 4 -> 6; matrix products, arithmetic and copies ran while one was open for 19% -> 1% of each run, Pallas kernels for 0% -> 8%
where the time goes in v1:
time: 176 us
  waiting for transfers between devices  99.7 us (57%)
  Pallas kernels  37.7 us (21%)
  starting transfers between devices  28.9 us (16%)
  local copies, waits for them, and re-layouts  3.55 us (2%)
  matrix products  2.7 us (2%)
  other arithmetic  2.32 us (1%)
    all_to_all x1, waiting for transfers between devices, direct(): lax.all_to_all(packed.reshape(count, cap, channels, cells), 'lon', split_...  76.7 us
    pallas_call x1, Pallas kernels, direct(): pl.pallas_call(functools.partial(local_kernel, sends), out_shape=(jax.Sha...  14.1 us
    all_to_all x1, waiting for transfers between devices, direct(): lax.all_to_all(finished, 'lon', split_axis=0, concat_axis=0, tiled=True)  12.3 us
    pallas_call x1, Pallas kernels, direct(): pl.pallas_call(functools.partial(send_kernel, sends), out_shape=jax.Shape...  11.3 us
    all_to_all x1, starting transfers between devices, direct(): lax.all_to_all(finished, 'lon', split_axis=0, concat_axis=0, tiled=True)  6.86 us
    all_to_all x1, starting transfers between devices, local(): lax.all_to_all(jnp.broadcast_to(keys[None, :], (count, pairs)), 'lon', sp...  6.34 us
    pallas_call x1, Pallas kernels, direct(): pl.pallas_call(functools.partial(merge_kernel, count, cap, mcap), out_sha...  6.19 us
    ppermute x2, starting transfers between devices, padded(): before = lax.ppermute(last, axis, up)  6.17 us
  transfers between devices with their start and end apart: 7, of which 6 were waited for; matrix products, arithmetic and copies ran while one was open for 1% of the time, Pallas kernels for 8%

profile of v1, /device:TPU:1, one launch (start us, length us, event | category | flops | bytes accessed | tf_op | source)
XLA Modules:
  0.0 176.4 jit_solution(963412927684555115)
XLA Ops:
  0.0 0.7 multiply_add_fusion
  0.7 0.6 broadcast_in_dim.23
  1.3 6.3 %all-to-all-start.4 = ((s32[8,1,256]{2,1,0:T(1,128)}), s32[8,1,256]{2,1,0:T(1,128)S(1)}, u32[]{:S(2)}, u32[]{:S(2)}) async-start(s32[8,1,256]{2,1,0:T(1,128)} %broadcast_in_dim.23), calls=%async_computation.4 | async-start | bytes 16384 | tf_op jit(solution)/shard_map/all_to_all | solution.py:594
  7.7 0.6 fusion.60
  8.8 4.2 %all-to-all-done.4 = s32[8,1,256]{2,1,0:T(1,128)S(1)} async-done(((s32[8,1,256]{2,1,0:T(1,128)}), s32[8,1,256]{2,1,0:T(1,128)S(1)}, u32[]{:S(2)}, u32[]{:S(2)}) %all-to-all-start.4) | async-done | bytes 8224 | tf_op jit(solution)/shard_map/all_to_all | solution.py:594
  13.0 0.6 copy.15
  13.6 4.6 %plan.1 = (s32[8,256]{1,0:T(8,128)S(1)}, s32[40,128]{1,0:T(8,128)S(1)}, s32[8,128]{1,0:T(8,128)S(1)}) custom-call(s32[1]{0:T(128)} %bitcast.9.me_ref, s32[8,256]{1,0:T(8,128)} %bitcast.80, s32[1,256]{1,0:T(1,128)} %bitcast.86), custom_call_target="tpu_custom_call" | custom-call | tf_op jit(solution)/shard_map/plan/pallas_call | solution.py:256
  18.2 0.6 slice.46
  19.5 135.5 %conditional.1 = (bf16[5,64,512]{2,1,0:T(8,128)(2,1)S(1)}) conditional(s32[]{:T(128)} %bitcast.12, (s32[256]{0:T(256)}, s32[256,1]{0,1:T(1,128)}, s32[256]{0:T(256)}, s32[256]{0:T(256)}, bf16[256,64,128]{2,1,0:T(8,128)(2,1)}, /*index=5*/bf16[256,128,128]{2,1,0:T(8,128)(2,1)}) %tuple.21, (s32[8,128]{1,0:T(8,128)S(1)}, s32[8,256]{1,0:T(8,128)S(1)}, ...), branch_computations={%region_0.12_spmd, %region_12.13_spmd} | conditional | flops 557957888 | bytes 215623744 | solution.py:598
  19.7 11.3 %leaving.1 = bf16[256,64,128]{2,1,0:T(8,128)(2,1)} custom-call(s32[8,256]{1,0:T(8,128)S(1)} %get-tuple-element.37.table, bf16[256,64,128]{2,1,0:T(8,128)(2,1)} %get-tuple-element.39.src, bf16[256,128,128]{2,1,0:T(8,128)(2,1)} %get-tuple-element.40.weights), custom_call_target="tpu_custom_call" | custom-call | tf_op jit(solution)/shard_map/cond/branch_1_fun/leaving/pallas_call | solution.py:488
  31.0 4.6 %all-to-all-start = ((bf16[8,32,64,128]{3,2,1,0:T(8,128)(2,1)}), bf16[8,32,64,128]{3,2,1,0:T(8,128)(2,1)}, u32[]{:S(2)}, u32[]{:S(2)}) async-start(bf16[8,32,64,128]{3,2,1,0:T(8,128)(2,1)} %bitcast.78), calls=%async_computation | async-start | bytes 8388608 | tf_op jit(solution)/shard_map/cond/branch_1_fun/all_to_all | solution.py:496
  35.6 14.1 %staying.1 = (f32[256,64,128]{2,1,0:T(8,128)}, f32[5,392,128]{2,1,0:T(8,128)}) custom-call(s32[8,256]{1,0:T(8,128)S(1)} %get-tuple-element.37.table, bf16[256,64,128]{2,1,0:T(8,128)(2,1)} %get-tuple-element.39.src, bf16[256,128,128]{2,1,0:T(8,128)(2,1)} %get-tuple-element.40.weights), custom_call_target="tpu_custom_call" | custom-call | tf_op jit(solution)/shard_map/cond/branch_1_fun/staying/pallas_call | solution.py:500
  49.7 76.7 %all-to-all-done = bf16[8,32,64,128]{3,2,1,0:T(8,128)(2,1)} async-done(((bf16[8,32,64,128]{3,2,1,0:T(8,128)(2,1)}), bf16[8,32,64,128]{3,2,1,0:T(8,128)(2,1)}, u32[]{:S(2)}, u32[]{:S(2)}) %all-to-all-start) | async-done | bytes 4194336 | tf_op jit(solution)/shard_map/cond/branch_1_fun/all_to_all | solution.py:496
  126.4 6.2 %merge.1 = bf16[8,5,48,128]{3,2,1,0:T(8,128)(2,1)} custom-call(s32[8,256]{1,0:T(8,128)S(1)} %get-tuple-element.37.table, s32[40,128]{1,0:T(8,128)S(1)} %get-tuple-element.38.entry, f32[256,64,128]{2,1,0:T(8,128)} %get-tuple-element.41.local_ref, bf16[256,64,128]{2,1,0:T(8,128)(2,1)} %bitcast.8.came, f32[5,392,128]{2,1,0:T(8,128)} %get-tuple-element.42.moments_in), custom_call_target="tpu_custom_call" | custom-call | tf_op jit(solution)/shard_map/cond/branch_1_fun/merge/pallas_call | solution.py:513
  132.6 6.9 %all-to-all-start.1 = ((bf16[8,5,48,128]{3,2,1,0:T(8,128)(2,1)}), bf16[8,5,48,128]{3,2,1,0:T(8,128)(2,1)S(1)}, u32[]{:S(2)}, u32[]{:S(2)}) async-start(bf16[8,5,48,128]{3,2,1,0:T(8,128)(2,1)} %merge.1), calls=%async_computation.1 | async-start | bytes 983040 | tf_op jit(solution)/shard_map/cond/branch_1_fun/all_to_all | solution.py:525
  139.5 0.1 reshape.87
  139.6 0.1 copy.11
  139.7 0.8 reshape.132.spot_ref
  140.5 12.3 %all-to-all-done.1.came = bf16[8,5,48,128]{3,2,1,0:T(8,128)(2,1)S(1)} async-done(((bf16[8,5,48,128]{3,2,1,0:T(8,128)(2,1)}), bf16[8,5,48,128]{3,2,1,0:T(8,128)(2,1)S(1)}, u32[]{:S(2)}, u32[]{:S(2)}) %all-to-all-start.1) | async-done | bytes 491552 | tf_op jit(solution)/shard_map/cond/branch_1_fun/all_to_all | solution.py:525
  152.7 0.0 copy-start
  152.7 0.8 copy-done
  153.5 1.5 spread.1
  155.0 4.9 %collective-permute-start = (bf16[5,16,512]{2,1,0:T(8,128)(2,1)S(1)}, bf16[5,16,512]{2,1,0:T(8,128)(2,1)S(1)}, u32[]{:S(2)}, u32[]{:S(2)}) collective-permute-start(bf16[5,16,512]{2,1,0:T(8,128)(2,1)S(1)} %get-tuple-element.56), channel_id=1, source_target_pairs={{0,8},{8,16},{16,24},{1,9},{9,17},{17,25},{2,10},{10,18},{18,26},{... | collective-permute-start | bytes 245768 | tf_op jit(solution)/shard_map/ppermute | solution.py:29
  160.0 1.9 %collective-permute-start.1 = (bf16[5,16,512]{2,1,0:T(8,128)(2,1)S(1)}, bf16[5,16,512]{2,1,0:T(8,128)(2,1)S(1)}, u32[]{:S(2)}, u32[]{:S(2)}) collective-permute-start(bf16[5,16,512]{2,1,0:T(8,128)(2,1)S(1)} %get-tuple-element.57), channel_id=1, source_target_pairs={{8,0},{16,8},{24,16},{9,1},{17,9},{25,17},{10,2},{18,10},{26,18},{... | collective-permute-start | bytes 245768 | tf_op jit(solution)/shard_map/ppermute | solution.py:30
  161.9 0.1 select_reduce_fusion
  162.0 0.0 collective-permute-done
  162.0 3.7 %collective-permute-done.1 = bf16[5,16,512]{2,1,0:T(8,128)(2,1)S(1)} collective-permute-done((bf16[5,16,512]{2,1,0:T(8,128)(2,1)S(1)}, bf16[5,16,512]{2,1,0:T(8,128)(2,1)S(1)}, u32[]{:S(2)}, u32[]{:S(2)}) %collective-permute-start.1) | collective-permute-done | bytes 81952 | tf_op jit(solution)/shard_map/ppermute | solution.py:30
  165.7 0.1 pad_maximum_fusion.2
  165.8 1.2 collective-permute-start.2
  167.1 3.0 %collective-permute-start.3 = (bf16[5,96,16]{2,1,0:T(8,128)(2,1)S(1)}, bf16[5,96,16]{2,1,0:T(8,128)(2,1)S(1)}, u32[]{:S(2)}, u32[]{:S(2)}) collective-permute-start(bf16[5,96,16]{2,1,0:T(8,128)(2,1)S(1)} %get-tuple-element.55), channel_id=1, source_target_pairs={{1,0},{2,1},{3,2},{4,3},{5,4},{6,5},{7,6},{0,7},{9,8},{10,9},{11,1... | collective-permute-start | bytes 46088 | tf_op jit(solution)/shard_map/ppermute | solution.py:30
  170.1 2.4 %collective-permute-done.2 = bf16[5,96,16]{2,1,0:T(8,128)(2,1)S(1)} collective-permute-done((bf16[5,96,16]{2,1,0:T(8,128)(2,1)S(1)}, bf16[5,96,16]{2,1,0:T(8,128)(2,1)S(1)}, u32[]{:S(2)}, u32[]{:S(2)}) %collective-permute-start.2) | collective-permute-done | bytes 15392 | tf_op jit(solution)/shard_map/ppermute | solution.py:29
  172.4 0.5 collective-permute-done.3
  172.9 1.9 %fusion.9 = f32[5,96,512]{2,1,0:T(8,128)S(1)} fusion(bf16[5,96,16]{2,1,0:T(8,128)(2,1)S(1)} %collective-permute-done.3, bf16[5,16,512]{2,1,0:T(8,128)(2,1)S(1)} %collective-permute-done.1, bf16[5,64,512]{2,1,0:T(8,128)(2,1)S(1)} %get-tuple-element.58, bf16[5,16,512]{2,1,0:T(8,128)(2,1)S(1)} %collective-permute-done, ...), kind=kOutput, calls=%fused_computation.33 | convolution fusion | flops 1609439232 | bytes 1505280 | tf_op jit(solution)/shard_map/krb,bj->krj/dot_general | solution.py:49
  174.8 0.8 convolution_bitcast_fusion
  175.6 0.8 fusion.34
  (5 shorter events, 0.0 us)
Async XLA Ops:
  1.3 11.7 %all-to-all-start.4 = ((s32[8,1,256]{2,1,0:T(1,128)}), s32[8,1,256]{2,1,0:T(1,128)S(1)}, u32[]{:S(2)}, u32[]{:S(2)}) async-start(s32[8,1,256]{2,1,0:T(1,128)} %broadcast_in_dim.23), calls=%async_computation.4 | async-start | bytes 16384 | tf_op jit(solution)/shard_map/all_to_all | solution.py:594
  31.0 95.4 %all-to-all-start = ((bf16[8,32,64,128]{3,2,1,0:T(8,128)(2,1)}), bf16[8,32,64,128]{3,2,1,0:T(8,128)(2,1)}, u32[]{:S(2)}, u32[]{:S(2)}) async-start(bf16[8,32,64,128]{3,2,1,0:T(8,128)(2,1)} %bitcast.78), calls=%async_computation | async-start | bytes 8388608 | tf_op jit(solution)/shard_map/cond/branch_1_fun/all_to_all | solution.py:496
  132.6 20.1 %all-to-all-start.1 = ((bf16[8,5,48,128]{3,2,1,0:T(8,128)(2,1)}), bf16[8,5,48,128]{3,2,1,0:T(8,128)(2,1)S(1)}, u32[]{:S(2)}, u32[]{:S(2)}) async-start(bf16[8,5,48,128]{3,2,1,0:T(8,128)(2,1)} %merge.1), calls=%async_computation.1 | async-start | bytes 983040 | tf_op jit(solution)/shard_map/cond/branch_1_fun/all_to_all | solution.py:525
  152.7 0.8 copy-start
  155.0 7.0 %collective-permute-start = (bf16[5,16,512]{2,1,0:T(8,128)(2,1)S(1)}, bf16[5,16,512]{2,1,0:T(8,128)(2,1)S(1)}, u32[]{:S(2)}, u32[]{:S(2)}) collective-permute-start(bf16[5,16,512]{2,1,0:T(8,128)(2,1)S(1)} %get-tuple-element.56), channel_id=1, source_target_pairs={{0,8},{8,16},{16,24},{1,9},{9,17},{17,25},{2,10},{10,18},{18,26},{... | collective-permute-start | bytes 245768 | tf_op jit(solution)/shard_map/ppermute | solution.py:29
  160.0 5.8 %collective-permute-start.1 = (bf16[5,16,512]{2,1,0:T(8,128)(2,1)S(1)}, bf16[5,16,512]{2,1,0:T(8,128)(2,1)S(1)}, u32[]{:S(2)}, u32[]{:S(2)}) collective-permute-start(bf16[5,16,512]{2,1,0:T(8,128)(2,1)S(1)} %get-tuple-element.57), channel_id=1, source_target_pairs={{8,0},{16,8},{24,16},{9,1},{17,9},{25,17},{10,2},{18,10},{26,18},{... | collective-permute-start | bytes 245768 | tf_op jit(solution)/shard_map/ppermute | solution.py:30
  165.8 6.6 %collective-permute-start.2 = (bf16[5,96,16]{2,1,0:T(8,128)(2,1)S(1)}, bf16[5,96,16]{2,1,0:T(8,128)(2,1)S(1)}, u32[]{:S(2)}, u32[]{:S(2)}) collective-permute-start(bf16[5,96,16]{2,1,0:T(8,128)(2,1)S(1)} %get-tuple-element.54), channel_id=1, source_target_pairs={{0,1},{1,2},{2,3},{3,4},{4,5},{5,6},{6,7},{7,0},{8,9},{9,10},{10,1... | collective-permute-start | bytes 46088 | tf_op jit(solution)/shard_map/ppermute | solution.py:29
  167.1 5.8 %collective-permute-start.3 = (bf16[5,96,16]{2,1,0:T(8,128)(2,1)S(1)}, bf16[5,96,16]{2,1,0:T(8,128)(2,1)S(1)}, u32[]{:S(2)}, u32[]{:S(2)}) collective-permute-start(bf16[5,96,16]{2,1,0:T(8,128)(2,1)S(1)} %get-tuple-element.55), channel_id=1, source_target_pairs={{1,0},{2,1},{3,2},{4,3},{5,4},{6,5},{7,6},{0,7},{9,8},{10,9},{11,1... | collective-permute-start | bytes 46088 | tf_op jit(solution)/shard_map/ppermute | solution.py:30

commit v2 on v1

--- a/solution.py
+++ b/solution.py
@@ -87,7 +87,7 @@
 
 
 def plan_kernel(
-    count, blocks, cap, mcap, me_ref, keys_ref, src_ref, table_ref, entry_ref, spot_ref, pres
+    count, blocks, cap, mcap, me_ref, keys_ref, src_ref, table_ref, entry_ref, spot_ref, pres, tall
 ):
     me = me_ref[0]
     pairs = keys_ref.shape[1]
@@ -98,29 +98,70 @@
     def held(d, carry):
         high, low = one_hots(keys_ref[pl.ds(d, 1), :], height)
         found = dot(high.astype(BF16), low.astype(BF16), ((1,), (1,)))
-        pres[d] = (found > 0.5).astype(F32)
+        found = (found > 0.5).astype(F32)
+        pres[d] = found
+        tall[pl.ds(d, height, stride=count), :] = found
         return carry
 
     repeat(count, held, 0)
 
     row_at = iota((height, LANES), 0)
-    turn = (row_at * LANES + iota((height, LANES), 1)) % count
-
     zero = jnp.zeros((height, LANES), F32)
     holders = repeat(count, lambda d, total: total + pres[d], zero)
-
-    def choose(d, carry):
-        best, owner = carry
-        rank = (d - turn + count) % count
-        rank = jnp.where(pres[d] > 0.5, rank, 4 * count)
-        better = rank < best
-        return jnp.where(better, rank, best), jnp.where(better, d, owner)
-
-    _, owner = repeat(
-        count,
-        choose,
-        (jnp.full((height, LANES), 4 * count, I32), jnp.full((height, LANES), -1, I32)),
-    )
+    device = iota((count, LANES), 0)
+    turn = (device + count - iota((count, LANES), 1) % count) % count
+    turn = turn.astype(F32)
+    others = [(device != s).astype(F32) for s in range(count)]
+
+    part = iota((count, LANES), 1) * 2 // LANES
+    halves = [(part == h).astype(F32) for h in range(2)]
+
+    def expect(r, sums):
+        here = tall[pl.ds(pl.multiple_of(r * count, count), count), :]
+        even = here / jnp.maximum(jnp.sum(here, axis=0, keepdims=True), 1.0)
+        return tuple(sums[s] + even * here[s : s + 1, :] for s in range(count))
+
+    nothing = tuple(jnp.zeros((count, LANES), F32) for _ in range(count))
+    sums = lax.fori_loop(0, height, expect, nothing)
+    loads = tuple(
+        jnp.broadcast_to(jnp.sum(sums[s], axis=1, keepdims=True), (count, LANES)) * others[s]
+        for s in range(count)
+    )
+
+    def settle(r, loads):
+        rows = pl.ds(pl.multiple_of(r * count, count), count)
+        here = tall[rows, :]
+        even = here / jnp.maximum(jnp.sum(here, axis=0, keepdims=True), 1.0)
+        picks = jnp.zeros((count, LANES), F32)
+        for half in halves:
+            cost = jnp.zeros((count, LANES), F32)
+            for s in range(count):
+                growth = loads[s] * loads[s]
+                cost = cost + growth * growth * here[s : s + 1, :]
+            cost = jnp.where(here > 0.5, cost, 1e30)
+            best = jnp.min(cost, axis=0, keepdims=True)
+            place_in_turn = jnp.where(cost == best, turn, 1e30)
+            nearest = jnp.min(place_in_turn, axis=0, keepdims=True)
+            pick = jnp.where(place_in_turn == nearest, here, 0.0) * half
+            picks = picks + pick
+            change = pick - even * half
+            loads = tuple(
+                loads[s] + others[s] * jnp.sum(change * here[s : s + 1, :], axis=1, keepdims=True)
+                for s in range(count)
+            )
+        tall[rows, :] = picks
+        return loads
+
+    loads = lax.fori_loop(0, height, settle, loads)
+    worst = loads[0]
+    for s in range(1, count):
+        worst = jnp.maximum(worst, loads[s])
+    worst = jnp.max(jnp.max(worst, axis=1, keepdims=True), axis=0, keepdims=True)
+
+    def own(d, owner):
+        return jnp.where(tall[pl.ds(d, height, stride=count), :] > 0.5, d, owner)
+
+    owner = repeat(count, own, jnp.full((height, LANES), -1, I32))
 
     ahead = (iota((LANES, LANES), 0) < iota((LANES, LANES), 1)).astype(BF16)
     ones = jnp.ones((LANES, LANES), BF16)
@@ -186,25 +227,8 @@
     pick = (iota((8, height), 1) == me * tile_rows + iota((8, height), 0)).astype(F32)
     spot_ref[...] = (dot(pick, finished, exact=True) + 0.5).astype(I32) - 1
 
-    wide = -(-count // 8) * 8
-    which = iota((wide, LANES), 0)
-    which_one = iota((wide, 1), 0)
-
-    def load_of(s, worst):
-        here = pres[s]
-
-        def into(d, sums):
-            part = jnp.sum(here * (owner == d).astype(F32), axis=0, keepdims=True)
-            return jnp.where(which == d, part, sums)
-
-        sums = repeat(count, into, jnp.zeros((wide, LANES), F32))
-        loads = jnp.sum(sums, axis=1, keepdims=True)
-        return jnp.maximum(worst, jnp.where(which_one == s, 0.0, loads))
-
-    worst = repeat(count, load_of, jnp.zeros((wide, 1), F32))
-    worst = jnp.max(worst, axis=0, keepdims=True)
     most = jnp.max(jnp.max(most, axis=1, keepdims=True), axis=0, keepdims=True)
-    over = jnp.where((worst > cap + 0.5) | (most > mcap + 0.5), 1, 0)
+    over = jnp.where((worst > cap + 0.25) | (most > mcap + 0.5), 1, 0)
 
     place = place + several * (sends + rank_several + 1.0)
     place = place + single * (sends + total_several + rank_single + 1.0)
@@ -214,18 +238,20 @@
     goes = look_up(place, high, low) - 1.0
     lands = look_up(moment_place, high, low)
     leaves = (goes < sends - 0.5).astype(F32)
-    square = (iota((pairs, pairs), 0) < iota((pairs, pairs), 1)).astype(BF16)
-    before = dot(jnp.broadcast_to(leaves, (8, pairs)).astype(BF16), square)[0:1, :]
     leaving = jnp.sum(leaves, axis=1, keepdims=True)
+    first_at, second_at = iota((pairs, pairs), 0), iota((pairs, pairs), 1)
+    same = (first_at == second_at).astype(F32)
+    upright = dot(same, jnp.broadcast_to(goes, (8, pairs)), ((1,), (1,)), exact=True)[:, 0:1]
+    earlier = (upright < goes - 0.5) | ((jnp.abs(upright - goes) < 0.5) & (first_at < second_at))
+    position = jnp.sum(earlier.astype(F32), axis=0, keepdims=True)
     at = iota((1, pairs), 1).astype(F32)
-    position = jnp.where(leaves > 0.5, before, leaving + at - before)
     kind = iota((8, pairs), 0)
     values = jnp.where(
         kind == 0,
         at,
         jnp.where(kind == 1, goes, jnp.where(kind == 2, src_ref[...].astype(F32), 0.0)),
     )
-    column_at = iota((pairs, pairs), 0)
+    column_at = first_at
     order = (column_at == (position + 0.5).astype(I32)).astype(F32)
     ordered = dot(values, order, ((1,), (1,)), exact=True)
     slot = jnp.where(leaves > 0.5, -1, (goes - sends + 0.5).astype(I32))
@@ -262,7 +288,10 @@
         ),
         in_specs=[pl.BlockSpec(memory_space=pltpu.SMEM), vmem, vmem],
         out_specs=(vmem, vmem, vmem),
-        scratch_shapes=[pltpu.VMEM((count, height, LANES), F32)],
+        scratch_shapes=[
+            pltpu.VMEM((count, height, LANES), F32),
+            pltpu.VMEM((height * count, LANES), F32),
+        ],
         name="plan",
     )(lax.axis_index("lon").astype(I32)[None], keys, pair_source[None, :])
 
@@ -275,7 +304,7 @@
     )
 
 
-def products(table, src, weights, xs, ws, x_sem, w_sem, low, high, target, first, last, dummy, while_loading):
+def products(table, src, weights, xs, ws, x_sem, w_sem, low, high, target, packed, first, last, dummy):
     copies = functools.partial(pair_copies, table, src, weights, xs, ws, x_sem, w_sem)
 
     def start(i):
@@ -290,7 +319,6 @@
         return carry
 
     lax.fori_loop(low, low + RING, prime, 0)
-    while_loading()
 
     def step(g, carry):
         base = g * GROUP
@@ -302,10 +330,15 @@
             slot = (base + u) % RING
             results.append(dot(xs[slot], ws[slot], ((1,), (1,))))
         for u in range(GROUP):
-            place = table[1, base + u]
+            i = base + u
+            place = table[1, i]
+            again = (i > low) & (table[1, jnp.maximum(i - 1, 0)] == place)
             inside = (place >= first) & (place < last)
             where = jnp.where(inside, place - first, dummy)
-            target[where] = target[where] + results[u]
+            value = results[u] + jnp.where(again, target[where], 0.0)
+            target[where] = value
+            if packed is not None:
+                packed[where] = value.astype(BF16)
 
         @pl.when(base + RING < high)
         def _():
@@ -317,26 +350,13 @@
     lax.fori_loop(low // GROUP, high // GROUP, step, 0)
 
 
-def send_kernel(sends, table, src, weights, out_ref, total, xs, ws, x_sem, w_sem):
+def send_kernel(sends, table, src, weights, out_ref, total, packed, xs, ws, x_sem, w_sem, out_sem):
     leaving = table[4, 0]
     high = (leaving + GROUP - 1) // GROUP * GROUP
-
-    def clear():
-        def one(i, carry):
-            total[i] = jnp.zeros(total.shape[1:], F32)
-            return carry
-
-        lax.fori_loop(0, sends, one, 0)
-
-    products(
-        table, src, weights, xs, ws, x_sem, w_sem, 0, high, total, 0, sends, sends, clear
-    )
-
-    def finish(i, carry):
-        out_ref[i] = total[i].astype(BF16)
-        return carry
-
-    lax.fori_loop(0, sends, finish, 0)
+    products(table, src, weights, xs, ws, x_sem, w_sem, 0, high, total, packed, 0, sends, sends)
+    out = pltpu.make_async_copy(packed.at[pl.ds(0, sends)], out_ref, out_sem)
+    out.start()
+    out.wait()
 
 
 def moment_rows(value):
@@ -374,29 +394,9 @@
     leaving, owned, several = table[4, 0], table[4, 1], table[4, 2]
     low = leaving // GROUP * GROUP
 
-    def clear():
-        def one(i, carry):
-            total[i] = jnp.zeros(total.shape[1:], F32)
-            return carry
-
-        lax.fori_loop(0, owned, one, 0)
-        moments[...] = jnp.zeros(moments.shape, F32)
-
+    moments[...] = jnp.zeros(moments.shape, F32)
     products(
-        table,
-        src,
-        weights,
-        xs,
-        ws,
-        x_sem,
-        w_sem,
-        low,
-        pairs,
-        total,
-        sends,
-        sends + pairs,
-        pairs,
-        clear,
+        table, src, weights, xs, ws, x_sem, w_sem, low, pairs, total, None, sends, sends + pairs, pairs
     )
     chunks = (several + CHUNK - 1) // CHUNK
 
@@ -489,8 +489,13 @@
         functools.partial(send_kernel, sends),
         out_shape=jax.ShapeDtypeStruct((sends, channels, cells), BF16),
         in_specs=[smem, hbm, hbm],
-        out_specs=vmem,
-        scratch_shapes=[pltpu.VMEM((sends + 1, channels, cells), F32)] + buffers,
+        out_specs=hbm,
+        scratch_shapes=[
+            pltpu.VMEM((sends + 1, channels, cells), F32),
+            pltpu.VMEM((sends + 1, channels, cells), BF16),
+        ]
+        + buffers
+        + [pltpu.SemaphoreType.DMA],
         name="leaving",
     )(table, source_fields, weight_blocks)
     came = lax.all_to_all(
@@ -587,7 +592,7 @@
     days = channels // 2
     pairs = pair_source.shape[0]
     share = -(-pairs // count)
-    cap = share
+    cap = max(share * 17 // 32, min(share, 8))
     mcap = -(-share * 3 // 2 // 16) * 16
     targets = pair_target[:, 0]
     keys = targets * blocks + pair_block

time: 176 us -> 135 us (0.77)
  waiting for transfers between devices: 99.7 us -> 57.8 us
    all_to_all x1, waiting for transfers between devices: 76.7 us -> 35.2 us  [direct(): lax.all_to_all(packed.reshape(count, cap, channels, cells), 'lon', split_...]
    pallas_call x1, Pallas kernels: 4.61 us -> 8.82 us  [make_plan(): pl.pallas_call(functools.partial(plan_kernel, count, blocks, cap, mcap),...]
    pallas_call x1, Pallas kernels: 11.3 us -> 8.03 us  [direct(): pl.pallas_call(functools.partial(send_kernel, sends), out_shape=jax.Shape...]
  transfers between devices with their start and end apart: 7 -> 7, of which waited for: 6 -> 6; matrix products, arithmetic and copies ran while one was open for 1% -> 1% of each run, Pallas kernels for 8% -> 10%
where the time goes in v2:
time: 135 us
  waiting for transfers between devices  57.8 us (43%)
  Pallas kernels  37.8 us (28%)
  starting transfers between devices  27.3 us (20%)
  local copies, waits for them, and re-layouts  4.98 us (4%)
  matrix products  2.69 us (2%)
  other arithmetic  2.32 us (2%)
    all_to_all x1, waiting for transfers between devices, direct(): lax.all_to_all(packed.reshape(count, cap, channels, cells), 'lon', split_...  35.2 us
    pallas_call x1, Pallas kernels, direct(): pl.pallas_call(functools.partial(local_kernel, sends), out_shape=(jax.Sha...  13.7 us
    all_to_all x1, waiting for transfers between devices, direct(): lax.all_to_all(finished, 'lon', split_axis=0, concat_axis=0, tiled=True)  11.8 us
    pallas_call x1, Pallas kernels, make_plan(): pl.pallas_call(functools.partial(plan_kernel, count, blocks, cap, mcap),...  8.82 us
    pallas_call x1, Pallas kernels, direct(): pl.pallas_call(functools.partial(send_kernel, sends), out_shape=jax.Shape...  8.03 us
    ppermute x2, starting transfers between devices, padded(): before = lax.ppermute(last, axis, up)  6.74 us
    all_to_all x1, starting transfers between devices, local(): lax.all_to_all(jnp.broadcast_to(keys[None, :], (count, pairs)), 'lon', sp...  6.34 us
    pallas_call x1, Pallas kernels, direct(): pl.pallas_call(functools.partial(merge_kernel, count, cap, mcap), out_sha...  5.73 us
  transfers between devices with their start and end apart: 7, of which 6 were waited for; matrix products, arithmetic and copies ran while one was open for 1% of the time, Pallas kernels for 10%

profile of v2, /device:TPU:1, one launch (start us, length us, event | category | flops | bytes accessed | tf_op | source)
XLA Modules:
  0.0 134.6 jit_solution(158133225423485732)
XLA Ops:
  0.0 0.7 multiply_add_fusion
  0.7 0.6 broadcast_in_dim.23
  1.3 6.3 %all-to-all-start.4 = ((s32[8,1,256]{2,1,0:T(1,128)}), s32[8,1,256]{2,1,0:T(1,128)S(1)}, u32[]{:S(2)}, u32[]{:S(2)}) async-start(s32[8,1,256]{2,1,0:T(1,128)} %broadcast_in_dim.23), calls=%async_computation.4 | async-start | bytes 16384 | tf_op jit(solution)/shard_map/all_to_all | solution.py:599
  7.7 0.6 fusion.60
  8.8 4.2 %all-to-all-done.4 = s32[8,1,256]{2,1,0:T(1,128)S(1)} async-done(((s32[8,1,256]{2,1,0:T(1,128)}), s32[8,1,256]{2,1,0:T(1,128)S(1)}, u32[]{:S(2)}, u32[]{:S(2)}) %all-to-all-start.4) | async-done | bytes 8224 | tf_op jit(solution)/shard_map/all_to_all | solution.py:599
  13.0 0.6 copy.15
  13.6 8.8 %plan.1 = (s32[8,256]{1,0:T(8,128)S(1)}, s32[32,128]{1,0:T(8,128)S(1)}, s32[8,128]{1,0:T(8,128)S(1)}) custom-call(s32[1]{0:T(128)} %bitcast.9.me_ref, s32[8,256]{1,0:T(8,128)} %bitcast.81, s32[1,256]{1,0:T(1,128)} %bitcast.87), custom_call_target="tpu_custom_call" | custom-call | tf_op jit(solution)/shard_map/plan/pallas_call | solution.py:282
  22.4 0.6 slice.46
  23.7 88.9 %conditional.1 = (bf16[5,64,512]{2,1,0:T(8,128)(2,1)S(1)}) conditional(s32[]{:T(128)} %bitcast.12, (s32[256]{0:T(256)}, s32[256,1]{0,1:T(1,128)}, s32[256]{0:T(256)}, s32[256]{0:T(256)}, bf16[256,64,128]{2,1,0:T(8,128)(2,1)}, /*index=5*/bf16[256,128,128]{2,1,0:T(8,128)(2,1)}) %tuple.21, (s32[8,128]{1,0:T(8,128)S(1)}, s32[8,256]{1,0:T(8,128)S(1)}, ...), branch_computations={%region_0.12_spmd, %region_12.13_spmd} | conditional | flops 557957888 | bytes 215623744 | solution.py:603
  23.9 8.0 %leaving.1 = bf16[136,64,128]{2,1,0:T(8,128)(2,1)} custom-call(s32[8,256]{1,0:T(8,128)S(1)} %get-tuple-element.37.table, bf16[256,64,128]{2,1,0:T(8,128)(2,1)} %get-tuple-element.39.src, bf16[256,128,128]{2,1,0:T(8,128)(2,1)} %get-tuple-element.40.weights), custom_call_target="tpu_custom_call" | custom-call | tf_op jit(solution)/shard_map/cond/branch_1_fun/leaving/pallas_call | solution.py:488
  32.0 3.6 %all-to-all-start = ((bf16[8,17,64,128]{3,2,1,0:T(8,128)(2,1)}), bf16[8,17,64,128]{3,2,1,0:T(8,128)(2,1)S(1)}, u32[]{:S(2)}, u32[]{:S(2)}) async-start(bf16[8,17,64,128]{3,2,1,0:T(8,128)(2,1)} %bitcast.79), calls=%async_computation | async-start | bytes 4456448 | tf_op jit(solution)/shard_map/cond/branch_1_fun/all_to_all | solution.py:501
  35.6 13.7 %staying.1 = (f32[256,64,128]{2,1,0:T(8,128)}, f32[5,392,128]{2,1,0:T(8,128)}) custom-call(s32[8,256]{1,0:T(8,128)S(1)} %get-tuple-element.37.table, bf16[256,64,128]{2,1,0:T(8,128)(2,1)} %get-tuple-element.39.src, bf16[256,128,128]{2,1,0:T(8,128)(2,1)} %get-tuple-element.40.weights), custom_call_target="tpu_custom_call" | custom-call | tf_op jit(solution)/shard_map/cond/branch_1_fun/staying/pallas_call | solution.py:505
  49.4 35.2 %all-to-all-done = bf16[8,17,64,128]{3,2,1,0:T(8,128)(2,1)S(1)} async-done(((bf16[8,17,64,128]{3,2,1,0:T(8,128)(2,1)}), bf16[8,17,64,128]{3,2,1,0:T(8,128)(2,1)S(1)}, u32[]{:S(2)}, u32[]{:S(2)}) %all-to-all-start) | async-done | bytes 2228256 | tf_op jit(solution)/shard_map/cond/branch_1_fun/all_to_all | solution.py:501
  84.6 0.0 copy-start
  84.6 1.4 %copy-done = bf16[8,17,64,128]{3,2,1,0:T(8,128)(2,1)} copy-done((bf16[8,17,64,128]{3,2,1,0:T(8,128)(2,1)}, bf16[8,17,64,128]{3,2,1,0:T(8,128)(2,1)S(1)}, u32[]{:S(2)}) %copy-start) | copy-done | bytes 2228248 | tf_op jit(solution)/shard_map/cond
  86.0 5.7 %merge.1 = bf16[8,5,48,128]{3,2,1,0:T(8,128)(2,1)} custom-call(s32[8,256]{1,0:T(8,128)S(1)} %get-tuple-element.37.table, s32[32,128]{1,0:T(8,128)S(1)} %get-tuple-element.38.entry, f32[256,64,128]{2,1,0:T(8,128)} %get-tuple-element.41.local_ref, bf16[136,64,128]{2,1,0:T(8,128)(2,1)} %bitcast.78, f32[5,392,128]{2,1,0:T(8,128)} %get-tuple-element.42.moments_in), custom_call_target="tpu_custom_call" | custom-call | tf_op jit(solution)/shard_map/cond/branch_1_fun/merge/pallas_call | solution.py:518
  91.8 5.7 %all-to-all-start.1 = ((bf16[8,5,48,128]{3,2,1,0:T(8,128)(2,1)}), bf16[8,5,48,128]{3,2,1,0:T(8,128)(2,1)S(1)}, u32[]{:S(2)}, u32[]{:S(2)}) async-start(bf16[8,5,48,128]{3,2,1,0:T(8,128)(2,1)} %merge.1), calls=%async_computation.1 | async-start | bytes 983040 | tf_op jit(solution)/shard_map/cond/branch_1_fun/all_to_all | solution.py:530
  97.5 0.1 reshape.87
  97.6 0.1 copy.11
  97.7 0.8 reshape.132.spot_ref
  98.5 11.8 %all-to-all-done.1.came = bf16[8,5,48,128]{3,2,1,0:T(8,128)(2,1)S(1)} async-done(((bf16[8,5,48,128]{3,2,1,0:T(8,128)(2,1)}), bf16[8,5,48,128]{3,2,1,0:T(8,128)(2,1)S(1)}, u32[]{:S(2)}, u32[]{:S(2)}) %all-to-all-start.1) | async-done | bytes 491552 | tf_op jit(solution)/shard_map/cond/branch_1_fun/all_to_all | solution.py:530
  110.3 0.0 copy-start.1
  110.3 0.8 copy-done.1
  111.0 1.5 %spread.1 = bf16[5,64,512]{2,1,0:T(8,128)(2,1)S(1)} custom-call(s32[256,1]{1,0:T(8,128)} %reshape.132.spot_ref, bf16[8,5,48,128]{3,2,1,0:T(8,128)(2,1)} %copy-done.1), custom_call_target="tpu_custom_call" | custom-call | tf_op jit(solution)/shard_map/cond/branch_1_fun/spread/pallas_call | solution.py:533
  112.6 5.5 %collective-permute-start = (bf16[5,16,512]{2,1,0:T(8,128)(2,1)S(1)}, bf16[5,16,512]{2,1,0:T(8,128)(2,1)S(1)}, u32[]{:S(2)}, u32[]{:S(2)}) collective-permute-start(bf16[5,16,512]{2,1,0:T(8,128)(2,1)S(1)} %get-tuple-element.56), channel_id=1, source_target_pairs={{0,8},{8,16},{16,24},{1,9},{9,17},{17,25},{2,10},{10,18},{18,26},{... | collective-permute-start | bytes 245768 | tf_op jit(solution)/shard_map/ppermute | solution.py:29
  118.1 1.9 %collective-permute-start.1 = (bf16[5,16,512]{2,1,0:T(8,128)(2,1)S(1)}, bf16[5,16,512]{2,1,0:T(8,128)(2,1)S(1)}, u32[]{:S(2)}, u32[]{:S(2)}) collective-permute-start(bf16[5,16,512]{2,1,0:T(8,128)(2,1)S(1)} %get-tuple-element.57), channel_id=1, source_target_pairs={{8,0},{16,8},{24,16},{9,1},{17,9},{25,17},{10,2},{18,10},{26,18},{... | collective-permute-start | bytes 245768 | tf_op jit(solution)/shard_map/ppermute | solution.py:30
  120.0 0.1 select_reduce_fusion
  120.1 0.0 collective-permute-done
  120.1 3.7 %collective-permute-done.1 = bf16[5,16,512]{2,1,0:T(8,128)(2,1)S(1)} collective-permute-done((bf16[5,16,512]{2,1,0:T(8,128)(2,1)S(1)}, bf16[5,16,512]{2,1,0:T(8,128)(2,1)S(1)}, u32[]{:S(2)}, u32[]{:S(2)}) %collective-permute-start.1) | collective-permute-done | bytes 81952 | tf_op jit(solution)/shard_map/ppermute | solution.py:30
  123.9 0.1 pad_maximum_fusion.2
  124.0 1.2 collective-permute-start.2
  125.2 3.0 %collective-permute-start.3 = (bf16[5,96,16]{2,1,0:T(8,128)(2,1)S(1)}, bf16[5,96,16]{2,1,0:T(8,128)(2,1)S(1)}, u32[]{:S(2)}, u32[]{:S(2)}) collective-permute-start(bf16[5,96,16]{2,1,0:T(8,128)(2,1)S(1)} %get-tuple-element.55), channel_id=1, source_target_pairs={{1,0},{2,1},{3,2},{4,3},{5,4},{6,5},{7,6},{0,7},{9,8},{10,9},{11,1... | collective-permute-start | bytes 46088 | tf_op jit(solution)/shard_map/ppermute | solution.py:30
  128.2 2.4 %collective-permute-done.2 = bf16[5,96,16]{2,1,0:T(8,128)(2,1)S(1)} collective-permute-done((bf16[5,96,16]{2,1,0:T(8,128)(2,1)S(1)}, bf16[5,96,16]{2,1,0:T(8,128)(2,1)S(1)}, u32[]{:S(2)}, u32[]{:S(2)}) %collective-permute-start.2) | collective-permute-done | bytes 15392 | tf_op jit(solution)/shard_map/ppermute | solution.py:29
  130.5 0.5 collective-permute-done.3
  131.0 1.9 %fusion.9 = f32[5,96,512]{2,1,0:T(8,128)S(1)} fusion(bf16[5,96,16]{2,1,0:T(8,128)(2,1)S(1)} %collective-permute-done.3, bf16[5,16,512]{2,1,0:T(8,128)(2,1)S(1)} %collective-permute-done.1, bf16[5,64,512]{2,1,0:T(8,128)(2,1)S(1)} %get-tuple-element.58, bf16[5,16,512]{2,1,0:T(8,128)(2,1)S(1)} %collective-permute-done, ...), kind=kOutput, calls=%fused_computation.33 | convolution fusion | flops 1609439232 | bytes 1505280 | tf_op jit(solution)/shard_map/krb,bj->krj/dot_general | solution.py:49
  132.9 0.8 convolution_bitcast_fusion
  133.8 0.8 fusion.34
  (5 shorter events, 0.0 us)
Async XLA Ops:
  1.3 11.7 %all-to-all-start.4 = ((s32[8,1,256]{2,1,0:T(1,128)}), s32[8,1,256]{2,1,0:T(1,128)S(1)}, u32[]{:S(2)}, u32[]{:S(2)}) async-start(s32[8,1,256]{2,1,0:T(1,128)} %broadcast_in_dim.23), calls=%async_computation.4 | async-start | bytes 16384 | tf_op jit(solution)/shard_map/all_to_all | solution.py:599
  32.0 52.6 %all-to-all-start = ((bf16[8,17,64,128]{3,2,1,0:T(8,128)(2,1)}), bf16[8,17,64,128]{3,2,1,0:T(8,128)(2,1)S(1)}, u32[]{:S(2)}, u32[]{:S(2)}) async-start(bf16[8,17,64,128]{3,2,1,0:T(8,128)(2,1)} %bitcast.79), calls=%async_computation | async-start | bytes 4456448 | tf_op jit(solution)/shard_map/cond/branch_1_fun/all_to_all | solution.py:501
  84.6 1.4 %copy-start = (bf16[8,17,64,128]{3,2,1,0:T(8,128)(2,1)}, bf16[8,17,64,128]{3,2,1,0:T(8,128)(2,1)S(1)}, u32[]{:S(2)}) copy-start(bf16[8,17,64,128]{3,2,1,0:T(8,128)(2,1)S(1)} %all-to-all-done) | copy-start | bytes 6684676 | tf_op jit(solution)/shard_map/cond
  91.8 18.5 %all-to-all-start.1 = ((bf16[8,5,48,128]{3,2,1,0:T(8,128)(2,1)}), bf16[8,5,48,128]{3,2,1,0:T(8,128)(2,1)S(1)}, u32[]{:S(2)}, u32[]{:S(2)}) async-start(bf16[8,5,48,128]{3,2,1,0:T(8,128)(2,1)} %merge.1), calls=%async_computation.1 | async-start | bytes 983040 | tf_op jit(solution)/shard_map/cond/branch_1_fun/all_to_all | solution.py:530
  110.3 0.8 copy-start.1
  112.6 7.5 %collective-permute-start = (bf16[5,16,512]{2,1,0:T(8,128)(2,1)S(1)}, bf16[5,16,512]{2,1,0:T(8,128)(2,1)S(1)}, u32[]{:S(2)}, u32[]{:S(2)}) collective-permute-start(bf16[5,16,512]{2,1,0:T(8,128)(2,1)S(1)} %get-tuple-element.56), channel_id=1, source_target_pairs={{0,8},{8,16},{16,24},{1,9},{9,17},{17,25},{2,10},{10,18},{18,26},{... | collective-permute-start | bytes 245768 | tf_op jit(solution)/shard_map/ppermute | solution.py:29
  118.1 5.8 %collective-permute-start.1 = (bf16[5,16,512]{2,1,0:T(8,128)(2,1)S(1)}, bf16[5,16,512]{2,1,0:T(8,128)(2,1)S(1)}, u32[]{:S(2)}, u32[]{:S(2)}) collective-permute-start(bf16[5,16,512]{2,1,0:T(8,128)(2,1)S(1)} %get-tuple-element.57), channel_id=1, source_target_pairs={{8,0},{16,8},{24,16},{9,1},{17,9},{25,17},{10,2},{18,10},{26,18},{... | collective-permute-start | bytes 245768 | tf_op jit(solution)/shard_map/ppermute | solution.py:30
  124.0 6.6 %collective-permute-start.2 = (bf16[5,96,16]{2,1,0:T(8,128)(2,1)S(1)}, bf16[5,96,16]{2,1,0:T(8,128)(2,1)S(1)}, u32[]{:S(2)}, u32[]{:S(2)}) collective-permute-start(bf16[5,96,16]{2,1,0:T(8,128)(2,1)S(1)} %get-tuple-element.54), channel_id=1, source_target_pairs={{0,1},{1,2},{2,3},{3,4},{4,5},{5,6},{6,7},{7,0},{8,9},{9,10},{10,1... | collective-permute-start | bytes 46088 | tf_op jit(solution)/shard_map/ppermute | solution.py:29
  125.2 5.8 %collective-permute-start.3 = (bf16[5,96,16]{2,1,0:T(8,128)(2,1)S(1)}, bf16[5,96,16]{2,1,0:T(8,128)(2,1)S(1)}, u32[]{:S(2)}, u32[]{:S(2)}) collective-permute-start(bf16[5,96,16]{2,1,0:T(8,128)(2,1)S(1)} %get-tuple-element.55), channel_id=1, source_target_pairs={{1,0},{2,1},{3,2},{4,3},{5,4},{6,5},{7,6},{0,7},{9,8},{10,9},{11,1... | collective-permute-start | bytes 46088 | tf_op jit(solution)/shard_map/ppermute | solution.py:30

commit v3 on v2

--- a/solution.py
+++ b/solution.py
@@ -86,17 +86,37 @@
     return jnp.sum(dot(table, low, exact=True) * high, axis=0, keepdims=True)
 
 
+def prefixes(height, tile_rows):
+    ahead = (iota((LANES, LANES), 0) < iota((LANES, LANES), 1)).astype(BF16)
+    ones = jnp.ones((LANES, LANES), BF16)
+    ahead_total = jnp.concatenate([ahead, ones], axis=1)
+    up, down = iota((height, height), 1), iota((height, height), 0)
+    rows_ahead = (up < down).astype(BF16)
+    same_tile = ((up < down) & (up // tile_rows == down // tile_rows)).astype(BF16)
+
+    def prefix(mask, rows):
+        both = dot(mask.astype(BF16), ahead_total)
+        return both[:, :LANES] + dot(rows, both[:, LANES:].astype(BF16))
+
+    return prefix, rows_ahead, same_tile
+
+
+def as_float(d):
+    return float(d) if isinstance(d, int) else lax.convert_element_type(d, F32)
+
+
 def plan_kernel(
-    count, blocks, cap, mcap, me_ref, keys_ref, src_ref, table_ref, entry_ref, spot_ref, pres, tall
+    count, blocks, cap, extra, mcap, me_ref, keys_ref, src_ref, table_ref, owner_ref, pres, tall
 ):
     me = me_ref[0]
-    pairs = keys_ref.shape[1]
+    pairs = keys_ref.shape[2]
     height = count * blocks // LANES
     tile_rows = blocks // LANES
-    sends = count * cap
+    half = count // 2
+    sends = count * cap + (half - 1) * extra
 
     def held(d, carry):
-        high, low = one_hots(keys_ref[pl.ds(d, 1), :], height)
+        high, low = one_hots(keys_ref[d], height)
         found = dot(high.astype(BF16), low.astype(BF16), ((1,), (1,)))
         found = (found > 0.5).astype(F32)
         pres[d] = found
@@ -105,19 +125,22 @@
 
     repeat(count, held, 0)
 
-    row_at = iota((height, LANES), 0)
     zero = jnp.zeros((height, LANES), F32)
     holders = repeat(count, lambda d, total: total + pres[d], zero)
     device = iota((count, LANES), 0)
     turn = (device + count - iota((count, LANES), 1) % count) % count
     turn = turn.astype(F32)
     others = [(device != s).astype(F32) for s in range(count)]
-
+    near = [(device // half == s // half).astype(F32) for s in range(count)]
+    weight = [1.0 - 0.8 * near[s] for s in range(count)]
     part = iota((count, LANES), 1) * 2 // LANES
-    halves = [(part == h).astype(F32) for h in range(2)]
+    sides = [(part == h).astype(F32) for h in range(2)]
+
+    def rows_of(r):
+        return pl.ds(pl.multiple_of(r * count, count), count)
 
     def expect(r, sums):
-        here = tall[pl.ds(pl.multiple_of(r * count, count), count), :]
+        here = tall[rows_of(r), :]
         even = here / jnp.maximum(jnp.sum(here, axis=0, keepdims=True), 1.0)
         return tuple(sums[s] + even * here[s : s + 1, :] for s in range(count))
 
@@ -129,51 +152,51 @@
     )
 
     def settle(r, loads):
-        rows = pl.ds(pl.multiple_of(r * count, count), count)
-        here = tall[rows, :]
+        here = tall[rows_of(r), :]
         even = here / jnp.maximum(jnp.sum(here, axis=0, keepdims=True), 1.0)
         picks = jnp.zeros((count, LANES), F32)
-        for half in halves:
+        for side in sides:
             cost = jnp.zeros((count, LANES), F32)
             for s in range(count):
                 growth = loads[s] * loads[s]
-                cost = cost + growth * growth * here[s : s + 1, :]
+                cost = cost + weight[s] * growth * growth * here[s : s + 1, :]
             cost = jnp.where(here > 0.5, cost, 1e30)
             best = jnp.min(cost, axis=0, keepdims=True)
             place_in_turn = jnp.where(cost == best, turn, 1e30)
             nearest = jnp.min(place_in_turn, axis=0, keepdims=True)
-            pick = jnp.where(place_in_turn == nearest, here, 0.0) * half
+            pick = jnp.where(place_in_turn == nearest, here, 0.0) * side
             picks = picks + pick
-            change = pick - even * half
+            change = pick - even * side
             loads = tuple(
                 loads[s] + others[s] * jnp.sum(change * here[s : s + 1, :], axis=1, keepdims=True)
                 for s in range(count)
             )
-        tall[rows, :] = picks
+        tall[rows_of(r), :] = picks
         return loads
 
     loads = lax.fori_loop(0, height, settle, loads)
-    worst = loads[0]
+    far_most, near_most = loads[0] * (1.0 - near[0]), loads[0] * near[0]
     for s in range(1, count):
-        worst = jnp.maximum(worst, loads[s])
-    worst = jnp.max(jnp.max(worst, axis=1, keepdims=True), axis=0, keepdims=True)
+        far_most = jnp.maximum(far_most, loads[s] * (1.0 - near[s]))
+        near_most = jnp.maximum(near_most, loads[s] * near[s])
+
+    def tile_most(o, most):
+        sums = tall[rows_of(o * tile_rows), :]
+        for i in range(1, tile_rows):
+            sums = sums + tall[rows_of(o * tile_rows + i), :]
+        return jnp.maximum(most, jnp.sum(sums, axis=1, keepdims=True))
+
+    most = repeat(count, tile_most, jnp.zeros((count, 1), F32))
+    fits = (far_most < cap + 0.25) & (near_most < cap + extra + 0.25) & (most < mcap + 0.5)
+    fits = jnp.min(jnp.min(fits.astype(F32), axis=1, keepdims=True), axis=0, keepdims=True)
+    over = 1 - fits.astype(I32)
 
     def own(d, owner):
         return jnp.where(tall[pl.ds(d, height, stride=count), :] > 0.5, d, owner)
 
     owner = repeat(count, own, jnp.full((height, LANES), -1, I32))
-
-    ahead = (iota((LANES, LANES), 0) < iota((LANES, LANES), 1)).astype(BF16)
-    ones = jnp.ones((LANES, LANES), BF16)
-    ahead_total = jnp.concatenate([ahead, ones], axis=1)
-    up, down = iota((height, height), 1), iota((height, height), 0)
-    rows_ahead = (up < down).astype(BF16)
-    same_tile = ((up < down) & (up // tile_rows == down // tile_rows)).astype(BF16)
-
-    def prefix(mask, rows):
-        both = dot(mask.astype(BF16), ahead_total)
-        return both[:, :LANES] + dot(rows, both[:, LANES:].astype(BF16))
-
+    owner_ref[...] = owner
+    prefix, rows_ahead, _ = prefixes(height, tile_rows)
     mine = (owner == me).astype(F32)
     several = mine * (holders > 1.5).astype(F32)
     single = mine - several
@@ -182,63 +205,22 @@
     total_several = jnp.sum(several, axis=(0, 1), keepdims=True)
     total_mine = jnp.sum(mine, axis=(0, 1), keepdims=True)
     held_here = pres[me]
-    entry_rows = entry_ref.shape[0] - 8
-    lane_at = iota((entry_rows, LANES), 1)
-    first_lane = iota((8, LANES), 1)
-
-    def route(d, carry):
-        place, finished, most, entries, counts = carry
+
+    def route(d, place):
         away = jnp.where(d == me, 0.0, 1.0)
-        theirs = (owner == d).astype(F32)
-        rank_theirs = prefix(theirs, same_tile)
-        base = lax.convert_element_type(d, F32) if not isinstance(d, int) else float(d)
-        finished = finished + theirs * (base * mcap + rank_theirs + 1.0)
-        most = jnp.maximum(most, theirs * (rank_theirs + 1.0))
-        leaving = held_here * theirs * away
-        rank_leaving = prefix(leaving, rows_ahead)
-        place = place + leaving * (base * cap + rank_leaving + 1.0)
-        coming = pres[d] * mine * away
-        rank_coming = prefix(coming, rows_ahead)
-        code = coming * (rank_coming * 1024.0 + rank_several + 1.0)
-        high, low = one_hots(keys_ref[pl.ds(d, 1), :], height)
-        seen = (look_up(code, high, low) + 0.5).astype(I32) - 1
-        rank, local = seen >> 10, seen & 1023
-        hit = iota((entry_rows, pairs), 0) == rank
-        column = jnp.max(jnp.where(hit, local, -1), axis=1, keepdims=True)
-        entries = jnp.where(lane_at == d, column, entries)
-        arrivals = jnp.sum(coming, axis=(0, 1), keepdims=True).astype(I32)
-        counts = jnp.where(first_lane == d, arrivals, counts)
-        return place, finished, most, entries, counts
-
-    place, finished, most, entries, counts = repeat(
-        count,
-        route,
-        (
-            zero,
-            zero,
-            zero,
-            jnp.full((entry_rows, LANES), -1, I32),
-            jnp.zeros((8, LANES), I32),
-        ),
-    )
-    entry_ref[:entry_rows, :] = entries
-    entry_ref[entry_rows:, :] = counts
-
-    pick = (iota((8, height), 1) == me * tile_rows + iota((8, height), 0)).astype(F32)
-    spot_ref[...] = (dot(pick, finished, exact=True) + 0.5).astype(I32) - 1
-
-    most = jnp.max(jnp.max(most, axis=1, keepdims=True), axis=0, keepdims=True)
-    over = jnp.where((worst > cap + 0.25) | (most > mcap + 0.5), 1, 0)
-
+        leaving = held_here * (owner == d).astype(F32) * away
+        rank = prefix(leaving, rows_ahead)
+        first = as_float(d) * cap + rank
+        steps = ((d % half + half - me % half) % half).astype(F32)
+        second = count * cap + (steps - 1.0) * extra + rank - cap
+        return place + leaving * (jnp.where(rank < cap - 0.5, first, second) + 1.0)
+
+    place = repeat(count, route, zero)
     place = place + several * (sends + rank_several + 1.0)
     place = place + single * (sends + total_several + rank_single + 1.0)
-    tile_of = (row_at // tile_rows).astype(F32)
-    moment_place = mine * (tile_of * mcap + finished - 1.0 - me.astype(F32) * mcap)
-    high, low = one_hots(keys_ref[pl.ds(me, 1), :], height)
+    high, low = one_hots(keys_ref[me], height)
     goes = look_up(place, high, low) - 1.0
-    lands = look_up(moment_place, high, low)
-    leaves = (goes < sends - 0.5).astype(F32)
-    leaving = jnp.sum(leaves, axis=1, keepdims=True)
+    leaving = jnp.sum((goes < sends - 0.5).astype(F32), axis=1, keepdims=True)
     first_at, second_at = iota((pairs, pairs), 0), iota((pairs, pairs), 1)
     same = (first_at == second_at).astype(F32)
     upright = dot(same, jnp.broadcast_to(goes, (8, pairs)), ((1,), (1,)), exact=True)[:, 0:1]
@@ -251,49 +233,110 @@
         at,
         jnp.where(kind == 1, goes, jnp.where(kind == 2, src_ref[...].astype(F32), 0.0)),
     )
-    column_at = first_at
-    order = (column_at == (position + 0.5).astype(I32)).astype(F32)
-    ordered = dot(values, order, ((1,), (1,)), exact=True)
-    slot = jnp.where(leaves > 0.5, -1, (goes - sends + 0.5).astype(I32))
-    in_slot = (column_at == slot).astype(F32)
-    weighed = jnp.where(kind == 0, lands, 1.0)
+    order = (first_at == (position + 0.5).astype(I32)).astype(F32)
+    result = (dot(values, order, ((1,), (1,)), exact=True) + 0.5).astype(I32)
+    lane = iota((8, pairs), 1)
+    facts = jnp.where(lane == 0, leaving.astype(I32), over)
+    facts = jnp.where(lane == 1, total_mine.astype(I32), facts)
+    facts = jnp.where(lane == 2, total_several.astype(I32), facts)
+    facts = jnp.where(lane == 4, me, facts)
+    result = jnp.where(kind == 4, facts, result)
+    table_ref[...] = jnp.where(kind == 5, (goes + 0.5).astype(I32), result)
+
+
+def finish_kernel(
+    count, blocks, sends, mcap, me_ref, keys_ref, owner_ref, pres, table_ref, entry_ref, spot_ref, landing_ref
+):
+    me = me_ref[0]
+    pairs = keys_ref.shape[2]
+    height = count * blocks // LANES
+    tile_rows = blocks // LANES
+    prefix, rows_ahead, same_tile = prefixes(height, tile_rows)
+    owner = owner_ref[...]
+    zero = jnp.zeros((height, LANES), F32)
+    holders = repeat(count, lambda d, total: total + pres[d], zero)
+    mine = (owner == me).astype(F32)
+    rank_several = prefix(mine * (holders > 1.5).astype(F32), rows_ahead)
+    entry_rows = entry_ref.shape[0] - 8
+    lane_at = iota((entry_rows, LANES), 1)
+    first_lane = iota((8, LANES), 1)
+
+    def route(d, carry):
+        finished, entries, counts = carry
+        away = jnp.where(d == me, 0.0, 1.0)
+        theirs = (owner == d).astype(F32)
+        rank_theirs = prefix(theirs, same_tile)
+        finished = finished + theirs * (as_float(d) * mcap + rank_theirs + 1.0)
+        coming = pres[d] * mine * away
+        rank_coming = prefix(coming, rows_ahead)
+        code = coming * (rank_coming * 1024.0 + rank_several + 1.0)
+        high, low = one_hots(keys_ref[d], height)
+        seen = (look_up(code, high, low) + 0.5).astype(I32) - 1
+        rank, local = seen >> 10, seen & 1023
+        hit = iota((entry_rows, pairs), 0) == rank
+        column = jnp.max(jnp.where(hit, local, -1), axis=1, keepdims=True)
+        entries = jnp.where(lane_at == d, column, entries)
+        arrivals = jnp.sum(coming, axis=(0, 1), keepdims=True).astype(I32)
+        counts = jnp.where(first_lane == d, arrivals, counts)
+        return finished, entries, counts
+
+    finished, entries, counts = repeat(
+        count,
+        route,
+        (zero, jnp.full((entry_rows, LANES), -1, I32), jnp.zeros((8, LANES), I32)),
+    )
+    entry_ref[:entry_rows, :] = entries
+    entry_ref[entry_rows:, :] = counts
+    pick = (iota((8, height), 1) == me * tile_rows + iota((8, height), 0)).astype(F32)
+    spot_ref[...] = (dot(pick, finished, exact=True) + 0.5).astype(I32) - 1
+    tile_of = (iota((height, LANES), 0) // tile_rows).astype(F32)
+    moment_place = mine * (tile_of * mcap + finished - 1.0 - me.astype(F32) * mcap)
+    high, low = one_hots(keys_ref[me], height)
+    lands = look_up(moment_place, high, low)
+    goes = table_ref[5:6, :]
+    slot = jnp.where(goes < sends, -1, goes - sends)
+    in_slot = (iota((pairs, pairs), 0) == slot).astype(F32)
+    weighed = jnp.where(iota((8, pairs), 0) == 0, lands, 1.0)
     summed = dot(weighed, in_slot, ((1,), (1,)), exact=True)
     landing = summed[0:1, :] / jnp.maximum(summed[1:2, :], 1.0)
-    result = (ordered + 0.5).astype(I32)
-    result = jnp.where(kind == 3, (landing + 0.25).astype(I32), result)
-    lane = iota((8, pairs), 1)
-    facts = jnp.where(
-        lane == 0,
-        leaving.astype(I32),
-        jnp.where(
-            lane == 1,
-            total_mine.astype(I32),
-            jnp.where(lane == 2, total_several.astype(I32), over),
-        ),
-    )
-    table_ref[...] = jnp.where(kind == 4, facts, result)
-
-
-def make_plan(keys, pair_source, count, blocks, cap, mcap):
-    pairs = keys.shape[1]
+    landing_ref[...] = jnp.broadcast_to((landing + 0.25).astype(I32), landing_ref.shape)
+
+
+def make_plan(me, keys, pair_source, count, blocks, cap, extra, mcap):
+    pairs = keys.shape[2]
     height = count * blocks // LANES
-    entry_rows = -(-cap // 8) * 8 + 8
     vmem = pl.BlockSpec(memory_space=pltpu.VMEM)
     return pl.pallas_call(
-        functools.partial(plan_kernel, count, blocks, cap, mcap),
+        functools.partial(plan_kernel, count, blocks, cap, extra, mcap),
         out_shape=(
             jax.ShapeDtypeStruct((8, pairs), I32),
-            jax.ShapeDtypeStruct((entry_rows, LANES), I32),
-            jax.ShapeDtypeStruct((8, LANES), I32),
+            jax.ShapeDtypeStruct((height, LANES), I32),
+            jax.ShapeDtypeStruct((count, height, LANES), F32),
         ),
         in_specs=[pl.BlockSpec(memory_space=pltpu.SMEM), vmem, vmem],
         out_specs=(vmem, vmem, vmem),
-        scratch_shapes=[
-            pltpu.VMEM((count, height, LANES), F32),
-            pltpu.VMEM((height * count, LANES), F32),
-        ],
+        scratch_shapes=[pltpu.VMEM((height * count, LANES), F32)],
         name="plan",
-    )(lax.axis_index("lon").astype(I32)[None], keys, pair_source[None, :])
+    )(me, keys, pair_source[None, :])
+
+
+def finish_plan(me, keys, owner, pres, table, count, blocks, cap, extra, mcap):
+    pairs = keys.shape[2]
+    entry_rows = -(-(cap + extra) // 8) * 8 + 8
+    sends = count * cap + (count // 2 - 1) * extra
+    vmem = pl.BlockSpec(memory_space=pltpu.VMEM)
+    return pl.pallas_call(
+        functools.partial(finish_kernel, count, blocks, sends, mcap),
+        out_shape=(
+            jax.ShapeDtypeStruct((entry_rows, LANES), I32),
+            jax.ShapeDtypeStruct((8, LANES), I32),
+            jax.ShapeDtypeStruct((8, pairs), I32),
+        ),
+        in_specs=[pl.BlockSpec(memory_space=pltpu.SMEM)] + [vmem] * 4,
+        out_specs=(vmem, vmem, vmem),
+        compiler_params=pltpu.CompilerParams(vmem_limit_bytes=8 << 20),
+        name="finish",
+    )(me, keys, owner, pres, table)
 
 
 def pair_copies(table, src, weights, xs, ws, x_sem, w_sem, i):
@@ -350,13 +393,21 @@
     lax.fori_loop(low // GROUP, high // GROUP, step, 0)
 
 
-def send_kernel(sends, table, src, weights, out_ref, total, packed, xs, ws, x_sem, w_sem, out_sem):
+def send_kernel(first, extra, parts, table, src, weights, *refs):
+    far_ref, near_refs = refs[0], refs[1 : 1 + parts]
+    total, packed, xs, ws, x_sem, w_sem, out_sem = refs[1 + parts :]
+    sends = packed.shape[0] - 1
     leaving = table[4, 0]
     high = (leaving + GROUP - 1) // GROUP * GROUP
     products(table, src, weights, xs, ws, x_sem, w_sem, 0, high, total, packed, 0, sends, sends)
-    out = pltpu.make_async_copy(packed.at[pl.ds(0, sends)], out_ref, out_sem)
-    out.start()
-    out.wait()
+    outs = [pltpu.make_async_copy(packed.at[pl.ds(0, first)], far_ref, out_sem.at[0])]
+    for j in range(parts):
+        rows = pl.ds(first + j * extra, extra)
+        outs.append(pltpu.make_async_copy(packed.at[rows], near_refs[j], out_sem.at[1 + j]))
+    for out in outs:
+        out.start()
+    for out in outs:
+        out.wait()
 
 
 def moment_rows(value):
@@ -368,13 +419,13 @@
     ]
 
 
-def put_moments(table, total, moments, spare, begin, end):
+def put_moments(landing, total, moments, spare, begin, end):
     def some(g, carry):
         for u in range(4):
             i = begin + g * 4 + u
             good = i < end
             at = jnp.where(good, i, 0)
-            place = jnp.where(good, table[3, at], spare)
+            place = jnp.where(good, landing[0, at], spare)
             for k, row in enumerate(moment_rows(total[at])):
                 moments[k, pl.ds(place, 1), :] = row
         return carry
@@ -388,7 +439,7 @@
 
 
 def local_kernel(
-    sends, table, src, weights, local_ref, moments, total, xs, ws, x_sem, w_sem, out_sem
+    sends, table, landing, src, weights, local_ref, moments, total, xs, ws, x_sem, w_sem, out_sem
 ):
     pairs = weights.shape[0]
     leaving, owned, several = table[4, 0], table[4, 1], table[4, 2]
@@ -405,7 +456,7 @@
         return carry
 
     lax.fori_loop(0, chunks, begin, 0)
-    put_moments(table, total, moments, moments.shape[1] - 8, several, owned)
+    put_moments(landing, total, moments, moments.shape[1] - 8, several, owned)
 
     def end(c, carry):
         chunk_copies(total, local_ref, out_sem, c).wait()
@@ -414,10 +465,12 @@
     lax.fori_loop(0, chunks, end, 0)
 
 
-def merge_kernel(
-    count, cap, mcap, table, entry, local_ref, came, moments_in, out_ref, total, moments, in_sem
-):
-    several = table[4, 2]
+def merge_kernel(count, cap, extra, mcap, table, landing, entry, local_ref, moments_in, far_ref, *refs):
+    parts = count // 2 - 1
+    near_refs = refs[:parts]
+    out_ref, total, near, moments, in_sem, near_sem, moment_sem = refs[parts:]
+    several, me = table[4, 2], table[4, 4]
+    half = count // 2
     spare = total.shape[0] - 1
     counts_row = entry.shape[0] - 8
     chunks = (several + CHUNK - 1) // CHUNK
@@ -426,8 +479,15 @@
         chunk_copies(local_ref, total, in_sem, c).start()
         return carry
 
+    near_copies = [
+        pltpu.make_async_copy(near_refs[j], near.at[pl.ds(j * extra, extra)], near_sem.at[j])
+        for j in range(parts)
+    ]
     lax.fori_loop(0, chunks, begin, 0)
-    moments[...] = moments_in[...]
+    for near_copy in near_copies:
+        near_copy.start()
+    moment_copy = pltpu.make_async_copy(moments_in, moments, moment_sem)
+    moment_copy.start()
 
     def end(c, carry):
         chunk_copies(local_ref, total, in_sem, c).wait()
@@ -435,23 +495,35 @@
 
     lax.fori_loop(0, chunks, end, 0)
 
-    def from_one(s, carry):
-        number = entry[counts_row, s]
-
+    def add(s, low, high, came, shift):
         def some(g, inner):
             for u in range(4):
-                r = g * 4 + u
-                good = r < number
-                at = jnp.where(good, r, 0)
+                r = low + g * 4 + u
+                good = r < high
+                at = jnp.where(good, r, low)
                 where = jnp.where(good, entry[at, s], spare)
-                total[where] = total[where] + came[s * cap + at].astype(F32)
+                total[where] = total[where] + came[shift + at].astype(F32)
             return inner
 
-        lax.fori_loop(0, (number + 3) // 4, some, 0)
-        return carry
-
-    lax.fori_loop(0, count, from_one, 0)
-    put_moments(table, total, moments, moments.shape[1] - 8, 0, several)
+        lax.fori_loop(0, (high - low + 3) // 4, some, 0)
+
+    def from_far(s, carry):
+        add(s, 0, jnp.minimum(entry[counts_row, s], cap), far_ref, s * cap)
+        return carry
+
+    lax.fori_loop(0, count, from_far, 0)
+    for near_copy in near_copies:
+        near_copy.wait()
+
+    def from_near(j, carry):
+        s = me // half * half + (me % half + half - j - 1) % half
+        number = jnp.maximum(entry[counts_row, s], cap)
+        add(s, cap, number, near, j * extra - cap)
+        return carry
+
+    lax.fori_loop(0, parts, from_near, 0)
+    moment_copy.wait()
+    put_moments(landing, total, moments, moments.shape[1] - 8, 0, several)
     for o in range(count):
         for k in range(5):
             out_ref[o, k] = moments[k, o * mcap : (o + 1) * mcap, :].astype(BF16)
@@ -471,11 +543,14 @@
             ].astype(BF16)
 
 
-def direct(cap, mcap, source_fields, weight_blocks, table, entry, spot):
+def direct(cap, extra, mcap, source_fields, weight_blocks, me, keys, table, owner, pres):
     count = lax.axis_size("lon")
+    half = count // 2
     blocks, channels, cells = source_fields.shape
     pairs = weight_blocks.shape[0]
-    sends = count * cap
+    parts = half - 1
+    first = count * cap
+    sends = first + parts * extra
     smem = pl.BlockSpec(memory_space=pltpu.SMEM)
     vmem = pl.BlockSpec(memory_space=pltpu.VMEM)
     hbm = pl.BlockSpec(memory_space=pl.ANY)
@@ -485,22 +560,31 @@
         pltpu.SemaphoreType.DMA((RING,)),
         pltpu.SemaphoreType.DMA((RING,)),
     ]
-    packed = pl.pallas_call(
-        functools.partial(send_kernel, sends),
-        out_shape=jax.ShapeDtypeStruct((sends, channels, cells), BF16),
+    sent = pl.pallas_call(
+        functools.partial(send_kernel, first, extra, parts),
+        out_shape=[jax.ShapeDtypeStruct((first, channels, cells), BF16)]
+        + [jax.ShapeDtypeStruct((extra, channels, cells), BF16)] * parts,
         in_specs=[smem, hbm, hbm],
-        out_specs=hbm,
+        out_specs=[hbm] + [hbm] * parts,
         scratch_shapes=[
             pltpu.VMEM((sends + 1, channels, cells), F32),
             pltpu.VMEM((sends + 1, channels, cells), BF16),
         ]
         + buffers
-        + [pltpu.SemaphoreType.DMA],
+        + [pltpu.SemaphoreType.DMA((1 + parts,))],
         name="leaving",
     )(table, source_fields, weight_blocks)
-    came = lax.all_to_all(
-        packed.reshape(count, cap, channels, cells), "lon", split_axis=0, concat_axis=0, tiled=True
-    ).reshape(sends, channels, cells)
+    sent, owner = lax.optimization_barrier((sent, owner))
+    far = lax.all_to_all(
+        sent[0].reshape(count, cap, channels, cells), "lon", split_axis=0, concat_axis=0, tiled=True
+    ).reshape(first, channels, cells)
+    near = []
+    for j in range(parts):
+        turn = [(i, i // half * half + (i % half + j + 1) % half) for i in range(count)]
+        near.append(lax.ppermute(sent[1 + j], "lon", turn))
+    entry, spot, landing = finish_plan(
+        me, keys, owner, pres, table, count, blocks, cap, extra, mcap
+    )
     chunk_count = -(-pairs // CHUNK)
     local, moments = pl.pallas_call(
         functools.partial(local_kernel, sends),
@@ -508,25 +592,29 @@
             jax.ShapeDtypeStruct((pairs, channels, cells), F32),
             jax.ShapeDtypeStruct((5, count * mcap + 8, cells), F32),
         ),
-        in_specs=[smem, hbm, hbm],
+        in_specs=[smem, smem, hbm, hbm],
         out_specs=(hbm, vmem),
         scratch_shapes=[pltpu.VMEM((pairs + 1, channels, cells), F32)]
         + buffers
         + [pltpu.SemaphoreType.DMA((chunk_count,))],
         name="staying",
-    )(table, source_fields, weight_blocks)
+    )(table, landing, source_fields, weight_blocks)
     finished = pl.pallas_call(
-        functools.partial(merge_kernel, count, cap, mcap),
+        functools.partial(merge_kernel, count, cap, extra, mcap),
         out_shape=jax.ShapeDtypeStruct((count, 5, mcap, cells), BF16),
-        in_specs=[smem, smem, hbm, vmem, vmem],
+        in_specs=[smem, smem, smem, hbm, hbm, vmem] + [hbm] * parts,
         out_specs=vmem,
         scratch_shapes=[
             pltpu.VMEM((pairs + 1, channels, cells), F32),
+            pltpu.VMEM((parts * extra, channels, cells), BF16),
             pltpu.VMEM((5, count * mcap + 8, cells), F32),
             pltpu.SemaphoreType.DMA((chunk_count,)),
+            pltpu.SemaphoreType.DMA((parts,)),
+            pltpu.SemaphoreType.DMA,
         ],
+        compiler_params=pltpu.CompilerParams(vmem_limit_bytes=50 << 20),
         name="merge",
-    )(table, entry, local, came, moments)
+    )(table, landing, entry, local, moments, far, *near)
     arrived = lax.all_to_all(finished, "lon", split_axis=0, concat_axis=0, tiled=True)
     wide = LON_DEV // cells
     where = spot.reshape(-1)[:blocks].reshape(LAT_DEV, wide).T.reshape(blocks, 1)
@@ -536,6 +624,7 @@
         in_specs=[vmem, vmem],
         out_specs=vmem,
         scratch_shapes=[pltpu.VMEM((count * mcap, 5 * cells), BF16)],
+        compiler_params=pltpu.CompilerParams(vmem_limit_bytes=8 << 20),
         name="spread",
     )(where, arrived)
 
@@ -592,17 +681,21 @@
     days = channels // 2
     pairs = pair_source.shape[0]
     share = -(-pairs // count)
-    cap = max(share * 17 // 32, min(share, 8))
+    cap = max(share * 7 // 16, min(share, 8))
+    extra = max(share * 3 // 16, 1)
     mcap = -(-share * 3 // 2 // 16) * 16
     targets = pair_target[:, 0]
-    keys = targets * blocks + pair_block
+    keys = pair_target.reshape(1, 1, pairs) * blocks + pair_block[None, None, :]
     all_keys = lax.all_to_all(
-        jnp.broadcast_to(keys[None, :], (count, pairs)), "lon", split_axis=0, concat_axis=0, tiled=True
-    )
-    table, entry, spot = make_plan(all_keys, pair_source, count, blocks, cap, mcap)
+        jnp.broadcast_to(keys, (count, 1, pairs)), "lon", split_axis=0, concat_axis=0, tiled=True
+    )
+    me = lax.axis_index("lon").astype(I32)[None]
+    table, owner, pres = make_plan(me, all_keys, pair_source, count, blocks, cap, extra, mcap)
     moments = lax.cond(
         table[4, 3] == 0,
-        lambda: direct(cap, mcap, source_fields, weight_blocks, table, entry, spot),
+        lambda: direct(
+            cap, extra, mcap, source_fields, weight_blocks, me, all_keys, table, owner, pres
+        ),
         lambda: padded_exchange(source_fields, weight_blocks, pair_source, targets, pair_block),
     )
     lon_band = band_matrix(LON_DEV)

time: 135 us -> 122 us (0.904)
  waiting for transfers between devices: 57.8 us -> 42.3 us
  starting transfers between devices: 27.3 us -> 31.4 us
  local copies, waits for them, and re-layouts: 4.98 us -> 3.34 us
    all_to_all x2, waiting for transfers between devices: 39.4 us -> 12.3 us  [the longest x1 8.39 us: direct(): lax.all_to_all(sent[0].reshape(count, cap, channels, cells), 'lon', split...]
    ppermute x0 -> x3, waiting for transfers between devices: none -> 10.8 us  [direct(): near.append(lax.ppermute(sent[1 + j], 'lon', turn))]
    ppermute x0 -> x3, starting transfers between devices: none -> 3.73 us  [direct(): near.append(lax.ppermute(sent[1 + j], 'lon', turn))]
    pallas_call x3 -> x4, Pallas kernels: 22.6 us -> 23.2 us  [the longest x1 7.96 us: direct(): pl.pallas_call(functools.partial(send_kernel, first, extra, parts), out_s...]
  transfers between devices with their start and end apart: 7 -> 10, of which waited for: 6 -> 9; matrix products, arithmetic and copies ran while one was open for 1% -> 1% of each run, Pallas kernels for 10% -> 14%
where the time goes in v3:
time: 122 us
  waiting for transfers between devices  42.3 us (35%)
  Pallas kernels  37.8 us (31%)
  starting transfers between devices  31.4 us (26%)
  local copies, waits for them, and re-layouts  3.34 us (3%)
  matrix products  2.7 us (2%)
  other arithmetic  2.41 us (2%)
  between operations  1.42 us (1%)
    pallas_call x1, Pallas kernels, direct(): pl.pallas_call(functools.partial(local_kernel, sends), out_shape=(jax.Sha...  14.1 us
    all_to_all x1, waiting for transfers between devices, direct(): lax.all_to_all(finished, 'lon', split_axis=0, concat_axis=0, tiled=True)  12.6 us
    ppermute x3, waiting for transfers between devices, direct(): near.append(lax.ppermute(sent[1 + j], 'lon', turn))  10.8 us
    all_to_all x1, waiting for transfers between devices, direct(): lax.all_to_all(sent[0].reshape(count, cap, channels, cells), 'lon', split...  8.39 us
    pallas_call x1, Pallas kernels, direct(): pl.pallas_call(functools.partial(send_kernel, first, extra, parts), out_s...  7.96 us
    pallas_call x1, Pallas kernels, make_plan(): pl.pallas_call(functools.partial(plan_kernel, count, blocks, cap, extra,...  7.62 us
    all_to_all x1, starting transfers between devices, direct(): lax.all_to_all(finished, 'lon', split_axis=0, concat_axis=0, tiled=True)  6.77 us
    all_to_all x1, starting transfers between devices, local(): lax.all_to_all(jnp.broadcast_to(keys, (count, 1, pairs)), 'lon', split_ax...  6.34 us
  transfers between devices with their start and end apart: 10, of which 9 were waited for; matrix products, arithmetic and copies ran while one was open for 1% of the time, Pallas kernels for 14%

profile of v3, /device:TPU:1, one launch (start us, length us, event | category | flops | bytes accessed | tf_op | source)
XLA Modules:
  0.0 121.7 jit_solution(13653104664553522909)
XLA Ops:
  0.0 0.7 multiply_add_fusion
  0.7 0.6 broadcast_in_dim.23
  1.3 6.3 %all-to-all-start.4 = ((s32[8,1,256]{2,1,0:T(1,128)}), s32[8,1,256]{2,1,0:T(1,128)S(1)}, u32[]{:S(2)}, u32[]{:S(2)}) async-start(s32[8,1,256]{2,1,0:T(1,128)} %broadcast_in_dim.23), calls=%async_computation.4 | async-start | bytes 16384 | tf_op jit(solution)/shard_map/all_to_all | solution.py:689
  7.7 0.7 fusion.60
  9.1 4.0 %all-to-all-done.4.keys_ref = s32[8,1,256]{2,1,0:T(1,128)S(1)} async-done(((s32[8,1,256]{2,1,0:T(1,128)}), s32[8,1,256]{2,1,0:T(1,128)S(1)}, u32[]{:S(2)}, u32[]{:S(2)}) %all-to-all-start.4) | async-done | bytes 8224 | tf_op jit(solution)/shard_map/all_to_all | solution.py:689
  13.0 7.6 %plan.1 = (s32[8,256]{1,0:T(8,128)S(1)}, s32[16,128]{1,0:T(8,128)S(1)}, f32[8,16,128]{2,1,0:T(8,128)S(1)}) custom-call(s32[1]{0:T(128)} %bitcast.9.me_ref, s32[8,1,256]{2,1,0:T(1,128)S(1)} %all-to-all-done.4.keys_ref, s32[1,256]{1,0:T(1,128)} %bitcast.83), custom_call_target="tpu_custom_call" | custom-call | tf_op jit(solution)/shard_map/plan/pallas_call | solution.py:309
  20.6 0.6 slice.46
  21.9 78.5 %conditional.1 = (bf16[5,64,512]{2,1,0:T(8,128)(2,1)S(1)}) conditional(s32[]{:T(128)} %bitcast.12, (s32[256]{0:T(256)}, s32[256,1]{0,1:T(1,128)}, s32[256]{0:T(256)}, s32[256]{0:T(256)}, bf16[256,64,128]{2,1,0:T(8,128)(2,1)}, /*index=5*/bf16[256,128,128]{2,1,0:T(8,128)(2,1)}) %tuple.22, (s32[8,256]{1,0:T(8,128)S(1)}, ...), branch_computations={%region_0.12_spmd, %region_12.13_spmd} | conditional | flops 557957888 | bytes 215623744 | solution.py:694
  22.1 8.0 %leaving.1 = (bf16[112,64,128]{2,1,0:T(8,128)(2,1)}, bf16[6,64,128]{2,1,0:T(8,128)(2,1)}, bf16[6,64,128]{2,1,0:T(8,128)(2,1)}, bf16[6,64,128]{2,1,0:T(8,128)(2,1)}) custom-call(s32[8,256]{1,0:T(8,128)S(1)} %get-tuple-element.42.table.table_ref, bf16[256,64,128]{2,1,0:T(8,128)(2,1)} %get-tuple-element.43.src, bf16[256,128,128]{2,1,0:T(8,128)(2,1)} %get-tuple-element.44.weights), custom_call_target="tpu_custom_call" | custom-call | tf_op jit(solution)/shard_map/cond/branch_1_fun/leaving/pallas_call | solution.py:563
  30.1 3.6 %all-to-all-start = ((bf16[8,14,64,128]{3,2,1,0:T(8,128)(2,1)}), bf16[8,14,64,128]{3,2,1,0:T(8,128)(2,1)S(1)}, u32[]{:S(2)}, u32[]{:S(2)}) async-start(bf16[8,14,64,128]{3,2,1,0:T(8,128)(2,1)} %bitcast.76), calls=%async_computation | async-start | bytes 3670016 | tf_op jit(solution)/shard_map/cond/branch_1_fun/all_to_all | solution.py:578
  33.7 1.4 %collective-permute-start = (bf16[6,64,128]{2,1,0:T(8,128)(2,1)}, bf16[6,64,128]{2,1,0:T(8,128)(2,1)S(1)}, u32[]{:S(2)}, u32[]{:S(2)}) collective-permute-start(bf16[6,64,128]{2,1,0:T(8,128)(2,1)} %get-tuple-element.58), channel_id=1, source_target_pairs={{0,1},{1,2},{2,3},{3,0},{4,5},{5,6},{6,7},{7,4},{8,9},{9,10},{10,1... | collective-permute-start | bytes 294920 | tf_op jit(solution)/shard_map/cond/branch_1_fun/ppermute | solution.py:584
  35.1 1.2 collective-permute-start.1
  36.3 1.2 collective-permute-start.2
  37.4 2.6 %finish.1 = (s32[32,128]{1,0:T(8,128)S(1)}, s32[8,128]{1,0:T(8,128)S(1)}, s32[8,256]{1,0:T(8,128)S(1)}) custom-call(s32[1]{0:T(128)} %get-tuple-element.40.me_ref, s32[8,1,256]{2,1,0:T(1,128)S(1)} %get-tuple-element.41.keys_ref, s32[16,128]{1,0:T(8,128)S(1)} %get-tuple-element.50.owner_ref, f32[8,16,128]{2,1,0:T(8,128)S(1)} %get-tuple-element.51.pres, ...), custom_call_target="tpu_custom_call" | custom-call | tf_op jit(solution)/shard_map/cond/branch_1_fun/finish/pallas_call | solution.py:328
  40.0 0.0 copy-start.1
  40.0 0.6 copy-done.1
  40.6 0.0 copy-start.2
  40.6 14.1 %staying.1 = (f32[256,64,128]{2,1,0:T(8,128)}, f32[5,392,128]{2,1,0:T(8,128)}) custom-call(s32[8,256]{1,0:T(8,128)S(1)} %get-tuple-element.42.table.table_ref, s32[8,256]{1,0:T(8,128)} %copy-done.1, bf16[256,64,128]{2,1,0:T(8,128)(2,1)} %get-tuple-element.43.src, bf16[256,128,128]{2,1,0:T(8,128)(2,1)} %get-tuple-element.44.weights), custom_call_target="tpu_custom_call" | custom-call | tf_op jit(solution)/shard_map/cond/branch_1_fun/staying/pallas_call | solution.py:589
  54.7 3.6 %collective-permute-done.refs_0_ = bf16[6,64,128]{2,1,0:T(8,128)(2,1)S(1)} collective-permute-done((bf16[6,64,128]{2,1,0:T(8,128)(2,1)}, bf16[6,64,128]{2,1,0:T(8,128)(2,1)S(1)}, u32[]{:S(2)}, u32[]{:S(2)}) %collective-permute-start) | collective-permute-done | bytes 98336 | tf_op jit(solution)/shard_map/cond/branch_1_fun/ppermute | solution.py:584
  58.4 5.1 %collective-permute-done.1.refs_1_ = bf16[6,64,128]{2,1,0:T(8,128)(2,1)S(1)} collective-permute-done((bf16[6,64,128]{2,1,0:T(8,128)(2,1)}, bf16[6,64,128]{2,1,0:T(8,128)(2,1)S(1)}, u32[]{:S(2)}, u32[]{:S(2)}) %collective-permute-start.1) | collective-permute-done | bytes 98336 | tf_op jit(solution)/shard_map/cond/branch_1_fun/ppermute | solution.py:584
  63.4 2.1 %collective-permute-done.2.refs_2_ = bf16[6,64,128]{2,1,0:T(8,128)(2,1)S(1)} collective-permute-done((bf16[6,64,128]{2,1,0:T(8,128)(2,1)}, bf16[6,64,128]{2,1,0:T(8,128)(2,1)S(1)}, u32[]{:S(2)}, u32[]{:S(2)}) %collective-permute-start.2) | collective-permute-done | bytes 98336 | tf_op jit(solution)/shard_map/cond/branch_1_fun/ppermute | solution.py:584
  65.6 8.4 %all-to-all-done = bf16[8,14,64,128]{3,2,1,0:T(8,128)(2,1)S(1)} async-done(((bf16[8,14,64,128]{3,2,1,0:T(8,128)(2,1)}), bf16[8,14,64,128]{3,2,1,0:T(8,128)(2,1)S(1)}, u32[]{:S(2)}, u32[]{:S(2)}) %all-to-all-start) | async-done | bytes 1835040 | tf_op jit(solution)/shard_map/cond/branch_1_fun/all_to_all | solution.py:578
  73.9 0.0 copy-done.2
  73.9 0.0 copy-start
  73.9 1.2 copy-done
  75.2 5.1 %merge.1 = bf16[8,5,48,128]{3,2,1,0:T(8,128)(2,1)} custom-call(s32[8,256]{1,0:T(8,128)S(1)} %get-tuple-element.42.table.table_ref, s32[8,256]{1,0:T(8,128)S(1)} %copy-done.2, s32[32,128]{1,0:T(8,128)S(1)} %get-tuple-element.54.entry, f32[256,64,128]{2,1,0:T(8,128)} %get-tuple-element.55.local_ref, f32[5,392,128]{2,1,0:T(8,128)S(1)} %copy-done, ...), custom_call_target="tpu_custom_call" | custom-call | tf_op jit(solution)/shard_map/cond/branch_1_fun/merge/pallas_call | solution.py:602
  80.3 6.8 %all-to-all-start.1 = ((bf16[8,5,48,128]{3,2,1,0:T(8,128)(2,1)}), bf16[8,5,48,128]{3,2,1,0:T(8,128)(2,1)S(1)}, u32[]{:S(2)}, u32[]{:S(2)}) async-start(bf16[8,5,48,128]{3,2,1,0:T(8,128)(2,1)} %merge.1), calls=%async_computation.1 | async-start | bytes 983040 | tf_op jit(solution)/shard_map/cond/branch_1_fun/all_to_all | solution.py:618
  87.0 0.1 reshape.89
  87.1 0.1 copy.9
  87.2 0.2 reshape.136.spot_ref
  87.4 12.6 %all-to-all-done.1.came = bf16[8,5,48,128]{3,2,1,0:T(8,128)(2,1)S(1)} async-done(((bf16[8,5,48,128]{3,2,1,0:T(8,128)(2,1)}), bf16[8,5,48,128]{3,2,1,0:T(8,128)(2,1)S(1)}, u32[]{:S(2)}, u32[]{:S(2)}) %all-to-all-start.1) | async-done | bytes 491552 | tf_op jit(solution)/shard_map/cond/branch_1_fun/all_to_all | solution.py:618
  100.0 0.4 spread.1
  100.4 4.8 %collective-permute-start.3 = (bf16[5,16,512]{2,1,0:T(8,128)(2,1)S(1)}, bf16[5,16,512]{2,1,0:T(8,128)(2,1)S(1)}, u32[]{:S(2)}, u32[]{:S(2)}) collective-permute-start(bf16[5,16,512]{2,1,0:T(8,128)(2,1)S(1)} %get-tuple-element.74), channel_id=1, source_target_pairs={{0,8},{8,16},{16,24},{1,9},{9,17},{17,25},{2,10},{10,18},{18,26},{... | collective-permute-start | bytes 245768 | tf_op jit(solution)/shard_map/ppermute | solution.py:29
  105.3 1.9 %collective-permute-start.4 = (bf16[5,16,512]{2,1,0:T(8,128)(2,1)S(1)}, bf16[5,16,512]{2,1,0:T(8,128)(2,1)S(1)}, u32[]{:S(2)}, u32[]{:S(2)}) collective-permute-start(bf16[5,16,512]{2,1,0:T(8,128)(2,1)S(1)} %get-tuple-element.75), channel_id=1, source_target_pairs={{8,0},{16,8},{24,16},{9,1},{17,9},{25,17},{10,2},{18,10},{26,18},{... | collective-permute-start | bytes 245768 | tf_op jit(solution)/shard_map/ppermute | solution.py:30
  107.2 0.1 select_reduce_fusion
  107.3 0.0 collective-permute-done.3
  107.3 3.7 %collective-permute-done.4 = bf16[5,16,512]{2,1,0:T(8,128)(2,1)S(1)} collective-permute-done((bf16[5,16,512]{2,1,0:T(8,128)(2,1)S(1)}, bf16[5,16,512]{2,1,0:T(8,128)(2,1)S(1)}, u32[]{:S(2)}, u32[]{:S(2)}) %collective-permute-start.4) | collective-permute-done | bytes 81952 | tf_op jit(solution)/shard_map/ppermute | solution.py:30
  111.0 0.1 pad_maximum_fusion.2
  111.1 1.2 %collective-permute-start.5 = (bf16[5,96,16]{2,1,0:T(8,128)(2,1)S(1)}, bf16[5,96,16]{2,1,0:T(8,128)(2,1)S(1)}, u32[]{:S(2)}, u32[]{:S(2)}) collective-permute-start(bf16[5,96,16]{2,1,0:T(8,128)(2,1)S(1)} %get-tuple-element.72), channel_id=1, source_target_pairs={{0,1},{1,2},{2,3},{3,4},{4,5},{5,6},{6,7},{7,0},{8,9},{9,10},{10,1... | collective-permute-start | bytes 46088 | tf_op jit(solution)/shard_map/ppermute | solution.py:29
  112.4 3.0 %collective-permute-start.6 = (bf16[5,96,16]{2,1,0:T(8,128)(2,1)S(1)}, bf16[5,96,16]{2,1,0:T(8,128)(2,1)S(1)}, u32[]{:S(2)}, u32[]{:S(2)}) collective-permute-start(bf16[5,96,16]{2,1,0:T(8,128)(2,1)S(1)} %get-tuple-element.73), channel_id=1, source_target_pairs={{1,0},{2,1},{3,2},{4,3},{5,4},{6,5},{7,6},{0,7},{9,8},{10,9},{11,1... | collective-permute-start | bytes 46088 | tf_op jit(solution)/shard_map/ppermute | solution.py:30
  115.3 2.4 %collective-permute-done.5 = bf16[5,96,16]{2,1,0:T(8,128)(2,1)S(1)} collective-permute-done((bf16[5,96,16]{2,1,0:T(8,128)(2,1)S(1)}, bf16[5,96,16]{2,1,0:T(8,128)(2,1)S(1)}, u32[]{:S(2)}, u32[]{:S(2)}) %collective-permute-start.5) | collective-permute-done | bytes 15392 | tf_op jit(solution)/shard_map/ppermute | solution.py:29
  117.7 0.5 collective-permute-done.6
  118.2 1.9 %fusion.9 = f32[5,96,512]{2,1,0:T(8,128)S(1)} fusion(bf16[5,96,16]{2,1,0:T(8,128)(2,1)S(1)} %collective-permute-done.6, bf16[5,16,512]{2,1,0:T(8,128)(2,1)S(1)} %collective-permute-done.4, bf16[5,64,512]{2,1,0:T(8,128)(2,1)S(1)} %get-tuple-element.76, bf16[5,16,512]{2,1,0:T(8,128)(2,1)S(1)} %collective-permute-done.3, ...), kind=kOutput, calls=%fused_computation.33 | convolution fusion | flops 1609439232 | bytes 1505280 | tf_op jit(solution)/shard_map/krb,bj->krj/dot_general | solution.py:49
  120.1 0.8 convolution_bitcast_fusion
  120.9 0.8 fusion.34
  (5 shorter events, 0.0 us)
Async XLA Ops:
  1.3 11.7 %all-to-all-start.4 = ((s32[8,1,256]{2,1,0:T(1,128)}), s32[8,1,256]{2,1,0:T(1,128)S(1)}, u32[]{:S(2)}, u32[]{:S(2)}) async-start(s32[8,1,256]{2,1,0:T(1,128)} %broadcast_in_dim.23), calls=%async_computation.4 | async-start | bytes 16384 | tf_op jit(solution)/shard_map/all_to_all | solution.py:689
  30.1 43.8 %all-to-all-start = ((bf16[8,14,64,128]{3,2,1,0:T(8,128)(2,1)}), bf16[8,14,64,128]{3,2,1,0:T(8,128)(2,1)S(1)}, u32[]{:S(2)}, u32[]{:S(2)}) async-start(bf16[8,14,64,128]{3,2,1,0:T(8,128)(2,1)} %bitcast.76), calls=%async_computation | async-start | bytes 3670016 | tf_op jit(solution)/shard_map/cond/branch_1_fun/all_to_all | solution.py:578
  33.7 24.7 %collective-permute-start = (bf16[6,64,128]{2,1,0:T(8,128)(2,1)}, bf16[6,64,128]{2,1,0:T(8,128)(2,1)S(1)}, u32[]{:S(2)}, u32[]{:S(2)}) collective-permute-start(bf16[6,64,128]{2,1,0:T(8,128)(2,1)} %get-tuple-element.58), channel_id=1, source_target_pairs={{0,1},{1,2},{2,3},{3,0},{4,5},{5,6},{6,7},{7,4},{8,9},{9,10},{10,1... | collective-permute-start | bytes 294920 | tf_op jit(solution)/shard_map/cond/branch_1_fun/ppermute | solution.py:584
  35.1 28.4 %collective-permute-start.1 = (bf16[6,64,128]{2,1,0:T(8,128)(2,1)}, bf16[6,64,128]{2,1,0:T(8,128)(2,1)S(1)}, u32[]{:S(2)}, u32[]{:S(2)}) collective-permute-start(bf16[6,64,128]{2,1,0:T(8,128)(2,1)} %get-tuple-element.59), channel_id=1, source_target_pairs={{0,2},{1,3},{2,0},{3,1},{4,6},{5,7},{6,4},{7,5},{8,10},{9,11},{10,... | collective-permute-start | bytes 294920 | tf_op jit(solution)/shard_map/cond/branch_1_fun/ppermute | solution.py:584
  36.3 29.3 %collective-permute-start.2 = (bf16[6,64,128]{2,1,0:T(8,128)(2,1)}, bf16[6,64,128]{2,1,0:T(8,128)(2,1)S(1)}, u32[]{:S(2)}, u32[]{:S(2)}) collective-permute-start(bf16[6,64,128]{2,1,0:T(8,128)(2,1)} %get-tuple-element.60), channel_id=1, source_target_pairs={{0,3},{1,0},{2,1},{3,2},{4,7},{5,4},{6,5},{7,6},{8,11},{9,8},{10,9... | collective-permute-start | bytes 294920 | tf_op jit(solution)/shard_map/cond/branch_1_fun/ppermute | solution.py:584
  40.0 0.6 copy-start.1
  40.6 33.3 %copy-start.2 = (s32[8,256]{1,0:T(8,128)S(1)}, s32[8,256]{1,0:T(8,128)}, u32[]{:S(2)}) copy-start(s32[8,256]{1,0:T(8,128)} %copy-done.1) | copy-start | bytes 24580 | tf_op jit(solution)/shard_map/cond
  73.9 1.2 copy-start
  80.3 19.7 %all-to-all-start.1 = ((bf16[8,5,48,128]{3,2,1,0:T(8,128)(2,1)}), bf16[8,5,48,128]{3,2,1,0:T(8,128)(2,1)S(1)}, u32[]{:S(2)}, u32[]{:S(2)}) async-start(bf16[8,5,48,128]{3,2,1,0:T(8,128)(2,1)} %merge.1), calls=%async_computation.1 | async-start | bytes 983040 | tf_op jit(solution)/shard_map/cond/branch_1_fun/all_to_all | solution.py:618
  100.4 6.9 %collective-permute-start.3 = (bf16[5,16,512]{2,1,0:T(8,128)(2,1)S(1)}, bf16[5,16,512]{2,1,0:T(8,128)(2,1)S(1)}, u32[]{:S(2)}, u32[]{:S(2)}) collective-permute-start(bf16[5,16,512]{2,1,0:T(8,128)(2,1)S(1)} %get-tuple-element.74), channel_id=1, source_target_pairs={{0,8},{8,16},{16,24},{1,9},{9,17},{17,25},{2,10},{10,18},{18,26},{... | collective-permute-start | bytes 245768 | tf_op jit(solution)/shard_map/ppermute | solution.py:29
  105.3 5.8 %collective-permute-start.4 = (bf16[5,16,512]{2,1,0:T(8,128)(2,1)S(1)}, bf16[5,16,512]{2,1,0:T(8,128)(2,1)S(1)}, u32[]{:S(2)}, u32[]{:S(2)}) collective-permute-start(bf16[5,16,512]{2,1,0:T(8,128)(2,1)S(1)} %get-tuple-element.75), channel_id=1, source_target_pairs={{8,0},{16,8},{24,16},{9,1},{17,9},{25,17},{10,2},{18,10},{26,18},{... | collective-permute-start | bytes 245768 | tf_op jit(solution)/shard_map/ppermute | solution.py:30
  111.1 6.6 %collective-permute-start.5 = (bf16[5,96,16]{2,1,0:T(8,128)(2,1)S(1)}, bf16[5,96,16]{2,1,0:T(8,128)(2,1)S(1)}, u32[]{:S(2)}, u32[]{:S(2)}) collective-permute-start(bf16[5,96,16]{2,1,0:T(8,128)(2,1)S(1)} %get-tuple-element.72), channel_id=1, source_target_pairs={{0,1},{1,2},{2,3},{3,4},{4,5},{5,6},{6,7},{7,0},{8,9},{9,10},{10,1... | collective-permute-start | bytes 46088 | tf_op jit(solution)/shard_map/ppermute | solution.py:29
  112.4 5.8 %collective-permute-start.6 = (bf16[5,96,16]{2,1,0:T(8,128)(2,1)S(1)}, bf16[5,96,16]{2,1,0:T(8,128)(2,1)S(1)}, u32[]{:S(2)}, u32[]{:S(2)}) collective-permute-start(bf16[5,96,16]{2,1,0:T(8,128)(2,1)S(1)} %get-tuple-element.73), channel_id=1, source_target_pairs={{1,0},{2,1},{3,2},{4,3},{5,4},{6,5},{7,6},{0,7},{9,8},{10,9},{11,1... | collective-permute-start | bytes 46088 | tf_op jit(solution)/shard_map/ppermute | solution.py:30

commit v4 on v3

--- a/solution.py
+++ b/solution.py
@@ -11,7 +11,6 @@
 LAT_DEV = 64
 LON_DEV = 512
 LANES = 128
-RING = 32
 GROUP = 8
 CHUNK = 16
 F32 = jnp.float32
@@ -82,8 +81,15 @@
     return high, low
 
 
+def split_dot(table, other, dims=((1,), (0,))):
+    upper = jnp.floor(table * (1.0 / 256.0))
+    lower = table - upper * 256.0
+    other = other.astype(BF16)
+    return dot(upper.astype(BF16), other, dims) * 256.0 + dot(lower.astype(BF16), other, dims)
+
+
 def look_up(table, high, low):
-    return jnp.sum(dot(table, low, exact=True) * high, axis=0, keepdims=True)
+    return jnp.sum(split_dot(table, low) * high, axis=0, keepdims=True)
 
 
 def prefixes(height, tile_rows):
@@ -105,7 +111,46 @@
     return float(d) if isinstance(d, int) else lax.convert_element_type(d, F32)
 
 
+def load_all(sources, targets, sem):
+    copies = []
+    for source, target in zip(sources, targets):
+        rows = source.shape[0] // 4
+        for c in range(4):
+            part = pl.ds(c * rows, rows)
+            copies.append(pltpu.make_async_copy(source.at[part], target.at[part], sem.at[len(copies)]))
+    return copies
+
+
 def plan_kernel(
+    count, blocks, cap, extra, mcap, parts, me_ref, keys_ref, src_ref, fields, weights, *refs
+):
+    table_ref, owner_ref, pres, far_ref = refs[:4]
+    near_refs = refs[4 : 4 + parts]
+    tall, xs, ws, total, packed, table, load_sem, table_sem, out_sem = refs[4 + parts :]
+    loading = load_all((fields, weights), (xs, ws), load_sem)
+    for copy in loading:
+        copy.start()
+    make_table(count, blocks, cap, extra, mcap, me_ref, keys_ref, src_ref, table_ref, owner_ref, pres, tall)
+    to_scalar = pltpu.make_async_copy(table_ref, table, table_sem)
+    to_scalar.start()
+    for copy in loading:
+        copy.wait()
+    to_scalar.wait()
+    sends = packed.shape[0] - 1
+    first = count * cap
+    high = (table[4, 0] + GROUP - 1) // GROUP * GROUP
+    products(table, xs, ws, 0, high, total, packed, 0, sends, sends)
+    outs = [pltpu.make_async_copy(packed.at[pl.ds(0, first)], far_ref, out_sem.at[0])]
+    for j in range(parts):
+        rows = pl.ds(first + j * extra, extra)
+        outs.append(pltpu.make_async_copy(packed.at[rows], near_refs[j], out_sem.at[1 + j]))
+    for out in outs:
+        out.start()
+    for out in outs:
+        out.wait()
+
+
+def make_table(
     count, blocks, cap, extra, mcap, me_ref, keys_ref, src_ref, table_ref, owner_ref, pres, tall
 ):
     me = me_ref[0]
@@ -222,19 +267,22 @@
     goes = look_up(place, high, low) - 1.0
     leaving = jnp.sum((goes < sends - 0.5).astype(F32), axis=1, keepdims=True)
     first_at, second_at = iota((pairs, pairs), 0), iota((pairs, pairs), 1)
+    kind = iota((8, pairs), 0)
     same = (first_at == second_at).astype(F32)
-    upright = dot(same, jnp.broadcast_to(goes, (8, pairs)), ((1,), (1,)), exact=True)[:, 0:1]
+    parts = jnp.where(kind == 0, jnp.floor(goes * (1.0 / 256.0)), 0.0)
+    parts = jnp.where(kind == 1, goes - 256.0 * parts[0:1, :], parts)
+    upright = dot(same.astype(BF16), parts.astype(BF16), ((1,), (1,)))
+    upright = upright[:, 0:1] * 256.0 + upright[:, 1:2]
     earlier = (upright < goes - 0.5) | ((jnp.abs(upright - goes) < 0.5) & (first_at < second_at))
     position = jnp.sum(earlier.astype(F32), axis=0, keepdims=True)
     at = iota((1, pairs), 1).astype(F32)
-    kind = iota((8, pairs), 0)
     values = jnp.where(
         kind == 0,
         at,
         jnp.where(kind == 1, goes, jnp.where(kind == 2, src_ref[...].astype(F32), 0.0)),
     )
     order = (first_at == (position + 0.5).astype(I32)).astype(F32)
-    result = (dot(values, order, ((1,), (1,)), exact=True) + 0.5).astype(I32)
+    result = (split_dot(values, order, ((1,), (1,))) + 0.5).astype(I32)
     lane = iota((8, pairs), 1)
     facts = jnp.where(lane == 0, leaving.astype(I32), over)
     facts = jnp.where(lane == 1, total_mine.astype(I32), facts)
@@ -271,7 +319,8 @@
         rank_coming = prefix(coming, rows_ahead)
         code = coming * (rank_coming * 1024.0 + rank_several + 1.0)
         high, low = one_hots(keys_ref[d], height)
-        seen = (look_up(code, high, low) + 0.5).astype(I32) - 1
+        seen = jnp.sum(dot(code, low, exact=True) * high, axis=0, keepdims=True)
+        seen = (seen + 0.5).astype(I32) - 1
         rank, local = seen >> 10, seen & 1023
         hit = iota((entry_rows, pairs), 0) == rank
         column = jnp.max(jnp.where(hit, local, -1), axis=1, keepdims=True)
@@ -297,27 +346,46 @@
     slot = jnp.where(goes < sends, -1, goes - sends)
     in_slot = (iota((pairs, pairs), 0) == slot).astype(F32)
     weighed = jnp.where(iota((8, pairs), 0) == 0, lands, 1.0)
-    summed = dot(weighed, in_slot, ((1,), (1,)), exact=True)
+    summed = split_dot(weighed, in_slot, ((1,), (1,)))
     landing = summed[0:1, :] / jnp.maximum(summed[1:2, :], 1.0)
     landing_ref[...] = jnp.broadcast_to((landing + 0.25).astype(I32), landing_ref.shape)
 
 
-def make_plan(me, keys, pair_source, count, blocks, cap, extra, mcap):
-    pairs = keys.shape[2]
+def make_plan(me, keys, pair_source, fields, weights, cap, extra, mcap):
+    count, _, pairs = keys.shape
+    blocks, channels, cells = fields.shape
     height = count * blocks // LANES
+    parts = count // 2 - 1
+    first = count * cap
+    sends = first + parts * extra
     vmem = pl.BlockSpec(memory_space=pltpu.VMEM)
-    return pl.pallas_call(
-        functools.partial(plan_kernel, count, blocks, cap, extra, mcap),
-        out_shape=(
+    hbm = pl.BlockSpec(memory_space=pl.ANY)
+    table, owner, pres, *sent = pl.pallas_call(
+        functools.partial(plan_kernel, count, blocks, cap, extra, mcap, parts),
+        out_shape=[
             jax.ShapeDtypeStruct((8, pairs), I32),
             jax.ShapeDtypeStruct((height, LANES), I32),
             jax.ShapeDtypeStruct((count, height, LANES), F32),
-        ),
-        in_specs=[pl.BlockSpec(memory_space=pltpu.SMEM), vmem, vmem],
-        out_specs=(vmem, vmem, vmem),
-        scratch_shapes=[pltpu.VMEM((height * count, LANES), F32)],
-        name="plan",
-    )(me, keys, pair_source[None, :])
+            jax.ShapeDtypeStruct((first, channels, cells), BF16),
+        ]
+        + [jax.ShapeDtypeStruct((extra, channels, cells), BF16)] * parts,
+        in_specs=[pl.BlockSpec(memory_space=pltpu.SMEM), vmem, vmem, hbm, hbm],
+        out_specs=[vmem] * 3 + [hbm] * (1 + parts),
+        scratch_shapes=[
+            pltpu.VMEM((height * count, LANES), F32),
+            pltpu.VMEM(fields.shape, BF16),
+            pltpu.VMEM(weights.shape, BF16),
+            pltpu.VMEM((sends + 1, channels, cells), F32),
+            pltpu.VMEM((sends + 1, channels, cells), BF16),
+            pltpu.SMEM((8, pairs), I32),
+            pltpu.SemaphoreType.DMA((8,)),
+            pltpu.SemaphoreType.DMA,
+            pltpu.SemaphoreType.DMA((1 + parts,)),
+        ],
+        compiler_params=pltpu.CompilerParams(vmem_limit_bytes=53 << 20),
+        name="leaving",
+    )(me, keys, pair_source[None, :], fields, weights)
+    return table, owner, pres, sent
 
 
 def finish_plan(me, keys, owner, pres, table, count, blocks, cap, extra, mcap):
@@ -339,39 +407,13 @@
     )(me, keys, owner, pres, table)
 
 
-def pair_copies(table, src, weights, xs, ws, x_sem, w_sem, i):
-    slot = i % RING
-    return (
-        pltpu.make_async_copy(src.at[table[2, i]], xs.at[slot], x_sem.at[slot]),
-        pltpu.make_async_copy(weights.at[table[0, i]], ws.at[slot], w_sem.at[slot]),
-    )
-
-
-def products(table, src, weights, xs, ws, x_sem, w_sem, low, high, target, packed, first, last, dummy):
-    copies = functools.partial(pair_copies, table, src, weights, xs, ws, x_sem, w_sem)
-
-    def start(i):
-        for copy in copies(i):
-            copy.start()
-
-    def prime(i, carry):
-        @pl.when(i < high)
-        def _():
-            start(i)
-
-        return carry
-
-    lax.fori_loop(low, low + RING, prime, 0)
-
+def products(table, xs, ws, low, high, target, packed, first, last, dummy):
     def step(g, carry):
         base = g * GROUP
-        for u in range(GROUP):
-            for copy in copies(base + u):
-                copy.wait()
         results = []
         for u in range(GROUP):
-            slot = (base + u) % RING
-            results.append(dot(xs[slot], ws[slot], ((1,), (1,))))
+            x, w = xs[table[2, base + u]], ws[table[0, base + u]]
+            results.append(dot(x, w, ((1,), (1,))))
         for u in range(GROUP):
             i = base + u
             place = table[1, i]
@@ -382,32 +424,9 @@
             target[where] = value
             if packed is not None:
                 packed[where] = value.astype(BF16)
-
-        @pl.when(base + RING < high)
-        def _():
-            for u in range(GROUP):
-                start(base + RING + u)
-
         return carry
 
     lax.fori_loop(low // GROUP, high // GROUP, step, 0)
-
-
-def send_kernel(first, extra, parts, table, src, weights, *refs):
-    far_ref, near_refs = refs[0], refs[1 : 1 + parts]
-    total, packed, xs, ws, x_sem, w_sem, out_sem = refs[1 + parts :]
-    sends = packed.shape[0] - 1
-    leaving = table[4, 0]
-    high = (leaving + GROUP - 1) // GROUP * GROUP
-    products(table, src, weights, xs, ws, x_sem, w_sem, 0, high, total, packed, 0, sends, sends)
-    outs = [pltpu.make_async_copy(packed.at[pl.ds(0, first)], far_ref, out_sem.at[0])]
-    for j in range(parts):
-        rows = pl.ds(first + j * extra, extra)
-        outs.append(pltpu.make_async_copy(packed.at[rows], near_refs[j], out_sem.at[1 + j]))
-    for out in outs:
-        out.start()
-    for out in outs:
-        out.wait()
 
 
 def moment_rows(value):
@@ -425,7 +444,7 @@
             i = begin + g * 4 + u
             good = i < end
             at = jnp.where(good, i, 0)
-            place = jnp.where(good, landing[0, at], spare)
+            place = jnp.where(good, jnp.minimum(landing[0, at], spare), spare)
             for k, row in enumerate(moment_rows(total[at])):
                 moments[k, pl.ds(place, 1), :] = row
         return carry
@@ -439,16 +458,18 @@
 
 
 def local_kernel(
-    sends, table, landing, src, weights, local_ref, moments, total, xs, ws, x_sem, w_sem, out_sem
+    sends, table, landing, fields, weights, local_ref, moments, total, xs, ws, load_sem, out_sem
 ):
     pairs = weights.shape[0]
     leaving, owned, several = table[4, 0], table[4, 1], table[4, 2]
     low = leaving // GROUP * GROUP
-
+    loading = load_all((fields, weights), (xs, ws), load_sem)
+    for copy in loading:
+        copy.start()
     moments[...] = jnp.zeros(moments.shape, F32)
-    products(
-        table, src, weights, xs, ws, x_sem, w_sem, low, pairs, total, None, sends, sends + pairs, pairs
-    )
+    for copy in loading:
+        copy.wait()
+    products(table, xs, ws, low, pairs, total, None, sends, sends + pairs, pairs)
     chunks = (several + CHUNK - 1) // CHUNK
 
     def begin(c, carry):
@@ -501,7 +522,7 @@
                 r = low + g * 4 + u
                 good = r < high
                 at = jnp.where(good, r, low)
-                where = jnp.where(good, entry[at, s], spare)
+                where = jnp.where(good, jnp.maximum(entry[at, s], 0), spare)
                 total[where] = total[where] + came[shift + at].astype(F32)
             return inner
 
@@ -517,7 +538,7 @@
 
     def from_near(j, carry):
         s = me // half * half + (me % half + half - j - 1) % half
-        number = jnp.maximum(entry[counts_row, s], cap)
+        number = jnp.clip(entry[counts_row, s], cap, cap + extra)
         add(s, cap, number, near, j * extra - cap)
         return carry
 
@@ -543,7 +564,7 @@
             ].astype(BF16)
 
 
-def direct(cap, extra, mcap, source_fields, weight_blocks, me, keys, table, owner, pres):
+def direct(cap, extra, mcap, source_fields, weight_blocks, me, keys, table, owner, pres, sent):
     count = lax.axis_size("lon")
     half = count // 2
     blocks, channels, cells = source_fields.shape
@@ -554,27 +575,6 @@
     smem = pl.BlockSpec(memory_space=pltpu.SMEM)
     vmem = pl.BlockSpec(memory_space=pltpu.VMEM)
     hbm = pl.BlockSpec(memory_space=pl.ANY)
-    buffers = [
-        pltpu.VMEM((RING, channels, cells), BF16),
-        pltpu.VMEM((RING, cells, cells), BF16),
-        pltpu.SemaphoreType.DMA((RING,)),
-        pltpu.SemaphoreType.DMA((RING,)),
-    ]
-    sent = pl.pallas_call(
-        functools.partial(send_kernel, first, extra, parts),
-        out_shape=[jax.ShapeDtypeStruct((first, channels, cells), BF16)]
-        + [jax.ShapeDtypeStruct((extra, channels, cells), BF16)] * parts,
-        in_specs=[smem, hbm, hbm],
-        out_specs=[hbm] + [hbm] * parts,
-        scratch_shapes=[
-            pltpu.VMEM((sends + 1, channels, cells), F32),
-            pltpu.VMEM((sends + 1, channels, cells), BF16),
-        ]
-        + buffers
-        + [pltpu.SemaphoreType.DMA((1 + parts,))],
-        name="leaving",
-    )(table, source_fields, weight_blocks)
-    sent, owner = lax.optimization_barrier((sent, owner))
     far = lax.all_to_all(
         sent[0].reshape(count, cap, channels, cells), "lon", split_axis=0, concat_axis=0, tiled=True
     ).reshape(first, channels, cells)
@@ -594,9 +594,14 @@
         ),
         in_specs=[smem, smem, hbm, hbm],
         out_specs=(hbm, vmem),
-        scratch_shapes=[pltpu.VMEM((pairs + 1, channels, cells), F32)]
-        + buffers
-        + [pltpu.SemaphoreType.DMA((chunk_count,))],
+        scratch_shapes=[
+            pltpu.VMEM((pairs + 1, channels, cells), F32),
+            pltpu.VMEM(source_fields.shape, BF16),
+            pltpu.VMEM(weight_blocks.shape, BF16),
+            pltpu.SemaphoreType.DMA((8,)),
+            pltpu.SemaphoreType.DMA((chunk_count,)),
+        ],
+        compiler_params=pltpu.CompilerParams(vmem_limit_bytes=50 << 20),
         name="staying",
     )(table, landing, source_fields, weight_blocks)
     finished = pl.pallas_call(
@@ -690,13 +695,20 @@
         jnp.broadcast_to(keys, (count, 1, pairs)), "lon", split_axis=0, concat_axis=0, tiled=True
     )
     me = lax.axis_index("lon").astype(I32)[None]
-    table, owner, pres = make_plan(me, all_keys, pair_source, count, blocks, cap, extra, mcap)
+    table, owner, pres, sent = make_plan(
+        me, all_keys, pair_source, source_fields, weight_blocks, cap, extra, mcap
+    )
+    sent, owner = lax.optimization_barrier((sent, owner))
+    moments = direct(
+        cap, extra, mcap, source_fields, weight_blocks, me, all_keys, table, owner, pres, sent
+    )
     moments = lax.cond(
         table[4, 3] == 0,
-        lambda: direct(
-            cap, extra, mcap, source_fields, weight_blocks, me, all_keys, table, owner, pres
+        lambda kept: kept,
+        lambda kept: padded_exchange(
+            source_fields, weight_blocks, pair_source, targets, pair_block
         ),
-        lambda: padded_exchange(source_fields, weight_blocks, pair_source, targets, pair_block),
+        moments,
     )
     lon_band = band_matrix(LON_DEV)
     lat_band = band_matrix(LAT_DEV)

time: 122 us -> 120 us (0.984)
  Pallas kernels: 37.8 us -> 34 us
    pallas_call x1 -> x0, Pallas kernels: 7.96 us -> none  [direct(): pl.pallas_call(functools.partial(send_kernel, first, extra, parts), out_s...]
    pallas_call x1, Pallas kernels: 7.62 us -> 12.3 us  [make_plan(): pl.pallas_call(functools.partial(plan_kernel, count, blocks, cap, extra,...]
    all_to_all x1, waiting for transfers between devices: 12.6 us -> 10.3 us  [direct(): lax.all_to_all(finished, 'lon', split_axis=0, concat_axis=0, tiled=True)]
    ppermute x3, waiting for transfers between devices: 10.8 us -> 12.7 us  [direct(): near.append(lax.ppermute(sent[1 + j], 'lon', turn))]
    cond x6 -> x0, local copies, waits for them, and re-layouts: 1.8 us -> none
    all_to_all x1, waiting for transfers between devices: 3.96 us -> 5.37 us  [local(): lax.all_to_all(jnp.broadcast_to(keys, (count, 1, pairs)), 'lon', split_ax...]
  transfers between devices with their start and end apart: 10 -> 10, of which waited for: 9 -> 9; matrix products, arithmetic and copies ran while one was open for 1% -> 1% of each run, Pallas kernels for 14% -> 13%
where the time goes in v4:
time: 120 us; the launch traced here: 119 us
  waiting for transfers between devices  43.3 us (36%)
  Pallas kernels  34 us (28%)
  starting transfers between devices  31 us (26%)
  matrix products  3.67 us (3%)
  other arithmetic  3.26 us (3%)
  local copies, waits for them, and re-layouts  2.46 us (2%)
  between operations  1.42 us (1%)
    pallas_call x1, Pallas kernels, direct(): pl.pallas_call(functools.partial(local_kernel, sends), out_shape=(jax.Sha...  13 us
    ppermute x3, waiting for transfers between devices, direct(): near.append(lax.ppermute(sent[1 + j], 'lon', turn))  12.7 us
    pallas_call x1, Pallas kernels, make_plan(): pl.pallas_call(functools.partial(plan_kernel, count, blocks, cap, extra,...  12.3 us
    all_to_all x1, waiting for transfers between devices, direct(): lax.all_to_all(finished, 'lon', split_axis=0, concat_axis=0, tiled=True)  10.3 us
    all_to_all x1, waiting for transfers between devices, direct(): lax.all_to_all(sent[0].reshape(count, cap, channels, cells), 'lon', split...  8.37 us
    all_to_all x1, starting transfers between devices, direct(): lax.all_to_all(finished, 'lon', split_axis=0, concat_axis=0, tiled=True)  6.99 us
    all_to_all x1, starting transfers between devices, local(): lax.all_to_all(jnp.broadcast_to(keys, (count, 1, pairs)), 'lon', split_ax...  6.34 us
    ppermute x2, starting transfers between devices, padded(): before = lax.ppermute(last, axis, up)  5.4 us
  transfers between devices with their start and end apart: 10, of which 9 were waited for; matrix products, arithmetic and copies ran while one was open for 1% of the time, Pallas kernels for 13%

profile of v4, /device:TPU:1, one launch (start us, length us, event | category | flops | bytes accessed | tf_op | source)
XLA Modules:
  0.0 119.1 jit_solution(13697126911361839008)
XLA Ops:
  0.0 0.7 multiply_add_fusion
  0.7 0.6 broadcast_in_dim.23
  1.3 6.3 %all-to-all-start.2 = ((s32[8,1,256]{2,1,0:T(1,128)}), s32[8,1,256]{2,1,0:T(1,128)S(1)}, u32[]{:S(2)}, u32[]{:S(2)}) async-start(s32[8,1,256]{2,1,0:T(1,128)} %broadcast_in_dim.23), calls=%async_computation.2 | async-start | bytes 16384 | tf_op jit(solution)/shard_map/all_to_all | solution.py:694
  7.6 5.4 %all-to-all-done.2.keys_ref = s32[8,1,256]{2,1,0:T(1,128)S(1)} async-done(((s32[8,1,256]{2,1,0:T(1,128)}), s32[8,1,256]{2,1,0:T(1,128)S(1)}, u32[]{:S(2)}, u32[]{:S(2)}) %all-to-all-start.2) | async-done | bytes 8224 | tf_op jit(solution)/shard_map/all_to_all | solution.py:694
  13.0 12.3 %leaving.1 = (s32[8,256]{1,0:T(8,128)S(1)}, s32[16,128]{1,0:T(8,128)S(1)}, f32[8,16,128]{2,1,0:T(8,128)S(1)}, bf16[112,64,128]{2,1,0:T(8,128)(2,1)}, bf16[6,64,1...) custom-call(s32[1]{0:T(128)} %bitcast.6.me_ref, ...), custom_call_target="tpu_custom_call" | custom-call | tf_op jit(solution)/shard_map/leaving/pallas_call | solution.py:363
  25.3 3.6 %all-to-all-start.3 = ((bf16[8,14,64,128]{3,2,1,0:T(8,128)(2,1)}), bf16[8,14,64,128]{3,2,1,0:T(8,128)(2,1)S(1)}, u32[]{:S(2)}, u32[]{:S(2)}) async-start(bf16[8,14,64,128]{3,2,1,0:T(8,128)(2,1)} %bitcast.76), calls=%async_computation.3 | async-start | bytes 3670016 | tf_op jit(solution)/shard_map/all_to_all | solution.py:578
  28.9 1.4 %collective-permute-start = (bf16[6,64,128]{2,1,0:T(8,128)(2,1)S(1)}, bf16[6,64,128]{2,1,0:T(8,128)(2,1)S(1)}, u32[]{:S(2)}, u32[]{:S(2)}) collective-permute-start(bf16[6,64,128]{2,1,0:T(8,128)(2,1)S(1)} %get-tuple-element.58), channel_id=1, source_target_pairs={{0,1},{1,2},{2,3},{3,0},{4,5},{5,6},{6,7},{7,4},{8,9},{9,10},{10,1... | collective-permute-start | bytes 294920 | tf_op jit(solution)/shard_map/ppermute | solution.py:584
  30.3 1.2 %collective-permute-start.1 = (bf16[6,64,128]{2,1,0:T(8,128)(2,1)S(1)}, bf16[6,64,128]{2,1,0:T(8,128)(2,1)S(1)}, u32[]{:S(2)}, u32[]{:S(2)}) collective-permute-start(bf16[6,64,128]{2,1,0:T(8,128)(2,1)S(1)} %get-tuple-element.59), channel_id=1, source_target_pairs={{0,2},{1,3},{2,0},{3,1},{4,6},{5,7},{6,4},{7,5},{8,10},{9,11},{10,... | collective-permute-start | bytes 294920 | tf_op jit(solution)/shard_map/ppermute | solution.py:584
  31.5 1.2 collective-permute-start.2
  32.7 2.4 %finish.1 = (s32[32,128]{1,0:T(8,128)S(1)}, s32[8,128]{1,0:T(8,128)S(1)}, s32[8,256]{1,0:T(8,128)S(1)}) custom-call(s32[1]{0:T(128)} %bitcast.6.me_ref, s32[8,1,256]{2,1,0:T(1,128)S(1)} %all-to-all-done.2.keys_ref, s32[16,128]{1,0:T(8,128)S(1)} %get-tuple-element.50.owner_ref, f32[8,16,128]{2,1,0:T(8,128)S(1)} %get-tuple-element.51.pres, ...), custom_call_target="tpu_custom_call" | custom-call | tf_op jit(solution)/shard_map/finish/pallas_call | solution.py:396
  35.1 13.0 %staying.1 = (f32[256,64,128]{2,1,0:T(8,128)}, f32[5,392,128]{2,1,0:T(8,128)S(1)}) custom-call(s32[8,256]{1,0:T(8,128)S(1)} %get-tuple-element.44.table_ref.table, s32[8,256]{1,0:T(8,128)S(1)} %get-tuple-element.53.landing, bf16[256,64,128]{2,1,0:T(8,128)(2,1)} %fields.3, bf16[256,128,128]{2,1,0:T(8,128)(2,1)} %weights.3), custom_call_target="tpu_custom_call" | custom-call | tf_op jit(solution)/shard_map/staying/pallas_call | solution.py:589
  48.1 5.7 %collective-permute-done.refs_0_ = bf16[6,64,128]{2,1,0:T(8,128)(2,1)S(1)} collective-permute-done((bf16[6,64,128]{2,1,0:T(8,128)(2,1)S(1)}, bf16[6,64,128]{2,1,0:T(8,128)(2,1)S(1)}, u32[]{:S(2)}, u32[]{:S(2)}) %collective-permute-start) | collective-permute-done | bytes 98336 | tf_op jit(solution)/shard_map/ppermute | solution.py:584
  53.8 4.9 %collective-permute-done.1.refs_1_ = bf16[6,64,128]{2,1,0:T(8,128)(2,1)S(1)} collective-permute-done((bf16[6,64,128]{2,1,0:T(8,128)(2,1)S(1)}, bf16[6,64,128]{2,1,0:T(8,128)(2,1)S(1)}, u32[]{:S(2)}, u32[]{:S(2)}) %collective-permute-start.1) | collective-permute-done | bytes 98336 | tf_op jit(solution)/shard_map/ppermute | solution.py:584
  58.7 2.1 %collective-permute-done.2.refs_2_ = bf16[6,64,128]{2,1,0:T(8,128)(2,1)S(1)} collective-permute-done((bf16[6,64,128]{2,1,0:T(8,128)(2,1)S(1)}, bf16[6,64,128]{2,1,0:T(8,128)(2,1)S(1)}, u32[]{:S(2)}, u32[]{:S(2)}) %collective-permute-start.2) | collective-permute-done | bytes 98336 | tf_op jit(solution)/shard_map/ppermute | solution.py:584
  60.8 8.4 %all-to-all-done.3 = bf16[8,14,64,128]{3,2,1,0:T(8,128)(2,1)S(1)} async-done(((bf16[8,14,64,128]{3,2,1,0:T(8,128)(2,1)}), bf16[8,14,64,128]{3,2,1,0:T(8,128)(2,1)S(1)}, u32[]{:S(2)}, u32[]{:S(2)}) %all-to-all-start.3) | async-done | bytes 1835040 | tf_op jit(solution)/shard_map/all_to_all | solution.py:578
  69.2 0.0 copy-start
  69.2 0.0 copy-start.1
  69.2 5.1 %merge.1 = bf16[8,5,48,128]{3,2,1,0:T(8,128)(2,1)} custom-call(s32[8,256]{1,0:T(8,128)S(1)} %get-tuple-element.44.table_ref.table, s32[8,256]{1,0:T(8,128)S(1)} %get-tuple-element.53.landing, s32[32,128]{1,0:T(8,128)S(1)} %get-tuple-element.54.entry, f32[256,64,128]{2,1,0:T(8,128)} %get-tuple-element.55.local_ref, ...), custom_call_target="tpu_custom_call" | custom-call | tf_op jit(solution)/shard_map/merge/pallas_call | solution.py:607
  74.4 7.0 %all-to-all-start.4 = ((bf16[8,5,48,128]{3,2,1,0:T(8,128)(2,1)}), bf16[8,5,48,128]{3,2,1,0:T(8,128)(2,1)S(1)}, u32[]{:S(2)}, u32[]{:S(2)}) async-start(bf16[8,5,48,128]{3,2,1,0:T(8,128)(2,1)} %merge.1), calls=%async_computation.4 | async-start | bytes 983040 | tf_op jit(solution)/shard_map/all_to_all | solution.py:623
  81.3 0.6 fusion.60
  82.6 0.6 slice.46
  83.2 0.1 reshape.95
  83.3 0.1 copy.9
  83.4 0.2 reshape.140.spot_ref
  84.2 10.3 %all-to-all-done.4.came = bf16[8,5,48,128]{3,2,1,0:T(8,128)(2,1)S(1)} async-done(((bf16[8,5,48,128]{3,2,1,0:T(8,128)(2,1)}), bf16[8,5,48,128]{3,2,1,0:T(8,128)(2,1)S(1)}, u32[]{:S(2)}, u32[]{:S(2)}) %all-to-all-start.4) | async-done | bytes 491552 | tf_op jit(solution)/shard_map/all_to_all | solution.py:623
  94.5 1.2 spread.1
  95.6 0.0 copy-done
  95.6 0.0 copy-done.1
  95.6 0.9 fusion.70
  96.6 4.2 %collective-permute-start.3 = (bf16[5,16,512]{2,1,0:T(8,128)(2,1)S(1)}, bf16[5,16,512]{2,1,0:T(8,128)(2,1)S(1)}, u32[]{:S(2)}, u32[]{:S(2)}) collective-permute-start(bf16[5,16,512]{2,1,0:T(8,128)(2,1)S(1)} %get-tuple-element.68), channel_id=1, source_target_pairs={{0,8},{8,16},{16,24},{1,9},{9,17},{17,25},{2,10},{10,18},{18,26},{... | collective-permute-start | bytes 245768 | tf_op jit(solution)/shard_map/ppermute | solution.py:28
  100.8 1.9 %collective-permute-start.4 = (bf16[5,16,512]{2,1,0:T(8,128)(2,1)S(1)}, bf16[5,16,512]{2,1,0:T(8,128)(2,1)S(1)}, u32[]{:S(2)}, u32[]{:S(2)}) collective-permute-start(bf16[5,16,512]{2,1,0:T(8,128)(2,1)S(1)} %get-tuple-element.69), channel_id=1, source_target_pairs={{8,0},{16,8},{24,16},{9,1},{17,9},{25,17},{10,2},{18,10},{26,18},{... | collective-permute-start | bytes 245768 | tf_op jit(solution)/shard_map/ppermute | solution.py:29
  102.7 0.1 select_reduce_fusion
  102.8 0.0 collective-permute-done.3
  102.8 3.7 %collective-permute-done.4 = bf16[5,16,512]{2,1,0:T(8,128)(2,1)S(1)} collective-permute-done((bf16[5,16,512]{2,1,0:T(8,128)(2,1)S(1)}, bf16[5,16,512]{2,1,0:T(8,128)(2,1)S(1)}, u32[]{:S(2)}, u32[]{:S(2)}) %collective-permute-start.4) | collective-permute-done | bytes 81952 | tf_op jit(solution)/shard_map/ppermute | solution.py:29
  106.5 1.0 pad_maximum_fusion.2
  107.6 1.2 %collective-permute-start.5 = (bf16[5,96,16]{2,1,0:T(8,128)(2,1)S(1)}, bf16[5,96,16]{2,1,0:T(8,128)(2,1)S(1)}, u32[]{:S(2)}, u32[]{:S(2)}) collective-permute-start(bf16[5,96,16]{2,1,0:T(8,128)(2,1)S(1)} %get-tuple-element.66), channel_id=1, source_target_pairs={{0,1},{1,2},{2,3},{3,4},{4,5},{5,6},{6,7},{7,0},{8,9},{9,10},{10,1... | collective-permute-start | bytes 46088 | tf_op jit(solution)/shard_map/ppermute | solution.py:28
  108.8 3.0 %collective-permute-start.6 = (bf16[5,96,16]{2,1,0:T(8,128)(2,1)S(1)}, bf16[5,96,16]{2,1,0:T(8,128)(2,1)S(1)}, u32[]{:S(2)}, u32[]{:S(2)}) collective-permute-start(bf16[5,96,16]{2,1,0:T(8,128)(2,1)S(1)} %get-tuple-element.67), channel_id=1, source_target_pairs={{1,0},{2,1},{3,2},{4,3},{5,4},{6,5},{7,6},{0,7},{9,8},{10,9},{11,1... | collective-permute-start | bytes 46088 | tf_op jit(solution)/shard_map/ppermute | solution.py:29
  111.8 2.4 %collective-permute-done.5 = bf16[5,96,16]{2,1,0:T(8,128)(2,1)S(1)} collective-permute-done((bf16[5,96,16]{2,1,0:T(8,128)(2,1)S(1)}, bf16[5,96,16]{2,1,0:T(8,128)(2,1)S(1)}, u32[]{:S(2)}, u32[]{:S(2)}) %collective-permute-start.5) | collective-permute-done | bytes 15392 | tf_op jit(solution)/shard_map/ppermute | solution.py:28
  114.1 0.5 collective-permute-done.6
  114.6 2.8 %fusion.9 = f32[5,96,512]{2,1,0:T(8,128)S(1)} fusion(bf16[5,96,16]{2,1,0:T(8,128)(2,1)S(1)} %collective-permute-done.6, bf16[5,16,512]{2,1,0:T(8,128)(2,1)S(1)} %collective-permute-done.4, bf16[5,64,512]{2,1,0:T(8,128)(2,1)} %get-tuple-element.70, bf16[5,16,512]{2,1,0:T(8,128)(2,1)S(1)} %collective-permute-done.3, ...), kind=kOutput, calls=%fused_computation.33 | convolution fusion | flops 1609439232 | bytes 1505280 | tf_op jit(solution)/shard_map/krb,bj->krj/dot_general | solution.py:48
  117.5 0.8 convolution_bitcast_fusion
  118.3 0.8 fusion.34
  (5 shorter events, 0.0 us)
Async XLA Ops:
  1.3 11.7 %all-to-all-start.2 = ((s32[8,1,256]{2,1,0:T(1,128)}), s32[8,1,256]{2,1,0:T(1,128)S(1)}, u32[]{:S(2)}, u32[]{:S(2)}) async-start(s32[8,1,256]{2,1,0:T(1,128)} %broadcast_in_dim.23), calls=%async_computation.2 | async-start | bytes 16384 | tf_op jit(solution)/shard_map/all_to_all | solution.py:694
  25.3 43.9 %all-to-all-start.3 = ((bf16[8,14,64,128]{3,2,1,0:T(8,128)(2,1)}), bf16[8,14,64,128]{3,2,1,0:T(8,128)(2,1)S(1)}, u32[]{:S(2)}, u32[]{:S(2)}) async-start(bf16[8,14,64,128]{3,2,1,0:T(8,128)(2,1)} %bitcast.76), calls=%async_computation.3 | async-start | bytes 3670016 | tf_op jit(solution)/shard_map/all_to_all | solution.py:578
  28.9 24.8 %collective-permute-start = (bf16[6,64,128]{2,1,0:T(8,128)(2,1)S(1)}, bf16[6,64,128]{2,1,0:T(8,128)(2,1)S(1)}, u32[]{:S(2)}, u32[]{:S(2)}) collective-permute-start(bf16[6,64,128]{2,1,0:T(8,128)(2,1)S(1)} %get-tuple-element.58), channel_id=1, source_target_pairs={{0,1},{1,2},{2,3},{3,0},{4,5},{5,6},{6,7},{7,4},{8,9},{9,10},{10,1... | collective-permute-start | bytes 294920 | tf_op jit(solution)/shard_map/ppermute | solution.py:584
  30.3 28.4 %collective-permute-start.1 = (bf16[6,64,128]{2,1,0:T(8,128)(2,1)S(1)}, bf16[6,64,128]{2,1,0:T(8,128)(2,1)S(1)}, u32[]{:S(2)}, u32[]{:S(2)}) collective-permute-start(bf16[6,64,128]{2,1,0:T(8,128)(2,1)S(1)} %get-tuple-element.59), channel_id=1, source_target_pairs={{0,2},{1,3},{2,0},{3,1},{4,6},{5,7},{6,4},{7,5},{8,10},{9,11},{10,... | collective-permute-start | bytes 294920 | tf_op jit(solution)/shard_map/ppermute | solution.py:584
  31.5 29.3 %collective-permute-start.2 = (bf16[6,64,128]{2,1,0:T(8,128)(2,1)S(1)}, bf16[6,64,128]{2,1,0:T(8,128)(2,1)S(1)}, u32[]{:S(2)}, u32[]{:S(2)}) collective-permute-start(bf16[6,64,128]{2,1,0:T(8,128)(2,1)S(1)} %get-tuple-element.60), channel_id=1, source_target_pairs={{0,3},{1,0},{2,1},{3,2},{4,7},{5,4},{6,5},{7,6},{8,11},{9,8},{10,9... | collective-permute-start | bytes 294920 | tf_op jit(solution)/shard_map/ppermute | solution.py:584
  69.2 26.4 %copy-start = (s32[256,1]{0,1:T(1,128)S(1)}, s32[256,1]{0,1:T(1,128)}, u32[]{:S(2)}) copy-start(s32[256,1]{0,1:T(1,128)} %param.10) | copy-start | bytes 3076
  69.2 26.4 %copy-start.1 = (s32[256]{0:T(256)S(1)}, s32[256]{0:T(256)}, u32[]{:S(2)}) copy-start(s32[256]{0:T(256)} %param.9) | copy-start | bytes 3076
  74.4 20.1 %all-to-all-start.4 = ((bf16[8,5,48,128]{3,2,1,0:T(8,128)(2,1)}), bf16[8,5,48,128]{3,2,1,0:T(8,128)(2,1)S(1)}, u32[]{:S(2)}, u32[]{:S(2)}) async-start(bf16[8,5,48,128]{3,2,1,0:T(8,128)(2,1)} %merge.1), calls=%async_computation.4 | async-start | bytes 983040 | tf_op jit(solution)/shard_map/all_to_all | solution.py:623
  96.6 6.2 %collective-permute-start.3 = (bf16[5,16,512]{2,1,0:T(8,128)(2,1)S(1)}, bf16[5,16,512]{2,1,0:T(8,128)(2,1)S(1)}, u32[]{:S(2)}, u32[]{:S(2)}) collective-permute-start(bf16[5,16,512]{2,1,0:T(8,128)(2,1)S(1)} %get-tuple-element.68), channel_id=1, source_target_pairs={{0,8},{8,16},{16,24},{1,9},{9,17},{17,25},{2,10},{10,18},{18,26},{... | collective-permute-start | bytes 245768 | tf_op jit(solution)/shard_map/ppermute | solution.py:28
  100.8 5.8 %collective-permute-start.4 = (bf16[5,16,512]{2,1,0:T(8,128)(2,1)S(1)}, bf16[5,16,512]{2,1,0:T(8,128)(2,1)S(1)}, u32[]{:S(2)}, u32[]{:S(2)}) collective-permute-start(bf16[5,16,512]{2,1,0:T(8,128)(2,1)S(1)} %get-tuple-element.69), channel_id=1, source_target_pairs={{8,0},{16,8},{24,16},{9,1},{17,9},{25,17},{10,2},{18,10},{26,18},{... | collective-permute-start | bytes 245768 | tf_op jit(solution)/shard_map/ppermute | solution.py:29
  107.6 6.6 %collective-permute-start.5 = (bf16[5,96,16]{2,1,0:T(8,128)(2,1)S(1)}, bf16[5,96,16]{2,1,0:T(8,128)(2,1)S(1)}, u32[]{:S(2)}, u32[]{:S(2)}) collective-permute-start(bf16[5,96,16]{2,1,0:T(8,128)(2,1)S(1)} %get-tuple-element.66), channel_id=1, source_target_pairs={{0,1},{1,2},{2,3},{3,4},{4,5},{5,6},{6,7},{7,0},{8,9},{9,10},{10,1... | collective-permute-start | bytes 46088 | tf_op jit(solution)/shard_map/ppermute | solution.py:28
  108.8 5.8 %collective-permute-start.6 = (bf16[5,96,16]{2,1,0:T(8,128)(2,1)S(1)}, bf16[5,96,16]{2,1,0:T(8,128)(2,1)S(1)}, u32[]{:S(2)}, u32[]{:S(2)}) collective-permute-start(bf16[5,96,16]{2,1,0:T(8,128)(2,1)S(1)} %get-tuple-element.67), channel_id=1, source_target_pairs={{1,0},{2,1},{3,2},{4,3},{5,4},{6,5},{7,6},{0,7},{9,8},{10,9},{11,1... | collective-permute-start | bytes 46088 | tf_op jit(solution)/shard_map/ppermute | solution.py:29

commit v5 on v4

--- a/solution.py
+++ b/solution.py
@@ -348,7 +348,8 @@
     weighed = jnp.where(iota((8, pairs), 0) == 0, lands, 1.0)
     summed = split_dot(weighed, in_slot, ((1,), (1,)))
     landing = summed[0:1, :] / jnp.maximum(summed[1:2, :], 1.0)
-    landing_ref[...] = jnp.broadcast_to((landing + 0.25).astype(I32), landing_ref.shape)
+    over = jnp.broadcast_to(table_ref[4:5, 3:4], (8, pairs))
+    landing_ref[...] = jnp.where(iota((8, pairs), 0) == 0, (landing + 0.25).astype(I32), over)
 
 
 def make_plan(me, keys, pair_source, fields, weights, cap, extra, mcap):
@@ -550,18 +551,150 @@
             out_ref[o, k] = moments[k, o * mcap : (o + 1) * mcap, :].astype(BF16)
 
 
-def spread_kernel(count, mcap, spot_ref, came, map_ref, flat):
+def spread_kernel(count, mcap, spot_ref, came, map_ref, top_ref, bottom_ref, flat):
     rows, blocks_wide = map_ref.shape[1], map_ref.shape[2] // LANES
     for a in range(count):
         for k in range(5):
             flat[a * mcap : (a + 1) * mcap, k * LANES : (k + 1) * LANES] = came[a, k]
     chosen = (iota((spot_ref.shape[0], count * mcap), 1) == spot_ref[...]).astype(F32)
-    laid = dot(chosen.astype(BF16), flat[...])
+    laid = dot(chosen.astype(BF16), flat[...]).astype(BF16)
     for q in range(blocks_wide):
         for k in range(5):
-            map_ref[k, :, q * LANES : (q + 1) * LANES] = laid[
-                q * rows : (q + 1) * rows, k * LANES : (k + 1) * LANES
-            ].astype(BF16)
+            tile = laid[q * rows : (q + 1) * rows, k * LANES : (k + 1) * LANES]
+            lanes = slice(q * LANES, (q + 1) * LANES)
+            map_ref[k, :, lanes] = tile
+            top_ref[k, :, lanes] = tile[:WINDOW_HALF]
+            bottom_ref[k, :, lanes] = tile[rows - WINDOW_HALF :]
+
+
+def tap(offset):
+    offset = offset.astype(F32)
+    value = jnp.exp(-offset * offset / (0.5 * WINDOW_HALF * WINDOW_HALF))
+    return jnp.where(jnp.abs(offset) <= WINDOW_HALF, value, 0.0)
+
+
+def halved(value):
+    upper = value.astype(BF16)
+    return upper, (value - upper.astype(F32)).astype(BF16)
+
+
+def bands_kernel(after_ref, upper_ref, lower_ref):
+    shape = upper_ref.shape
+    upper_ref[...], lower_ref[...] = halved(tap(iota(shape, 0) - iota(shape, 1)))
+
+
+def across(fields, upper, lower):
+    return dot(fields, upper) + dot(fields, lower)
+
+
+def center_kernel(map_ref, upper, lower, out_ref):
+    fields = jnp.concatenate([map_ref[k] for k in range(5)], axis=0)
+    rows = map_ref.shape[1]
+    smooth = across(fields, upper[...], lower[...])
+    for k in range(5):
+        out_ref[k] = smooth[k * rows : (k + 1) * rows]
+
+
+def lat_weights(rows):
+    shape = (rows, rows + 2 * WINDOW_HALF)
+    return tap(iota(shape, 1) - iota(shape, 0) - WINDOW_HALF)
+
+
+def rows_kernel(before, after, upper, lower, center, out_ref):
+    rows = center.shape[1]
+    half = WINDOW_HALF
+    fields = jnp.concatenate([before[k] for k in range(5)] + [after[k] for k in range(5)], axis=0)
+    smooth = across(fields, upper[...], lower[...])
+    weights = lat_weights(rows)
+    for k in range(5):
+        first = smooth[k * half : (k + 1) * half]
+        last = smooth[(5 + k) * half : (6 + k) * half]
+        tall = jnp.concatenate([first, center[k], last], axis=0)
+        out_ref[k] = dot(weights, tall, exact=True)
+
+
+def result_kernel(height, days, lat_ref, left, right, partial, out_ref, edges):
+    rows, width = out_ref.shape
+    half = WINDOW_HALF
+    tall = rows + 2 * half
+    at, lane = iota((half, LANES), 0), iota((half, LANES), 1)
+    for side, (ref, offset) in enumerate(((left, at - half - lane), (right, LANES + at - lane))):
+        upper, lower = halved(tap(offset))
+        fields = jnp.concatenate([ref[k] for k in range(5)], axis=0)
+        smooth = across(fields, upper, lower)
+        for k in range(5):
+            place = (side * 5 + k) * LANES
+            edges[:, place : place + LANES] = smooth[k * tall : (k + 1) * tall]
+    beside = dot(lat_weights(rows), edges[...], exact=True)
+    k_at = iota((rows, LANES), 1) - half
+    row = lat_ref[0] * rows + iota((rows, LANES), 0) + k_at
+    taps = tap(k_at)
+    inside = jnp.where((row >= 0) & (row < height), taps, 0.0)
+    weight = jnp.sum(inside, axis=1, keepdims=True) * (jnp.sum(taps, axis=1, keepdims=True) * days)
+    scale = 1.0 / weight
+    tiles = width // LANES
+    for q in range(tiles):
+        lanes = slice(q * LANES, (q + 1) * LANES)
+        values = []
+        for k in range(5):
+            value = partial[k, :, lanes]
+            if q == 0:
+                value = value + beside[:, k * LANES : (k + 1) * LANES]
+            if q == tiles - 1:
+                value = value + beside[:, (5 + k) * LANES : (6 + k) * LANES]
+            values.append(value * scale)
+        mean_t, mean_m, square_t, square_m, cross = values
+        var_t = square_t - mean_t * mean_t
+        var_m = square_m - mean_m * mean_m
+        covar = cross - mean_t * mean_m
+        out_ref[:, lanes] = covar / jnp.sqrt(var_t * var_m + 1e-06)
+
+
+def neighbours(low, high, axis, wrap):
+    count = lax.axis_size(axis)
+    up = [(i, (i + 1) % count) for i in range(count if wrap else count - 1)]
+    down = [(j, i) for i, j in up]
+    return lax.ppermute(high, axis, up), lax.ppermute(low, axis, down)
+
+
+def correlate(days, moments, top, bottom, bands):
+    vmem = pl.BlockSpec(memory_space=pltpu.VMEM)
+    smem = pl.BlockSpec(memory_space=pltpu.SMEM)
+    small = pltpu.CompilerParams(vmem_limit_bytes=16 << 20)
+    _, rows, width = moments.shape
+    whole = jax.ShapeDtypeStruct(moments.shape, F32)
+    before, after = neighbours(top, bottom, "lat", False)
+    center = pl.pallas_call(
+        center_kernel,
+        out_shape=whole,
+        in_specs=[vmem] * 3,
+        out_specs=vmem,
+        compiler_params=small,
+        name="center",
+    )(moments, *bands)
+    before, after, center = lax.optimization_barrier((before, after, center))
+    tall = (before, moments, after)
+    low = jnp.concatenate([each[:, :, :WINDOW_HALF] for each in tall], axis=1)
+    high = jnp.concatenate([each[:, :, width - WINDOW_HALF :] for each in tall], axis=1)
+    left, right = neighbours(low, high, "lon", True)
+    partial = pl.pallas_call(
+        rows_kernel,
+        out_shape=whole,
+        in_specs=[vmem] * 5,
+        out_specs=vmem,
+        compiler_params=small,
+        name="rows",
+    )(before, after, *bands, center)
+    height = rows * lax.axis_size("lat")
+    return pl.pallas_call(
+        functools.partial(result_kernel, height, days),
+        out_shape=jax.ShapeDtypeStruct((rows, width), F32),
+        in_specs=[smem, vmem, vmem, vmem],
+        out_specs=vmem,
+        scratch_shapes=[pltpu.VMEM((rows + 2 * WINDOW_HALF, 10 * LANES), F32)],
+        compiler_params=small,
+        name="result",
+    )(lax.axis_index("lat").astype(I32)[None], left, right, partial)
 
 
 def direct(cap, extra, mcap, source_fields, weight_blocks, me, keys, table, owner, pres, sent):
@@ -585,6 +718,12 @@
     entry, spot, landing = finish_plan(
         me, keys, owner, pres, table, count, blocks, cap, extra, mcap
     )
+    lat_count = lax.axis_size("lat")
+    flag = landing[1:2, :LANES]
+    flags = [flag]
+    for j in range(1, lat_count):
+        turn = [(i, (i + j) % lat_count) for i in range(lat_count)]
+        flags.append(lax.ppermute(flag, "lat", turn))
     chunk_count = -(-pairs // CHUNK)
     local, moments = pl.pallas_call(
         functools.partial(local_kernel, sends),
@@ -604,6 +743,7 @@
         compiler_params=pltpu.CompilerParams(vmem_limit_bytes=50 << 20),
         name="staying",
     )(table, landing, source_fields, weight_blocks)
+    far, near, flags = lax.optimization_barrier((far, near, flags))
     finished = pl.pallas_call(
         functools.partial(merge_kernel, count, cap, extra, mcap),
         out_shape=jax.ShapeDtypeStruct((count, 5, mcap, cells), BF16),
@@ -620,18 +760,31 @@
         compiler_params=pltpu.CompilerParams(vmem_limit_bytes=50 << 20),
         name="merge",
     )(table, landing, entry, local, moments, far, *near)
+    bands = pl.pallas_call(
+        bands_kernel,
+        out_shape=[jax.ShapeDtypeStruct((LON_DEV, LON_DEV), BF16)] * 2,
+        in_specs=[hbm],
+        out_specs=[vmem] * 2,
+        compiler_params=pltpu.CompilerParams(vmem_limit_bytes=50 << 20),
+        name="bands",
+    )(finished)
     arrived = lax.all_to_all(finished, "lon", split_axis=0, concat_axis=0, tiled=True)
     wide = LON_DEV // cells
     where = spot.reshape(-1)[:blocks].reshape(LAT_DEV, wide).T.reshape(blocks, 1)
-    return pl.pallas_call(
+    moments, top, bottom = pl.pallas_call(
         functools.partial(spread_kernel, count, mcap),
-        out_shape=jax.ShapeDtypeStruct((5, LAT_DEV, LON_DEV), BF16),
+        out_shape=[
+            jax.ShapeDtypeStruct((5, each, LON_DEV), BF16)
+            for each in (LAT_DEV, WINDOW_HALF, WINDOW_HALF)
+        ],
         in_specs=[vmem, vmem],
-        out_specs=vmem,
+        out_specs=[vmem] * 3,
         scratch_shapes=[pltpu.VMEM((count * mcap, 5 * cells), BF16)],
         compiler_params=pltpu.CompilerParams(vmem_limit_bytes=8 << 20),
         name="spread",
     )(where, arrived)
+    arrived_flags = functools.reduce(jnp.maximum, flags)
+    return correlate(channels // 2, moments, top, bottom, bands), arrived_flags
 
 
 def padded_exchange(source_fields, weight_blocks, pair_source, targets, pair_block):
@@ -680,36 +833,9 @@
     return moments.reshape(5, LAT_DEV, LON_DEV).astype(BF16)
 
 
-def local(source_fields, weight_blocks, pair_source, pair_target, pair_block):
-    count = lax.axis_size("lon")
-    blocks, channels, _ = source_fields.shape
-    days = channels // 2
-    pairs = pair_source.shape[0]
-    share = -(-pairs // count)
-    cap = max(share * 7 // 16, min(share, 8))
-    extra = max(share * 3 // 16, 1)
-    mcap = -(-share * 3 // 2 // 16) * 16
-    targets = pair_target[:, 0]
-    keys = pair_target.reshape(1, 1, pairs) * blocks + pair_block[None, None, :]
-    all_keys = lax.all_to_all(
-        jnp.broadcast_to(keys, (count, 1, pairs)), "lon", split_axis=0, concat_axis=0, tiled=True
-    )
-    me = lax.axis_index("lon").astype(I32)[None]
-    table, owner, pres, sent = make_plan(
-        me, all_keys, pair_source, source_fields, weight_blocks, cap, extra, mcap
-    )
-    sent, owner = lax.optimization_barrier((sent, owner))
-    moments = direct(
-        cap, extra, mcap, source_fields, weight_blocks, me, all_keys, table, owner, pres, sent
-    )
-    moments = lax.cond(
-        table[4, 3] == 0,
-        lambda kept: kept,
-        lambda kept: padded_exchange(
-            source_fields, weight_blocks, pair_source, targets, pair_block
-        ),
-        moments,
-    )
+def padded_result(source_fields, weight_blocks, pair_source, targets, pair_block):
+    moments = padded_exchange(source_fields, weight_blocks, pair_source, targets, pair_block)
+    days = source_fields.shape[1] // 2
     lon_band = band_matrix(LON_DEV)
     lat_band = band_matrix(LAT_DEV)
     taller = padded(moments, (("lat", 1),), WINDOW_HALF, False)
@@ -734,6 +860,37 @@
     return covar / jnp.sqrt(var_temper * var_moist + 1e-06)
 
 
+def local(source_fields, weight_blocks, pair_source, pair_target, pair_block):
+    count = lax.axis_size("lon")
+    blocks = source_fields.shape[0]
+    pairs = pair_source.shape[0]
+    share = -(-pairs // count)
+    cap = max(share * 7 // 16, min(share, 8))
+    extra = max(share * 3 // 16, 1)
+    mcap = -(-share * 3 // 2 // 16) * 16
+    targets = pair_target[:, 0]
+    keys = pair_target.reshape(1, 1, pairs) * blocks + pair_block[None, None, :]
+    all_keys = lax.all_to_all(
+        jnp.broadcast_to(keys, (count, 1, pairs)), "lon", split_axis=0, concat_axis=0, tiled=True
+    )
+    me = lax.axis_index("lon").astype(I32)[None]
+    table, owner, pres, sent = make_plan(
+        me, all_keys, pair_source, source_fields, weight_blocks, cap, extra, mcap
+    )
+    sent, owner = lax.optimization_barrier((sent, owner))
+    result, flags = direct(
+        cap, extra, mcap, source_fields, weight_blocks, me, all_keys, table, owner, pres, sent
+    )
+    return lax.cond(
+        jnp.max(flags) == 0,
+        lambda kept: kept,
+        lambda kept: padded_result(
+            source_fields, weight_blocks, pair_source, targets, pair_block
+        ),
+        result,
+    )
+
+
 def solution(mesh):
     placed = (
         P(("lat", "lon"), None, None),

time: 120 us -> 116 us (0.967)
  starting transfers between devices: 31 us -> 35.3 us
  matrix products: 3.67 us -> 0 us
  waiting for transfers between devices: 43.3 us -> 39.7 us
  Pallas kernels: 34 us -> 36.2 us
  other arithmetic: 3.26 us -> 1.39 us
    ppermute x3, waiting for transfers between devices: 12.7 us -> 5.82 us  [direct(): near.append(lax.ppermute(sent[1 + j], 'lon', turn))]
    ppermute x4 -> x7, starting transfers between devices: 10.3 us -> 14.8 us  [the longest x4 8.96 us: neighbours(): return (lax.ppermute(high, axis, up), lax.ppermute(low, axis, down))]
    dot_general x2 -> x0, matrix products: 3.67 us -> none  [the longest x1 2.85 us: smooth_lon(): jnp.einsum('krb,bj->krj', fields, lon_band, precision=lax.Precision.HIGHEST)]
    pallas_call x1 -> x5, Pallas kernels: 1.16 us -> 3.06 us  [the longest x1 1 us: correlate(): pl.pallas_call(rows_kernel, out_shape=whole, in_specs=[vmem] * 5, out_spe...]
    all_to_all x1, waiting for transfers between devices: 10.3 us -> 12.1 us  [direct(): lax.all_to_all(finished, 'lon', split_axis=0, concat_axis=0, tiled=True)]
    ppermute x4 -> x7, waiting for transfers between devices: 6.6 us -> 8.06 us  [the longest x4 7.33 us: neighbours(): return (lax.ppermute(high, axis, up), lax.ppermute(low, axis, down))]
    slice x2 -> x3, local copies, waits for them, and re-layouts: 1.52 us -> 0.19 us  [the longest x2 0.18 us: correlate(): low = jnp.concatenate([each[:, :, :WINDOW_HALF] for each in tall], axis=1)]
  transfers between devices with their start and end apart: 10 -> 13, of which waited for: 9 -> 8; matrix products, arithmetic and copies ran while one was open for 1% -> 1% of each run, Pallas kernels for 13% -> 15%
where the time goes in v5:
time: 116 us; the launch traced here: 115 us
  waiting for transfers between devices  39.7 us (34%)
  Pallas kernels  36.2 us (31%)
  starting transfers between devices  35.3 us (30%)
  local copies, waits for them, and re-layouts  1.78 us (2%)
  other arithmetic  1.39 us (1%)
    pallas_call x1, Pallas kernels, direct(): pl.pallas_call(functools.partial(local_kernel, sends), out_shape=(jax.Sha...  13.3 us
    pallas_call x1, Pallas kernels, make_plan(): pl.pallas_call(functools.partial(plan_kernel, count, blocks, cap, extra,...  12.3 us
    all_to_all x1, waiting for transfers between devices, direct(): lax.all_to_all(finished, 'lon', split_axis=0, concat_axis=0, tiled=True)  12.1 us
    ppermute x4, starting transfers between devices, neighbours(): return (lax.ppermute(high, axis, up), lax.ppermute(low, axis, down))  8.96 us
    all_to_all x1, waiting for transfers between devices, direct(): lax.all_to_all(sent[0].reshape(count, cap, channels, cells), 'lon', split...  8.37 us
    ppermute x4, waiting for transfers between devices, neighbours(): return (lax.ppermute(high, axis, up), lax.ppermute(low, axis, down))  7.33 us
    all_to_all x1, starting transfers between devices, direct(): lax.all_to_all(finished, 'lon', split_axis=0, concat_axis=0, tiled=True)  6.82 us
    all_to_all x1, starting transfers between devices, local(): lax.all_to_all(jnp.broadcast_to(keys, (count, 1, pairs)), 'lon', split_ax...  6.34 us
  transfers between devices with their start and end apart: 13, of which 8 were waited for; matrix products, arithmetic and copies ran while one was open for 1% of the time, Pallas kernels for 15%

profile of v5, /device:TPU:1, one launch (start us, length us, event | category | flops | bytes accessed | tf_op | source)
XLA Modules:
  0.0 115.5 jit_solution(2573914178775533168)
XLA Ops:
  0.0 0.7 multiply_add_fusion
  0.7 0.6 broadcast_in_dim.21
  1.3 6.3 %all-to-all-start.2 = ((s32[8,1,256]{2,1,0:T(1,128)}), s32[8,1,256]{2,1,0:T(1,128)S(1)}, u32[]{:S(2)}, u32[]{:S(2)}) async-start(s32[8,1,256]{2,1,0:T(1,128)} %broadcast_in_dim.21), calls=%async_computation.2 | async-start | bytes 16384 | tf_op jit(solution)/shard_map/all_to_all | solution.py:873
  7.6 5.4 %all-to-all-done.2.keys_ref = s32[8,1,256]{2,1,0:T(1,128)S(1)} async-done(((s32[8,1,256]{2,1,0:T(1,128)}), s32[8,1,256]{2,1,0:T(1,128)S(1)}, u32[]{:S(2)}, u32[]{:S(2)}) %all-to-all-start.2) | async-done | bytes 8224 | tf_op jit(solution)/shard_map/all_to_all | solution.py:873
  13.0 12.3 %leaving.1 = (s32[8,256]{1,0:T(8,128)S(1)}, s32[16,128]{1,0:T(8,128)S(1)}, f32[8,16,128]{2,1,0:T(8,128)S(1)}, bf16[112,64,128]{2,1,0:T(8,128)(2,1)}, bf16[6,64,1...) custom-call(s32[1]{0:T(128)} %bitcast.14.me_ref, ...), custom_call_target="tpu_custom_call" | custom-call | tf_op jit(solution)/shard_map/leaving/pallas_call | solution.py:364
  25.3 3.6 %all-to-all-start.3 = ((bf16[8,14,64,128]{3,2,1,0:T(8,128)(2,1)}), bf16[8,14,64,128]{3,2,1,0:T(8,128)(2,1)S(1)}, u32[]{:S(2)}, u32[]{:S(2)}) async-start(bf16[8,14,64,128]{3,2,1,0:T(8,128)(2,1)} %bitcast.76), calls=%async_computation.3 | async-start | bytes 3670016 | tf_op jit(solution)/shard_map/all_to_all | solution.py:711
  28.9 1.4 %collective-permute-start.4 = (bf16[6,64,128]{2,1,0:T(8,128)(2,1)S(1)}, bf16[6,64,128]{2,1,0:T(8,128)(2,1)S(1)}, u32[]{:S(2)}, u32[]{:S(2)}) collective-permute-start(bf16[6,64,128]{2,1,0:T(8,128)(2,1)S(1)} %get-tuple-element.66), channel_id=1, source_target_pairs={{0,1},{1,2},{2,3},{3,0},{4,5},{5,6},{6,7},{7,4},{8,9},{9,10},{10,1... | collective-permute-start | bytes 294920 | tf_op jit(solution)/shard_map/ppermute | solution.py:717
  30.3 1.2 %collective-permute-start.5 = (bf16[6,64,128]{2,1,0:T(8,128)(2,1)S(1)}, bf16[6,64,128]{2,1,0:T(8,128)(2,1)S(1)}, u32[]{:S(2)}, u32[]{:S(2)}) collective-permute-start(bf16[6,64,128]{2,1,0:T(8,128)(2,1)S(1)} %get-tuple-element.67), channel_id=1, source_target_pairs={{0,2},{1,3},{2,0},{3,1},{4,6},{5,7},{6,4},{7,5},{8,10},{9,11},{10,... | collective-permute-start | bytes 294920 | tf_op jit(solution)/shard_map/ppermute | solution.py:717
  31.5 1.2 %collective-permute-start.6 = (bf16[6,64,128]{2,1,0:T(8,128)(2,1)S(1)}, bf16[6,64,128]{2,1,0:T(8,128)(2,1)S(1)}, u32[]{:S(2)}, u32[]{:S(2)}) collective-permute-start(bf16[6,64,128]{2,1,0:T(8,128)(2,1)S(1)} %get-tuple-element.68), channel_id=1, source_target_pairs={{0,3},{1,0},{2,1},{3,2},{4,7},{5,4},{6,5},{7,6},{8,11},{9,8},{10,9... | collective-permute-start | bytes 294920 | tf_op jit(solution)/shard_map/ppermute | solution.py:717
  32.7 2.4 %finish.1 = (s32[32,128]{1,0:T(8,128)S(1)}, s32[8,128]{1,0:T(8,128)S(1)}, s32[8,256]{1,0:T(8,128)S(1)}) custom-call(s32[1]{0:T(128)} %bitcast.14.me_ref, s32[8,1,256]{2,1,0:T(1,128)S(1)} %all-to-all-done.2.keys_ref, s32[16,128]{1,0:T(8,128)S(1)} %get-tuple-element.69.owner_ref, f32[8,16,128]{2,1,0:T(8,128)S(1)} %get-tuple-element.70.pres, ...), custom_call_target="tpu_custom_call" | custom-call | tf_op jit(solution)/shard_map/finish/pallas_call | solution.py:397
  35.1 5.0 %collective-permute-start.7 = (s32[1,128]{1,0:T(1,128)S(1)}, s32[1,128]{1,0:T(1,128)S(1)}, u32[]{:S(2)}, u32[]{:S(2)}) collective-permute-start(s32[1,128]{1,0:T(1,128)S(1)} %slice.64), channel_id=1, source_target_pairs={{0,8},{8,16},{16,24},{24,0},{1,9},{9,17},{17,25},{25,1},{2,10},{10... | collective-permute-start | bytes 1544 | tf_op jit(solution)/shard_map/ppermute | solution.py:726
  40.1 0.0 collective-permute-start.8
  40.1 0.7 collective-permute-done.7
  40.8 0.9 collective-permute-start.9
  41.6 13.3 %staying.1 = (f32[256,64,128]{2,1,0:T(8,128)}, f32[5,392,128]{2,1,0:T(8,128)S(1)}) custom-call(s32[8,256]{1,0:T(8,128)S(1)} %get-tuple-element.71.table_ref.table, s32[8,256]{1,0:T(8,128)S(1)} %get-tuple-element.72.landing, bf16[256,64,128]{2,1,0:T(8,128)(2,1)} %fields.3, bf16[256,128,128]{2,1,0:T(8,128)(2,1)} %weights.3), custom_call_target="tpu_custom_call" | custom-call | tf_op jit(solution)/shard_map/staying/pallas_call | solution.py:728
  55.0 0.0 collective-permute-done.8
  55.0 0.0 collective-permute-done.9
  55.0 0.0 collective-permute-done.4.refs_0_
  55.0 3.7 %collective-permute-done.5.refs_1_ = bf16[6,64,128]{2,1,0:T(8,128)(2,1)S(1)} collective-permute-done((bf16[6,64,128]{2,1,0:T(8,128)(2,1)S(1)}, bf16[6,64,128]{2,1,0:T(8,128)(2,1)S(1)}, u32[]{:S(2)}, u32[]{:S(2)}) %collective-permute-start.5) | collective-permute-done | bytes 98336 | tf_op jit(solution)/shard_map/ppermute | solution.py:717
  58.7 2.1 %collective-permute-done.6.refs_2_ = bf16[6,64,128]{2,1,0:T(8,128)(2,1)S(1)} collective-permute-done((bf16[6,64,128]{2,1,0:T(8,128)(2,1)S(1)}, bf16[6,64,128]{2,1,0:T(8,128)(2,1)S(1)}, u32[]{:S(2)}, u32[]{:S(2)}) %collective-permute-start.6) | collective-permute-done | bytes 98336 | tf_op jit(solution)/shard_map/ppermute | solution.py:717
  60.8 8.4 %all-to-all-done.3 = bf16[8,14,64,128]{3,2,1,0:T(8,128)(2,1)S(1)} async-done(((bf16[8,14,64,128]{3,2,1,0:T(8,128)(2,1)}), bf16[8,14,64,128]{3,2,1,0:T(8,128)(2,1)S(1)}, u32[]{:S(2)}, u32[]{:S(2)}) %all-to-all-start.3) | async-done | bytes 1835040 | tf_op jit(solution)/shard_map/all_to_all | solution.py:711
  69.2 5.1 %merge.1.after_ref = bf16[8,5,48,128]{3,2,1,0:T(8,128)(2,1)} custom-call(s32[8,256]{1,0:T(8,128)S(1)} %get-tuple-element.71.table_ref.table, s32[8,256]{1,0:T(8,128)S(1)} %get-tuple-element.72.landing, s32[32,128]{1,0:T(8,128)S(1)} %get-tuple-element.78.entry, f32[256,64,128]{2,1,0:T(8,128)} %get-tuple-element.79.local_ref, ...), custom_call_target="tpu_custom_call" | custom-call | tf_op jit(solution)/shard_map/merge/pallas_call | solution.py:747
  74.3 0.0 copy-start.1
  74.3 0.0 copy-start.2
  74.3 6.8 %all-to-all-start.4 = ((bf16[8,5,48,128]{3,2,1,0:T(8,128)(2,1)}), bf16[8,5,48,128]{3,2,1,0:T(8,128)(2,1)S(1)}, u32[]{:S(2)}, u32[]{:S(2)}) async-start(bf16[8,5,48,128]{3,2,1,0:T(8,128)(2,1)} %merge.1.after_ref), calls=%async_computation.4 | async-start | bytes 983040 | tf_op jit(solution)/shard_map/all_to_all | solution.py:771
  81.2 0.1 reshape.93
  81.3 0.1 copy.21
  81.3 0.2 reshape.135.spot_ref
  81.5 0.5 bands.1
  82.0 12.1 %all-to-all-done.4.came = bf16[8,5,48,128]{3,2,1,0:T(8,128)(2,1)S(1)} async-done(((bf16[8,5,48,128]{3,2,1,0:T(8,128)(2,1)}), bf16[8,5,48,128]{3,2,1,0:T(8,128)(2,1)S(1)}, u32[]{:S(2)}, u32[]{:S(2)}) %all-to-all-start.4) | async-done | bytes 491552 | tf_op jit(solution)/shard_map/all_to_all | solution.py:771
  94.1 0.4 spread.1
  94.5 4.8 %collective-permute-start.10 = (bf16[5,16,512]{2,1,0:T(8,128)(2,1)S(1)}, bf16[5,16,512]{2,1,0:T(8,128)(2,1)S(1)}, u32[]{:S(2)}, u32[]{:S(2)}) collective-permute-start(bf16[5,16,512]{2,1,0:T(8,128)(2,1)S(1)} %get-tuple-element.85), channel_id=1, source_target_pairs={{0,8},{8,16},{16,24},{1,9},{9,17},{17,25},{2,10},{10,18},{18,26},{... | collective-permute-start | bytes 245768 | tf_op jit(solution)/shard_map/ppermute | solution.py:657
  99.4 1.9 %collective-permute-start.11 = (bf16[5,16,512]{2,1,0:T(8,128)(2,1)S(1)}, bf16[5,16,512]{2,1,0:T(8,128)(2,1)S(1)}, u32[]{:S(2)}, u32[]{:S(2)}) collective-permute-start(bf16[5,16,512]{2,1,0:T(8,128)(2,1)S(1)} %get-tuple-element.86), channel_id=1, source_target_pairs={{8,0},{16,8},{24,16},{9,1},{17,9},{25,17},{10,2},{18,10},{26,18},{... | collective-permute-start | bytes 245768 | tf_op jit(solution)/shard_map/ppermute | solution.py:657
  101.3 0.1 fusion.71
  101.4 0.5 center.1
  101.9 0.0 collective-permute-done.10.before
  101.9 3.2 %collective-permute-done.11.after = bf16[5,16,512]{2,1,0:T(8,128)(2,1)S(1)} collective-permute-done((bf16[5,16,512]{2,1,0:T(8,128)(2,1)S(1)}, bf16[5,16,512]{2,1,0:T(8,128)(2,1)S(1)}, u32[]{:S(2)}, u32[]{:S(2)}) %collective-permute-start.11) | collective-permute-done | bytes 81952 | tf_op jit(solution)/shard_map/ppermute | solution.py:657
  105.1 0.1 fusion.72
  105.2 2.1 %collective-permute-start.13 = (bf16[5,96,16]{2,1,0:T(8,128)(2,1)S(1)}, bf16[5,96,16]{2,1,0:T(8,128)(2,1)S(1)}, u32[]{:S(2)}, u32[]{:S(2)}) collective-permute-start(bf16[5,96,16]{2,1,0:T(8,128)(2,1)S(1)} %pad_maximum_fusion.4), channel_id=1, source_target_pairs={{1,0},{2,1},{3,2},{4,3},{5,4},{6,5},{7,6},{0,7},{9,8},{10,9},{11,1... | collective-permute-start | bytes 46088 | tf_op jit(solution)/shard_map/ppermute | solution.py:657
  107.4 0.1 collective-permute-start.12
  107.5 0.6 maximum_reduce_fusion
  108.8 1.0 rows.1.partial
  109.8 0.0 collective-permute-done.13.right
  109.8 4.1 %collective-permute-done.12.left = bf16[5,96,16]{2,1,0:T(8,128)(2,1)S(1)} collective-permute-done((bf16[5,96,16]{2,1,0:T(8,128)(2,1)S(1)}, bf16[5,96,16]{2,1,0:T(8,128)(2,1)S(1)}, u32[]{:S(2)}, u32[]{:S(2)}) %collective-permute-start.12) | collective-permute-done | bytes 15392 | tf_op jit(solution)/shard_map/ppermute | solution.py:657
  113.9 0.6 result.1
  114.6 0.2 conditional.1
  114.8 0.0 copy-start
  114.8 0.6 copy-done
  (6 shorter events, 0.1 us)
Async XLA Ops:
  1.3 11.7 %all-to-all-start.2 = ((s32[8,1,256]{2,1,0:T(1,128)}), s32[8,1,256]{2,1,0:T(1,128)S(1)}, u32[]{:S(2)}, u32[]{:S(2)}) async-start(s32[8,1,256]{2,1,0:T(1,128)} %broadcast_in_dim.21), calls=%async_computation.2 | async-start | bytes 16384 | tf_op jit(solution)/shard_map/all_to_all | solution.py:873
  25.3 43.9 %all-to-all-start.3 = ((bf16[8,14,64,128]{3,2,1,0:T(8,128)(2,1)}), bf16[8,14,64,128]{3,2,1,0:T(8,128)(2,1)S(1)}, u32[]{:S(2)}, u32[]{:S(2)}) async-start(bf16[8,14,64,128]{3,2,1,0:T(8,128)(2,1)} %bitcast.76), calls=%async_computation.3 | async-start | bytes 3670016 | tf_op jit(solution)/shard_map/all_to_all | solution.py:711
  28.9 26.1 %collective-permute-start.4 = (bf16[6,64,128]{2,1,0:T(8,128)(2,1)S(1)}, bf16[6,64,128]{2,1,0:T(8,128)(2,1)S(1)}, u32[]{:S(2)}, u32[]{:S(2)}) collective-permute-start(bf16[6,64,128]{2,1,0:T(8,128)(2,1)S(1)} %get-tuple-element.66), channel_id=1, source_target_pairs={{0,1},{1,2},{2,3},{3,0},{4,5},{5,6},{6,7},{7,4},{8,9},{9,10},{10,1... | collective-permute-start | bytes 294920 | tf_op jit(solution)/shard_map/ppermute | solution.py:717
  30.3 28.4 %collective-permute-start.5 = (bf16[6,64,128]{2,1,0:T(8,128)(2,1)S(1)}, bf16[6,64,128]{2,1,0:T(8,128)(2,1)S(1)}, u32[]{:S(2)}, u32[]{:S(2)}) collective-permute-start(bf16[6,64,128]{2,1,0:T(8,128)(2,1)S(1)} %get-tuple-element.67), channel_id=1, source_target_pairs={{0,2},{1,3},{2,0},{3,1},{4,6},{5,7},{6,4},{7,5},{8,10},{9,11},{10,... | collective-permute-start | bytes 294920 | tf_op jit(solution)/shard_map/ppermute | solution.py:717
  31.5 29.3 %collective-permute-start.6 = (bf16[6,64,128]{2,1,0:T(8,128)(2,1)S(1)}, bf16[6,64,128]{2,1,0:T(8,128)(2,1)S(1)}, u32[]{:S(2)}, u32[]{:S(2)}) collective-permute-start(bf16[6,64,128]{2,1,0:T(8,128)(2,1)S(1)} %get-tuple-element.68), channel_id=1, source_target_pairs={{0,3},{1,0},{2,1},{3,2},{4,7},{5,4},{6,5},{7,6},{8,11},{9,8},{10,9... | collective-permute-start | bytes 294920 | tf_op jit(solution)/shard_map/ppermute | solution.py:717
  35.1 5.7 %collective-permute-start.7 = (s32[1,128]{1,0:T(1,128)S(1)}, s32[1,128]{1,0:T(1,128)S(1)}, u32[]{:S(2)}, u32[]{:S(2)}) collective-permute-start(s32[1,128]{1,0:T(1,128)S(1)} %slice.64), channel_id=1, source_target_pairs={{0,8},{8,16},{16,24},{24,0},{1,9},{9,17},{17,25},{25,1},{2,10},{10... | collective-permute-start | bytes 1544 | tf_op jit(solution)/shard_map/ppermute | solution.py:726
  40.1 14.9 %collective-permute-start.8 = (s32[1,128]{1,0:T(1,128)S(1)}, s32[1,128]{1,0:T(1,128)S(1)}, u32[]{:S(2)}, u32[]{:S(2)}) collective-permute-start(s32[1,128]{1,0:T(1,128)S(1)} %slice.64), channel_id=1, source_target_pairs={{0,16},{8,24},{16,0},{24,8},{1,17},{9,25},{17,1},{25,9},{2,18},{10... | collective-permute-start | bytes 1544 | tf_op jit(solution)/shard_map/ppermute | solution.py:726
  40.8 14.2 %collective-permute-start.9 = (s32[1,128]{1,0:T(1,128)S(1)}, s32[1,128]{1,0:T(1,128)S(1)}, u32[]{:S(2)}, u32[]{:S(2)}) collective-permute-start(s32[1,128]{1,0:T(1,128)S(1)} %slice.64), channel_id=1, source_target_pairs={{0,24},{8,0},{16,8},{24,16},{1,25},{9,1},{17,9},{25,17},{2,26},{10... | collective-permute-start | bytes 1544 | tf_op jit(solution)/shard_map/ppermute | solution.py:726
  74.3 39.6 %copy-start.1 = (s32[256,1]{0,1:T(1,128)S(1)}, s32[256,1]{0,1:T(1,128)}, u32[]{:S(2)}) copy-start(s32[256,1]{0,1:T(1,128)} %param.10) | copy-start | bytes 3076
  74.3 39.6 %copy-start.2 = (s32[256]{0:T(256)S(1)}, s32[256]{0:T(256)}, u32[]{:S(2)}) copy-start(s32[256]{0:T(256)} %param.9) | copy-start | bytes 3076
  74.3 19.8 %all-to-all-start.4 = ((bf16[8,5,48,128]{3,2,1,0:T(8,128)(2,1)}), bf16[8,5,48,128]{3,2,1,0:T(8,128)(2,1)S(1)}, u32[]{:S(2)}, u32[]{:S(2)}) async-start(bf16[8,5,48,128]{3,2,1,0:T(8,128)(2,1)} %merge.1.after_ref), calls=%async_computation.4 | async-start | bytes 983040 | tf_op jit(solution)/shard_map/all_to_all | solution.py:771
  94.5 7.4 %collective-permute-start.10 = (bf16[5,16,512]{2,1,0:T(8,128)(2,1)S(1)}, bf16[5,16,512]{2,1,0:T(8,128)(2,1)S(1)}, u32[]{:S(2)}, u32[]{:S(2)}) collective-permute-start(bf16[5,16,512]{2,1,0:T(8,128)(2,1)S(1)} %get-tuple-element.85), channel_id=1, source_target_pairs={{0,8},{8,16},{16,24},{1,9},{9,17},{17,25},{2,10},{10,18},{18,26},{... | collective-permute-start | bytes 245768 | tf_op jit(solution)/shard_map/ppermute | solution.py:657
  99.4 5.8 %collective-permute-start.11 = (bf16[5,16,512]{2,1,0:T(8,128)(2,1)S(1)}, bf16[5,16,512]{2,1,0:T(8,128)(2,1)S(1)}, u32[]{:S(2)}, u32[]{:S(2)}) collective-permute-start(bf16[5,16,512]{2,1,0:T(8,128)(2,1)S(1)} %get-tuple-element.86), channel_id=1, source_target_pairs={{8,0},{16,8},{24,16},{9,1},{17,9},{25,17},{10,2},{18,10},{26,18},{... | collective-permute-start | bytes 245768 | tf_op jit(solution)/shard_map/ppermute | solution.py:657
  105.2 4.5 %collective-permute-start.13 = (bf16[5,96,16]{2,1,0:T(8,128)(2,1)S(1)}, bf16[5,96,16]{2,1,0:T(8,128)(2,1)S(1)}, u32[]{:S(2)}, u32[]{:S(2)}) collective-permute-start(bf16[5,96,16]{2,1,0:T(8,128)(2,1)S(1)} %pad_maximum_fusion.4), channel_id=1, source_target_pairs={{1,0},{2,1},{3,2},{4,3},{5,4},{6,5},{7,6},{0,7},{9,8},{10,9},{11,1... | collective-permute-start | bytes 46088 | tf_op jit(solution)/shard_map/ppermute | solution.py:657
  107.4 6.5 %collective-permute-start.12 = (bf16[5,96,16]{2,1,0:T(8,128)(2,1)S(1)}, bf16[5,96,16]{2,1,0:T(8,128)(2,1)S(1)}, u32[]{:S(2)}, u32[]{:S(2)}) collective-permute-start(bf16[5,96,16]{2,1,0:T(8,128)(2,1)S(1)} %pad_maximum_fusion.3), channel_id=1, source_target_pairs={{0,1},{1,2},{2,3},{3,4},{4,5},{5,6},{6,7},{7,0},{8,9},{9,10},{10,1... | collective-permute-start | bytes 46088 | tf_op jit(solution)/shard_map/ppermute | solution.py:657
  114.8 0.7 copy-start
